TPU v7x, 32 devices: a whole 2x2x4 slice. The times are simulated.
32 devices in a mesh: grp: 4 (over y, x), mem: 8 (over z, core).
Axes of the slice: x: 2, y: 2, z: 4, core: 2. Of those that a mesh axis runs over, the one named last changes fastest.
Arguments:
- tokens: bfloat16 [4096, 1024], P(('grp', 'mem')), may hold values from -6 to 6
- segment_ids: int32 [4096], P('grp'), may hold values from 0 to 127, never falling along the last dimension, each value on 1 to 512 neighbouring positions
- picks: int32 [4096, 4, 32], P(('grp', 'mem')), may hold values from 0 to 65535, as said below
- attn_gain: bfloat16 [1024], P('mem'), may hold values from 0.5 to 1.5
- qkv_weight: bfloat16 [1024, 3072], P('mem'), may hold values from -0.1875 to 0.1875
- attn_proj: bfloat16 [1024, 1024], P('mem'), may hold values from -1 to 1
- mem_gain: bfloat16 [1024], P('mem'), may hold values from 0.5 to 1.5
- query_weight: bfloat16 [1024, 4096], P('mem'), may hold values from -0.1875 to 0.1875
- half_keys: bfloat16 [2048, 512], P('mem'), may hold values from -0.29882812 to 0.29882812
- memory_values: bfloat16 [65536, 1024], P(('grp', 'mem')), may hold values from -6 to 6
- gate_weight: bfloat16 [1024, 1024], P('mem'), may hold values from -0.1875 to 0.1875
- out_weight: bfloat16 [1024, 1024], P('mem'), may hold values from -0.25 to 0.25
- out_cotangent: bfloat16 [4096, 1024], P(('grp', 'mem')), may hold values from -6 to 6
Outputs:
- block_out: bfloat16 [4096, 1024], P(('grp', 'mem'))
- tokens_grad: float32 [4096, 1024], P(('grp', 'mem'))
- attn_gain_grad: float32 [1024], P('mem')
- qkv_weight_grad: float32 [1024, 3072], P('mem')
- attn_proj_grad: float32 [1024, 1024], P('mem')
- mem_gain_grad: float32 [1024], P('mem')
- query_weight_grad: float32 [1024, 4096], P('mem')
- half_keys_grad: float32 [2048, 512], P('mem')
- memory_values_grad: float32 [65536, 1024], P(('grp', 'mem'))
- gate_weight_grad: float32 [1024, 1024], P('mem')
- out_weight_grad: float32 [1024, 1024], P('mem')
Inputs may be any that keep to these rules, and one draw needn't show every extreme that they name: Of the picks of the 128 tokens that one device of grp+mem holds, at most 1024 fall in the 2048 value rows that any one device holds; one such block of rows receives exactly 1024 from every device.
All inputs are finite; a program needn't handle non-finite values.
Results may differ from a plain program's by a relative error of at most 0.02.
Values may be sent and summed in bfloat16 or wider, within the bound.
A program may use at most 384 MiB of HBM per device.

v0:
```python
import math

import jax
import jax.numpy as jnp
from jax import lax
from jax.sharding import PartitionSpec as P

HEADS = 16
HDIM = 64
MHEADS = 4
NK = 256
HALF = 512
TOPK = 32


def rms_norm(values, gain):
    return values * lax.rsqrt(jnp.mean(values * values, axis=-1, keepdims=True) + 1e-05) * gain


def block_scores(query_heads, key_block, query_pos, query_seg, key_start, key_seg):
    scores = (
        jnp.einsum("qhd,khd->hqk", query_heads, key_block, preferred_element_type=jnp.float32)
        * 0.125
    )
    key_pos = key_start + jnp.arange(key_block.shape[0], dtype=jnp.int32)
    allowed = (key_pos[None, :] <= query_pos[:, None]) & (key_seg[None, :] == query_seg[:, None])
    return jnp.where(allowed[None], scores, -1e30)


def block_live(query_pos, query_seg, key_start, key_seg):
    return (
        (key_start <= query_pos[-1]) & (key_seg[0] <= query_seg[-1]) & (key_seg[-1] >= query_seg[0])
    )


def per_device(
    tokens,
    segment_ids,
    picks,
    attn_gain,
    qkv_weight,
    attn_proj,
    mem_gain,
    query_weight,
    half_keys,
    memory_values,
    gate_weight,
    out_weight,
    out_cotangent,
):
    gain_one, qkv_full, proj_full, gain_two, query_full, keys_full, gate_full, output_full = (
        lax.all_gather(attn_gain, "mem", axis=0, tiled=True),
        lax.all_gather(qkv_weight, "mem", axis=0, tiled=True),
        lax.all_gather(attn_proj, "mem", axis=0, tiled=True),
        lax.all_gather(mem_gain, "mem", axis=0, tiled=True),
        lax.all_gather(query_weight, "mem", axis=0, tiled=True),
        lax.all_gather(half_keys, "mem", axis=0, tiled=True),
        lax.all_gather(gate_weight, "mem", axis=0, tiled=True),
        lax.all_gather(out_weight, "mem", axis=0, tiled=True),
    )
    width = tokens.shape[1]
    rows_here = tokens.shape[0]
    group_len = segment_ids.shape[0]
    first_row = lax.axis_index("mem") * rows_here
    positions = first_row + jnp.arange(rows_here, dtype=jnp.int32)
    own_segments = lax.dynamic_slice_in_dim(segment_ids, first_row, rows_here)
    block_len = min(512, group_len)
    block_count = group_len // block_len
    seg_blocks = segment_ids.reshape(block_count, block_len)
    block_starts = jnp.arange(block_count, dtype=jnp.int32) * block_len
    inputs = tokens.astype(jnp.float32)
    normed_one, norm_one_back = jax.vjp(rms_norm, inputs, gain_one.astype(jnp.float32))
    normed_low = normed_one.astype(jnp.bfloat16)
    projected = jnp.dot(normed_low, qkv_full, preferred_element_type=jnp.float32).astype(
        jnp.bfloat16
    )
    queries = projected[:, :width]
    keys_own = projected[:, width : 2 * width]
    values_own = projected[:, 2 * width :]
    keys_all, values_all = (
        lax.all_gather(keys_own, "mem", axis=0, tiled=True),
        lax.all_gather(values_own, "mem", axis=0, tiled=True),
    )
    query_heads = queries.reshape(rows_here, HEADS, HDIM)
    key_blocks = keys_all.reshape(block_count, block_len, HEADS, HDIM)
    value_blocks = values_all.reshape(block_count, block_len, HEADS, HDIM)

    def stats_step(carry, block):
        run_max, run_sum = carry
        key_block, key_seg, key_start = block

        def stats_update():
            scores = block_scores(
                query_heads, key_block, positions, own_segments, key_start, key_seg
            )
            new_max = jnp.maximum(run_max, jnp.max(scores, axis=-1))
            new_sum = run_sum * jnp.exp(run_max - new_max) + jnp.sum(
                jnp.exp(scores - new_max[..., None]), axis=-1
            )
            return (new_max, new_sum)

        live = block_live(positions, own_segments, key_start, key_seg)
        return (lax.cond(live, stats_update, lambda: (run_max, run_sum)), None)

    start_stats = (
        jnp.full((HEADS, rows_here), -1e30, jnp.float32),
        jnp.zeros((HEADS, rows_here), jnp.float32),
    )
    (row_max, row_sum), _ = lax.scan(
        stats_step, start_stats, (key_blocks, seg_blocks, block_starts)
    )

    def probs_of(key_block, key_seg, key_start):
        scores = block_scores(query_heads, key_block, positions, own_segments, key_start, key_seg)
        return jnp.exp(scores - row_max[..., None]) / row_sum[..., None]

    def output_step(total, block):
        key_block, value_block, key_seg, key_start = block

        def output_update():
            probs_low = probs_of(key_block, key_seg, key_start).astype(jnp.bfloat16)
            return total + jnp.einsum(
                "hqk,khd->qhd", probs_low, value_block, preferred_element_type=jnp.float32
            )

        live = block_live(positions, own_segments, key_start, key_seg)
        return (lax.cond(live, output_update, lambda: total), None)

    attn_sum, _ = lax.scan(
        output_step,
        jnp.zeros((rows_here, HEADS, HDIM), jnp.float32),
        (key_blocks, value_blocks, seg_blocks, block_starts),
    )
    attended = attn_sum.reshape(rows_here, width).astype(jnp.bfloat16)
    residual = inputs + jnp.dot(attended, proj_full, preferred_element_type=jnp.float32)
    normed_two, norm_two_back = jax.vjp(rms_norm, residual, gain_two.astype(jnp.float32))
    second_low = normed_two.astype(jnp.bfloat16)
    mem_query = jnp.dot(second_low, query_full, preferred_element_type=jnp.float32).astype(
        jnp.bfloat16
    )
    half_query = mem_query.reshape(rows_here, MHEADS, 2, HALF)
    key_table = keys_full.reshape(MHEADS, 2, NK, HALF)
    half_scores = jnp.einsum(
        "thcf,hcnf->thcn", half_query, key_table, preferred_element_type=jnp.float32
    )
    first_index = picks // NK
    second_index = picks % NK
    pick_scores = jnp.take_along_axis(
        half_scores[:, :, 0], first_index, axis=2
    ) + jnp.take_along_axis(half_scores[:, :, 1], second_index, axis=2)
    pick_weights = jax.nn.softmax(pick_scores, axis=-1)
    weights_low = pick_weights.astype(jnp.bfloat16)
    total_picks = rows_here * MHEADS * TOPK
    local_rows = memory_values.shape[0]
    grp_size = lax.axis_size("grp")
    mem_size = lax.axis_size("mem")
    owners = grp_size * mem_size
    capacity = 2 * total_picks // owners
    slots_total = owners * capacity
    flat_picks = picks.reshape(total_picks)
    owner_of = flat_picks // local_rows
    row_of = flat_picks % local_rows
    ranking = jnp.argsort(owner_of, stable=True)
    counts = jnp.sum(
        (owner_of[:, None] == jnp.arange(owners, dtype=jnp.int32)[None, :]).astype(jnp.int32),
        axis=0,
    )
    owner_starts = jnp.cumsum(counts) - counts
    sorted_owner = owner_of[ranking]
    sorted_slot = (
        sorted_owner * capacity
        + jnp.arange(total_picks, dtype=jnp.int32)
        - owner_starts[sorted_owner]
    )
    slot_of = jnp.zeros((total_picks,), jnp.int32).at[ranking].set(sorted_slot)
    requests = (
        jnp.full((slots_total,), -1, jnp.int32).at[slot_of].set(row_of).reshape(owners, capacity)
    )
    arrived = lax.all_to_all(requests, ("grp", "mem"), split_axis=0, concat_axis=0, tiled=True)
    block_rows = math.gcd(slots_total, 2048)
    row_ids = jnp.arange(local_rows, dtype=jnp.int32)
    wanted_blocks = arrived.reshape(slots_total // block_rows, block_rows)

    def fetch(wanted):
        one_hot = (wanted[:, None] == row_ids[None, :]).astype(jnp.bfloat16)
        return jnp.dot(one_hot, memory_values, preferred_element_type=jnp.float32).astype(
            jnp.bfloat16
        )

    served = lax.map(fetch, wanted_blocks).reshape(owners, capacity, width)
    returned = lax.all_to_all(served, ("grp", "mem"), split_axis=0, concat_axis=0, tiled=True)
    picked_rows = returned.reshape(slots_total, width)[slot_of].reshape(
        rows_here, MHEADS * TOPK, width
    )
    flat_weights = weights_low.reshape(rows_here, MHEADS * TOPK)
    memory_out = jnp.einsum(
        "tj,tjd->td", flat_weights, picked_rows, preferred_element_type=jnp.float32
    )
    gate_pre = jnp.dot(second_low, gate_full, preferred_element_type=jnp.float32)
    gate_act, gate_back = jax.vjp(jax.nn.silu, gate_pre)
    mixed = (memory_out * gate_act).astype(jnp.bfloat16)
    block_out = (residual + jnp.dot(mixed, output_full, preferred_element_type=jnp.float32)).astype(
        jnp.bfloat16
    )
    out_w_grad = jnp.dot(mixed.T, out_cotangent, preferred_element_type=jnp.float32)
    mixed_grad = jnp.dot(out_cotangent, output_full.T, preferred_element_type=jnp.float32)
    memory_grad = (mixed_grad * gate_act).astype(jnp.bfloat16)
    gate_grad = gate_back(mixed_grad * memory_out)[0].astype(jnp.bfloat16)
    gate_w_grad = jnp.dot(second_low.T, gate_grad, preferred_element_type=jnp.float32)
    row_grads = (
        flat_weights[:, :, None].astype(jnp.float32) * memory_grad[:, None, :].astype(jnp.float32)
    ).astype(jnp.bfloat16)
    weight_grad = jnp.einsum(
        "tjd,td->tj", picked_rows, memory_grad, preferred_element_type=jnp.float32
    ).reshape(rows_here, MHEADS, TOPK)
    score_grad = (
        pick_weights * (weight_grad - jnp.sum(pick_weights * weight_grad, axis=-1, keepdims=True))
    ).astype(jnp.bfloat16)
    send_back = (
        jnp.zeros((slots_total, width), jnp.bfloat16)
        .at[slot_of]
        .set(row_grads.reshape(total_picks, width))
    )
    grads_home = lax.all_to_all(
        send_back.reshape(owners, capacity, width),
        ("grp", "mem"),
        split_axis=0,
        concat_axis=0,
        tiled=True,
    )

    def accumulate(total, block):
        wanted, grads_block = block
        one_hot = (wanted[:, None] == row_ids[None, :]).astype(jnp.bfloat16)
        return (
            total
            + jnp.einsum("sr,sd->rd", one_hot, grads_block, preferred_element_type=jnp.float32),
            None,
        )

    values_grad, _ = lax.scan(
        accumulate,
        jnp.zeros((local_rows, width), jnp.float32),
        (wanted_blocks, grads_home.reshape(slots_total // block_rows, block_rows, width)),
    )
    index_range = jnp.arange(NK, dtype=jnp.int32)
    score_full = score_grad.astype(jnp.float32)
    first_hot = (first_index[..., None] == index_range).astype(jnp.float32)
    second_hot = (second_index[..., None] == index_range).astype(jnp.float32)
    half_grad = jnp.stack(
        [
            jnp.einsum("thj,thjn->thn", score_full, first_hot, precision=lax.Precision.HIGHEST),
            jnp.einsum("thj,thjn->thn", score_full, second_hot, precision=lax.Precision.HIGHEST),
        ],
        axis=2,
    )
    query_grad = (
        jnp.einsum(
            "thcn,hcnf->thcf",
            half_grad,
            key_table.astype(jnp.float32),
            precision=lax.Precision.HIGHEST,
        )
        .astype(jnp.bfloat16)
        .reshape(rows_here, MHEADS * 2 * HALF)
    )
    keys_grad = jnp.einsum(
        "thcn,thcf->hcnf",
        half_grad,
        half_query.astype(jnp.float32),
        precision=lax.Precision.HIGHEST,
    ).reshape(MHEADS * 2 * NK, HALF)
    query_w_grad = jnp.dot(second_low.T, query_grad, preferred_element_type=jnp.float32)
    second_grad = jnp.dot(gate_grad, gate_full.T, preferred_element_type=jnp.float32) + jnp.dot(
        query_grad, query_full.T, preferred_element_type=jnp.float32
    )
    resid_from_norm, gain_two_grad = norm_two_back(second_grad)
    resid_grad = out_cotangent.astype(jnp.float32) + resid_from_norm
    resid_low = resid_grad.astype(jnp.bfloat16)
    proj_grad = jnp.dot(attended.T, resid_low, preferred_element_type=jnp.float32)
    attn_grad = jnp.dot(resid_low, proj_full.T, preferred_element_type=jnp.float32).astype(
        jnp.bfloat16
    )
    attn_grad = attn_grad.reshape(rows_here, HEADS, HDIM)

    def delta_step(total, block):
        key_block, value_block, key_seg, key_start = block

        def delta_update():
            probs = probs_of(key_block, key_seg, key_start)
            dprobs = jnp.einsum(
                "qhd,khd->hqk", attn_grad, value_block, preferred_element_type=jnp.float32
            )
            return total + jnp.sum(probs * dprobs, axis=-1)

        live = block_live(positions, own_segments, key_start, key_seg)
        return (lax.cond(live, delta_update, lambda: total), None)

    delta, _ = lax.scan(
        delta_step,
        jnp.zeros((HEADS, rows_here), jnp.float32),
        (key_blocks, value_blocks, seg_blocks, block_starts),
    )

    def grad_step(total, block):
        key_block, value_block, key_seg, key_start = block

        def grad_update():
            probs = probs_of(key_block, key_seg, key_start)
            probs_low = probs.astype(jnp.bfloat16)
            dprobs = jnp.einsum(
                "qhd,khd->hqk", attn_grad, value_block, preferred_element_type=jnp.float32
            )
            scores_low = (probs * (dprobs - delta[..., None])).astype(jnp.bfloat16)
            new_total = (
                total
                + jnp.einsum(
                    "hqk,khd->qhd", scores_low, key_block, preferred_element_type=jnp.float32
                )
                * 0.125
            )
            key_part = (
                jnp.einsum(
                    "hqk,qhd->khd", scores_low, query_heads, preferred_element_type=jnp.float32
                )
                * 0.125
            )
            value_part = jnp.einsum(
                "hqk,qhd->khd", probs_low, attn_grad, preferred_element_type=jnp.float32
            )
            return (
                new_total,
                key_part.reshape(block_len, width),
                value_part.reshape(block_len, width),
            )

        def skipped():
            empty = jnp.zeros((block_len, width), jnp.float32)
            return (total, empty, empty)

        live = block_live(positions, own_segments, key_start, key_seg)
        new_total, key_part, value_part = lax.cond(live, grad_update, skipped)
        return (new_total, (key_part, value_part))

    query_sum, (key_parts, value_parts) = lax.scan(
        grad_step,
        jnp.zeros((rows_here, HEADS, HDIM), jnp.float32),
        (key_blocks, value_blocks, seg_blocks, block_starts),
    )
    key_sum, value_sum = (
        lax.psum_scatter(
            key_parts.reshape(group_len, width).astype(jnp.bfloat16),
            "mem",
            scatter_dimension=0,
            tiled=True,
        ).astype(jnp.float32),
        lax.psum_scatter(
            value_parts.reshape(group_len, width).astype(jnp.bfloat16),
            "mem",
            scatter_dimension=0,
            tiled=True,
        ).astype(jnp.float32),
    )
    qkv_rows = jnp.concatenate(
        [
            query_sum.reshape(rows_here, width).astype(jnp.bfloat16),
            key_sum.astype(jnp.bfloat16),
            value_sum.astype(jnp.bfloat16),
        ],
        axis=1,
    )
    qkv_w_grad = jnp.dot(normed_low.T, qkv_rows, preferred_element_type=jnp.float32)
    first_grad = jnp.dot(qkv_rows, qkv_full.T, preferred_element_type=jnp.float32)
    input_from_norm, gain_one_grad = norm_one_back(first_grad)
    tokens_grad = resid_grad + input_from_norm
    shares = (
        lax.psum_scatter(
            gain_one_grad.astype(jnp.bfloat16), "mem", scatter_dimension=0, tiled=True
        ).astype(jnp.float32),
        lax.psum_scatter(
            qkv_w_grad.astype(jnp.bfloat16), "mem", scatter_dimension=0, tiled=True
        ).astype(jnp.float32),
        lax.psum_scatter(
            proj_grad.astype(jnp.bfloat16), "mem", scatter_dimension=0, tiled=True
        ).astype(jnp.float32),
        lax.psum_scatter(
            gain_two_grad.astype(jnp.bfloat16), "mem", scatter_dimension=0, tiled=True
        ).astype(jnp.float32),
        lax.psum_scatter(
            query_w_grad.astype(jnp.bfloat16), "mem", scatter_dimension=0, tiled=True
        ).astype(jnp.float32),
        lax.psum_scatter(
            keys_grad.astype(jnp.bfloat16), "mem", scatter_dimension=0, tiled=True
        ).astype(jnp.float32),
        lax.psum_scatter(
            gate_w_grad.astype(jnp.bfloat16), "mem", scatter_dimension=0, tiled=True
        ).astype(jnp.float32),
        lax.psum_scatter(
            out_w_grad.astype(jnp.bfloat16), "mem", scatter_dimension=0, tiled=True
        ).astype(jnp.float32),
    )
    totals = (
        lax.psum(shares[0].astype(jnp.bfloat16), "grp").astype(jnp.float32),
        lax.psum(shares[1].astype(jnp.bfloat16), "grp").astype(jnp.float32),
        lax.psum(shares[2].astype(jnp.bfloat16), "grp").astype(jnp.float32),
        lax.psum(shares[3].astype(jnp.bfloat16), "grp").astype(jnp.float32),
        lax.psum(shares[4].astype(jnp.bfloat16), "grp").astype(jnp.float32),
        lax.psum(shares[5].astype(jnp.bfloat16), "grp").astype(jnp.float32),
        lax.psum(shares[6].astype(jnp.bfloat16), "grp").astype(jnp.float32),
        lax.psum(shares[7].astype(jnp.bfloat16), "grp").astype(jnp.float32),
    )
    return (
        block_out,
        tokens_grad,
        totals[0],
        totals[1],
        totals[2],
        totals[3],
        totals[4],
        totals[5],
        values_grad,
        totals[6],
        totals[7],
    )


def solution(mesh):
    placed = (
        P(("grp", "mem"), None),
        P("grp"),
        P(("grp", "mem"), None, None),
        P("mem"),
        P("mem", None),
        P("mem", None),
        P("mem"),
        P("mem", None),
        P("mem", None),
        P(("grp", "mem"), None),
        P("mem", None),
        P("mem", None),
        P(("grp", "mem"), None),
    )
    return jax.shard_map(
        per_device,
        mesh=mesh,
        in_specs=placed,
        out_specs=(
            P(("grp", "mem"), None),
            P(("grp", "mem"), None),
            P("mem"),
            P("mem", None),
            P("mem", None),
            P("mem"),
            P("mem", None),
            P("mem", None),
            P(("grp", "mem"), None),
            P("mem", None),
            P("mem", None),
        ),
        check_vma=False,
    )
```

profile of v0, /device:TPU:0, one launch (start us, length us, event | category | flops | bytes accessed | tf_op | source)
XLA Modules:
  0.0 5055.0 jit_solution(478578805095108014)
XLA Ops:
  18.9 90.7 %gather_fusion = s32[16384]{0:T(1024)S(1)} fusion(s32[16384]{0:T(1024)S(1)} %get-tuple-element.1133, s32[16384]{0:T(1024)S(1)} %get-tuple-element.1134), kind=kCustom, calls=%fused_computation.2 | custom fusion | bytes 196608 | tf_op jit(solution)/shard_map/gather | solution.py:169
  119.4 16.0 select_subtract_fusion
  135.4 60.3 %scatter_custom_fusion = s32[16384]{0:T(1024)S(1)} fusion(s32[16384]{0:T(1024)S(1)} %get-tuple-element.1135, s32[16384]{0:T(1024)S(1)} %select_subtract_fusion, s32[]{:T(128)} %constant.210.clone.1), kind=kCustom, calls=%fused_computation.243 | custom fusion | bytes 65540 | tf_op jit(solution)/shard_map/scatter | solution.py:175
  196.4 60.9 %scatter_custom_fusion.1 = s32[32768]{0:T(1024)} fusion(s32[16384]{0:T(1024)S(1)} %get-tuple-element.1131, s32[16384]{0:T(1024)S(1)} %get-tuple-element.1132, s32[]{:T(128)} %constant.222.clone.1), kind=kCustom, calls=%fused_computation.236 | custom fusion | bytes 131076 | tf_op jit(solution)/shard_map/scatter | solution.py:177
  273.4 201.9 %while.81 = (s32[]{:T(128)}, bf16[16,2048,1024]{2,1,0:T(8,128)(2,1)}, s32[16,2048]{1,0:T(8,128)S(1)}, bf16[2048,1024]{1,0:T(8,128)(2,1)}, s32[]{:T(128)}) while((s32[]{:T(128)}, bf16[16,2048,1024]{2,1,0:T(8,128)(2,1)}, s32[16,2048]{1,0:T(8,128)S(1)}, bf16[2048,1024]{1,0:T(8,128)(2,1)}, s32[]{:T(128)}) %tuple.285), condition=%wide.region_20.22_spmd.clone, body=%wide.region_19.21_spmd.clone.sunk | while | flops 8596226048 | bytes 8413261 | solution.py:190
  273.4 12.7 bitcast_dynamic-update-slice_fusion.2
  286.1 12.6 bitcast_dynamic-update-slice_fusion.2
  298.7 12.6 bitcast_dynamic-update-slice_fusion.2
  311.3 12.6 bitcast_dynamic-update-slice_fusion.2
  323.9 12.6 bitcast_dynamic-update-slice_fusion.2
  336.5 12.6 bitcast_dynamic-update-slice_fusion.2
  349.1 12.6 bitcast_dynamic-update-slice_fusion.2
  361.7 12.6 bitcast_dynamic-update-slice_fusion.2
  374.3 12.6 bitcast_dynamic-update-slice_fusion.2
  386.9 12.6 bitcast_dynamic-update-slice_fusion.2
  399.6 12.6 bitcast_dynamic-update-slice_fusion.2
  412.2 12.6 bitcast_dynamic-update-slice_fusion.2
  424.9 12.6 bitcast_dynamic-update-slice_fusion.2
  437.5 12.6 bitcast_dynamic-update-slice_fusion.2
  450.1 12.6 bitcast_dynamic-update-slice_fusion.2
  462.7 12.6 bitcast_dynamic-update-slice_fusion.2
  481.8 1137.1 %all-gather = bf16[8,1,128]{2,1,0:T(2,128)(2,1)S(1)} all-gather(bf16[1,1,128]{2,1,0:T(2,128)(2,1)S(1)} %bitcast.356), channel_id=1, replica_groups=mesh['grp'=4,'mem'=8] {'mem'}, dimensions={0}, use_global_device_ids=true | all-gather | bytes 2304 | tf_op jit(solution)/shard_map/all_gather | solution.py:52
  1628.5 367.0 %all-gather.1 = bf16[8,1,128]{2,1,0:T(2,128)(2,1)S(1)} all-gather(bf16[1,1,128]{2,1,0:T(2,128)(2,1)S(1)} %bitcast.357), channel_id=1, replica_groups=mesh['grp'=4,'mem'=8] {'mem'}, dimensions={0}, use_global_device_ids=true | all-gather | bytes 2304 | tf_op jit(solution)/shard_map/all_gather | solution.py:55
  2021.4 19.5 all-gather.15.cloned.1.call-done
  2052.7 15.3 while.77
  2068.1 16.5 while.78
  2092.0 61.9 %all-gather.19.cloned.1.call-done = bf16[1024,4096]{1,0:T(8,128)(2,1)} async-done(((bf16[128,4096]{1,0:T(8,128)(2,1)}), bf16[1024,4096]{1,0:T(8,128)(2,1)}) %all-gather.19.cloned.1.call-update) | async-done | bytes 8388624 | tf_op jit(solution)/shard_map/all_gather | solution.py:56
  2162.3 20.8 all-gather.21.cloned.1.call-done
  2186.0 157.2 %gather_fusion.3 = f32[16384]{0:T(1024)S(1)} fusion(f32[128,4,256]{2,0,1:T(8,128)S(1)} %get-tuple-element.1123, s32[16384]{0:T(1024)S(1)} %reshape.732), kind=kCustom, calls=%fused_computation.1.clone | custom fusion | bytes 327680 | tf_op jit(solution)/shard_map/jit(take_along_axis)/gather | solution.py:150
  2343.4 157.4 %gather_fusion.2 = f32[16384]{0:T(1024)S(1)} fusion(f32[128,4,256]{2,0,1:T(8,128)S(1)} %get-tuple-element.1122, s32[16384]{0:T(1024)S(1)} %reshape.727), kind=kCustom, calls=%fused_computation.clone | custom fusion | bytes 327680 | tf_op jit(solution)/shard_map/jit(take_along_axis)/gather | solution.py:148
  2504.9 299.7 %gather_fusion.1 = bf16[16384,1024]{1,0:T(8,128)(2,1)} fusion(bf16[32768,1024]{1,0:T(8,128)(2,1)} %bitcast.98, s32[16384]{0:T(1024)S(1)} %copy-done.52), kind=kCustom, calls=%fused_computation.3 | custom fusion | bytes 67174400 | tf_op jit(solution)/shard_map/gather | solution.py:192
  2804.6 12.9 fusion.136
  2831.9 256.0 %scatter_custom_fusion.2 = bf16[32768,1024]{1,0:T(8,128)(2,1)} fusion(s32[16384]{0:T(1024)} %get-tuple-element.942, bf16[16384,1024]{1,0:T(8,128)(2,1)} %fusion.66, s32[16384]{0:T(1024)} %broadcast_clamp_fusion.1, bf16[]{:T(256)} %constant.225.clone.1), kind=kCustom, calls=%fused_computation.102 | custom fusion | bytes 67109376 | tf_op jit(solution)/shard_map/scatter | solution.py:222
  3093.0 14.2 fusion.98
  3134.4 17.0 while.79
  3152.3 36.2 while.80
  3206.5 107.7 %reduce-scatter.27.cloned.1.call-done = bf16[128,1024]{1,0:T(8,128)(2,1)} async-done(((bf16[1024,1024]{1,0:T(8,128)(2,1)}), bf16[128,1024]{1,0:T(8,128)(2,1)}) %reduce-scatter.27.cloned.1.call-update) | async-done | bytes 262160
  3315.2 92.9 %reduce-scatter.25.cloned.1.call-done = bf16[128,1024]{1,0:T(8,128)(2,1)} async-done(((bf16[1024,1024]{1,0:T(8,128)(2,1)}), bf16[128,1024]{1,0:T(8,128)(2,1)}) %reduce-scatter.25.cloned.1.call-update) | async-done | bytes 262160
  3413.9 208.3 %reduce-scatter.15.cloned.1.call-done = bf16[128,1024]{1,0:T(8,128)(2,1)} async-done(((bf16[1024,1024]{1,0:T(8,128)(2,1)}), bf16[128,1024]{1,0:T(8,128)(2,1)}) %reduce-scatter.15.cloned.1.call-update) | async-done | bytes 262160 | tf_op jit(solution)/shard_map/reduce_scatter | solution.py:383
  3622.2 155.3 %reduce-scatter.19.cloned.1.call-done = bf16[256,512]{1,0:T(8,128)(2,1)} async-done(((bf16[2048,512]{1,0:T(8,128)(2,1)}), bf16[256,512]{1,0:T(8,128)(2,1)}) %reduce-scatter.19.cloned.1.call-update) | async-done | bytes 262160 | tf_op jit(solution)/shard_map/reduce_scatter | solution.py:392
  3777.5 186.0 %reduce-scatter.21.cloned.1.call-done = bf16[128,1024]{1,0:T(8,128)(2,1)} async-done(((bf16[1024,1024]{1,0:T(8,128)(2,1)}), bf16[128,1024]{1,0:T(8,128)(2,1)}) %reduce-scatter.21.cloned.1.call-update) | async-done | bytes 262160 | tf_op jit(solution)/shard_map/reduce_scatter | solution.py:395
  3963.6 113.0 %reduce-scatter.23.cloned.1.call-done = bf16[128,1024]{1,0:T(8,128)(2,1)} async-done(((bf16[1024,1024]{1,0:T(8,128)(2,1)}), bf16[128,1024]{1,0:T(8,128)(2,1)}) %reduce-scatter.23.cloned.1.call-update) | async-done | bytes 262160 | tf_op jit(solution)/shard_map/reduce_scatter | solution.py:398
  4076.6 239.4 %reduce-scatter.17.cloned.1.call-done = bf16[128,4096]{1,0:T(8,128)(2,1)} async-done(((bf16[1024,4096]{1,0:T(8,128)(2,1)}), bf16[128,4096]{1,0:T(8,128)(2,1)}) %reduce-scatter.17.cloned.1.call-update) | async-done | bytes 1048592 | tf_op jit(solution)/shard_map/reduce_scatter | solution.py:389
  4315.9 194.3 %reduce-scatter.13.cloned.1.call-done = bf16[128,3072]{1,0:T(8,128)(2,1)} async-done(((bf16[1024,3072]{1,0:T(8,128)(2,1)}), bf16[128,3072]{1,0:T(8,128)(2,1)}) %reduce-scatter.13.cloned.1.call-update) | async-done | bytes 786448 | tf_op jit(solution)/shard_map/reduce_scatter | solution.py:380
  4519.4 48.8 all-reduce.2
  4580.2 80.6 %all-reduce.7.cloned.1.call-done = (bf16[128,3072]{1,0:T(8,128)(2,1)}, bf16[128,1024]{1,0:T(8,128)(2,1)}, bf16[128,4096]{1,0:T(8,128)(2,1)}, bf16[256,512]{1,0:T...) async-done(((bf16[128,3072]{1,0:T(8,128)(2,1)}, bf16[128,1024]{1,0:T(8,128)(2,1)}, bf16[128,4096]{1,0:T(8,128)(2,1)}, bf16[256,512]{1,0:T(8,128)(2,1)}, ...) | async-done | bytes 2883600 | tf_op jit(solution)/shard_map/psum | solution.py:404
  4670.5 121.5 %all-to-all-done.2 = bf16[32,1024,1024]{2,1,0:T(8,128)(2,1)} async-done(((bf16[32,1024,1024]{2,1,0:T(8,128)(2,1)}), bf16[32,1024,1024]{2,1,0:T(8,128)(2,1)}, u32[]{:S(2)}, u32[]{:S(2)}) %all-to-all-start.2) | async-done | bytes 67108896 | tf_op jit(solution)/shard_map/all_to_all | solution.py:224
  4792.0 256.0 %while.82 = (s32[]{:T(128)}, f32[2048,1024]{1,0:T(8,128)}, s32[16,2048]{1,0:T(8,128)}, bf16[16,2048,1024]{2,1,0:T(8,128)(2,1)}, s32[]{:T(128)}, /*index=5*/s32[]{:T(128)}) while((s32[]{:T(128)}, f32[2048,1024]{1,0:T(8,128)}, s32[16,2048]{1,0:T(8,128)}, bf16[16,2048,1024]{2,1,0:T(8,128)(2,1)}, s32[]{:T(128)}, ...), condition=%wide.region_51.53_spmd.clone, body=%wide.region_50.52_spmd.clone.sunk | while | flops 8598323200 | bytes 20996188 | solution.py:241
  4792.8 14.0 select_add_fusion.4
  4807.7 15.2 select_add_fusion.4
  4823.8 15.2 select_add_fusion.4
  4839.9 15.2 select_add_fusion.4
  4855.9 15.2 select_add_fusion.4
  4872.0 15.2 select_add_fusion.4
  4888.1 15.2 select_add_fusion.4
  4904.2 15.2 select_add_fusion.4
  4920.3 15.2 select_add_fusion.4
  4936.3 15.2 select_add_fusion.4
  4952.4 15.2 select_add_fusion.4
  4968.5 15.2 select_add_fusion.4
  4984.6 15.2 select_add_fusion.4
  5000.7 15.2 select_add_fusion.4
  5016.7 15.2 select_add_fusion.4
  5032.8 15.2 select_add_fusion.4
  (427 shorter events, 302.0 us)
Async XLA Ops:
  257.3 15.7 all-to-all-start
  475.3 6.5 copy-start.75
  475.3 1143.7 %copy-start.14 = (bf16[128,1024]{1,0:T(8,128)(2,1)S(1)}, bf16[128,1024]{1,0:T(8,128)(2,1)}, u32[]{:S(2)}) copy-start(bf16[128,1024]{1,0:T(8,128)(2,1)} %param.35) | copy-start | bytes 786436
  475.9 2028.9 %all-to-all-start.1 = ((bf16[32,1024,1024]{2,1,0:T(8,128)(2,1)}), bf16[32,1024,1024]{2,1,0:T(8,128)(2,1)}, u32[]{:S(2)}, u32[]{:S(2)}) async-start(bf16[32,1024,1024]{2,1,0:T(8,128)(2,1)} %bitcast.97), calls=%async_computation.1 | async-start | bytes 134217728 | tf_op jit(solution)/shard_map/all_to_all | solution.py:191
  481.0 1138.1 %all-gather.11.cloned.1.call-start = ((), (), s32[]{:S(2)}) async-start(), calls=%async_computation.11 | async-start | bytes 7077888 | tf_op jit(solution)/shard_map/all_gather | solution.py:53
  481.7 1528.3 %all-gather.13.cloned.1.call-start = ((), (), s32[]{:S(2)}) async-start(), calls=%async_computation.12 | async-start | bytes 2359296 | tf_op jit(solution)/shard_map/all_gather | solution.py:81
  1619.1 4.4 copy-start.68
  1623.5 4.9 copy-start.72
  1623.5 5.0 copy-start.76
  1623.5 372.0 %copy-start.32 = (s32[128,4,32]{2,1,0:T(4,128)S(1)}, s32[128,4,32]{2,1,0:T(4,128)}, u32[]{:S(2)}) copy-start(s32[128,4,32]{2,1,0:T(4,128)} %copy-done.31) | copy-start | bytes 196612
  1624.4 416.5 %all-gather.15.cloned.1.call-start = ((), (), s32[]{:S(2)}) async-start(), calls=%async_computation.13 | async-start | bytes 2359296 | tf_op jit(solution)/shard_map/all_gather | solution.py:82
  1625.1 463.0 %all-gather.17.cloned.1.call-start = ((), (), s32[]{:S(2)}) async-start(), calls=%async_computation.14 | async-start | bytes 2359296 | tf_op jit(solution)/shard_map/all_gather | solution.py:54
  1625.7 528.3 %all-gather.19.cloned.1.call-start = ((), (), s32[]{:S(2)}) async-start(), calls=%async_computation.15 | async-start | bytes 9437184 | tf_op jit(solution)/shard_map/all_gather | solution.py:56
  1626.3 556.8 %all-gather.21.cloned.1.call-start = ((), (), s32[]{:S(2)}) async-start(), calls=%async_computation.16 | async-start | bytes 2359296 | tf_op jit(solution)/shard_map/all_gather | solution.py:57
  1626.8 875.9 %all-gather.23.cloned.1.call-start = ((), (), s32[]{:S(2)}) async-start(), calls=%async_computation.17 | async-start | bytes 2359296 | tf_op jit(solution)/shard_map/all_gather | solution.py:58
  1627.6 1189.9 %all-gather.25.cloned.1.call-start = ((), (), s32[]{:S(2)}) async-start(), calls=%async_computation.18 | async-start | bytes 2359296 | tf_op jit(solution)/shard_map/all_gather | solution.py:59
  1995.4 95.7 %copy-start.64 = (f32[8,1,128]{2,1,0:T(1,128)}, f32[8,1,128]{2,1,0:T(1,128)S(1)}, u32[]{:S(2)}) copy-start(f32[8,1,128]{2,1,0:T(1,128)S(1)} %convert_element_type.258) | copy-start | bytes 12292
  2088.0 71.6 %copy-start = (bf16[2,512,16,64]{1,3,2,0:T(8,128)(2,1)}, bf16[2,512,16,64]{1,3,2,0:T(8,128)(2,1)S(1)}, u32[]{:S(2)}) copy-start(bf16[2,512,16,64]{1,3,2,0:T(8,128)(2,1)S(1)} %get-tuple-element.1810) | copy-start | bytes 6291460
  2088.0 71.6 %copy-start.4 = (bf16[128,16,64]{0,2,1:T(8,128)(2,1)}, bf16[128,16,64]{0,2,1:T(8,128)(2,1)S(1)}, u32[]{:S(2)}) copy-start(bf16[128,16,64]{0,2,1:T(8,128)(2,1)S(1)} %get-tuple-element.1813) | copy-start | bytes 786436
  2088.1 71.5 %copy-start.33 = (bf16[128,16,64]{0,2,1:T(8,128)(2,1)}, bf16[128,16,64]{0,2,1:T(8,128)(2,1)S(1)}, u32[]{:S(2)}) copy-start(bf16[128,16,64]{0,2,1:T(8,128)(2,1)S(1)} %convert_element_type.212) | copy-start | bytes 786436
  2091.1 68.5 %copy-start.77 = (f32[128]{0:T(128)}, f32[128]{0:T(128)S(1)}, u32[]{:S(2)}) copy-start(f32[128]{0:T(128)S(1)} %get-tuple-element.1168) | copy-start | bytes 1540
  2091.2 68.5 %copy-start.70 = (f32[128]{0:T(128)}, f32[128]{0:T(128)S(1)}, u32[]{:S(2)}) copy-start(f32[128]{0:T(128)S(1)} %fusion.119) | copy-start | bytes 1540
  2092.0 67.6 %copy-start.16 = (bf16[128,1024]{1,0:T(8,128)(2,1)}, bf16[128,1024]{1,0:T(8,128)(2,1)S(1)}, u32[]{:S(2)}) copy-start(bf16[128,1024]{1,0:T(8,128)(2,1)S(1)} %multiply_convert_fusion.1) | copy-start | bytes 786436
  2343.4 157.6 %copy-start.53 = (s32[128,4,32]{2,1,0:T(4,128)S(1)}, s32[128,4,32]{2,1,0:T(4,128)}, u32[]{:S(2)}) copy-start(s32[128,4,32]{2,1,0:T(4,128)} %get-tuple-element.1098) | copy-start | bytes 196612
  2343.4 157.6 %copy-start.55 = (s32[128,4,32]{2,1,0:T(4,128)S(1)}, s32[128,4,32]{2,1,0:T(4,128)}, u32[]{:S(2)}) copy-start(s32[128,4,32]{2,1,0:T(4,128)} %get-tuple-element.1129) | copy-start | bytes 196612
  2343.4 159.4 %copy-start.17 = (bf16[128,1024]{1,0:T(8,128)(2,1)S(1)}, bf16[128,1024]{1,0:T(8,128)(2,1)}, u32[]{:S(2)}) copy-start(bf16[128,1024]{1,0:T(8,128)(2,1)} %copy-done.16) | copy-start | bytes 786436
  2500.8 4.0 copy-start.52
  2501.6 303.0 %copy-start.60 = (f32[128,4,32]{2,1,0:T(4,128)}, f32[128,4,32]{2,1,0:T(4,128)S(1)}, u32[]{:S(2)}) copy-start(f32[128,4,32]{2,1,0:T(4,128)S(1)} %get-tuple-element.1171) | copy-start | bytes 196612
  2804.6 12.9 copy-start.37
  3087.8 1704.2 %all-to-all-start.2 = ((bf16[32,1024,1024]{2,1,0:T(8,128)(2,1)}), bf16[32,1024,1024]{2,1,0:T(8,128)(2,1)}, u32[]{:S(2)}, u32[]{:S(2)}) async-start(bf16[32,1024,1024]{2,1,0:T(8,128)(2,1)} %bitcast.118), calls=%async_computation.6 | async-start | bytes 134217728 | tf_op jit(solution)/shard_map/all_to_all | solution.py:224
  3092.9 221.2 %reduce-scatter.27.cloned.1.call-start = ((), (), s32[]{:S(2)}) async-start(), calls=%async_computation.26 | async-start | bytes 2359296
  3093.0 14.5 copy-start.61
  3093.0 14.5 copy-start.67
  3107.2 5.9 copy-start.56
  3113.1 4.0 copy-start.54
  3117.2 5.2 copy-start.24
  3124.2 6.8 copy-start.20
  3124.3 6.8 copy-start.12
  3124.3 6.8 copy-start.22
  3124.3 6.8 copy-start.41
  3124.3 6.8 copy-start.65
  3124.3 6.8 copy-start.71
  3124.3 7.9 copy-start.78
  3124.3 7.9 copy-start.38
  3188.5 219.6 %reduce-scatter.25.cloned.1.call-start = ((), (), s32[]{:S(2)}) async-start(), calls=%async_computation.25 | async-start | bytes 2359296
  3189.1 433.1 %reduce-scatter.15.cloned.1.call-start = ((), (), s32[]{:S(2)}) async-start(), calls=%async_computation.20 | async-start | bytes 2359296 | tf_op jit(solution)/shard_map/reduce_scatter | solution.py:383
  3191.6 3.6 copy-start.18
  3191.6 3.6 copy-start.42
  3191.6 585.9 %reduce-scatter.19.cloned.1.call-start = ((), (), s32[]{:S(2)}) async-start(), calls=%async_computation.22 | async-start | bytes 2359296 | tf_op jit(solution)/shard_map/reduce_scatter | solution.py:392
  3195.2 4.4 copy-start.21
  3195.2 768.4 %reduce-scatter.21.cloned.1.call-start = ((), (), s32[]{:S(2)}) async-start(), calls=%async_computation.23 | async-start | bytes 2359296 | tf_op jit(solution)/shard_map/reduce_scatter | solution.py:395
  3197.4 879.2 %reduce-scatter.23.cloned.1.call-start = ((), (), s32[]{:S(2)}) async-start(), calls=%async_computation.24 | async-start | bytes 2359296 | tf_op jit(solution)/shard_map/reduce_scatter | solution.py:398
  3199.5 1116.4 %reduce-scatter.17.cloned.1.call-start = ((), (), s32[]{:S(2)}) async-start(), calls=%async_computation.21 | async-start | bytes 9437184 | tf_op jit(solution)/shard_map/reduce_scatter | solution.py:389
  3205.4 203.9 %copy-start.15 = (bf16[128,1024]{1,0:T(8,128)(2,1)S(1)}, bf16[128,1024]{1,0:T(8,128)(2,1)}, u32[]{:S(2)}) copy-start(bf16[128,1024]{1,0:T(8,128)(2,1)} %param.35) | copy-start | bytes 786436
  3205.4 203.9 %copy-start.48 = (f32[8,1,128]{2,1,0:T(1,128)S(1)}, f32[8,1,128]{2,1,0:T(1,128)}, u32[]{:S(2)}) copy-start(f32[8,1,128]{2,1,0:T(1,128)} %copy-done.47) | copy-start | bytes 12292
  3205.4 203.9 %copy-start.69 = (f32[128]{0:T(128)S(1)}, f32[128]{0:T(128)}, u32[]{:S(2)}) copy-start(f32[128]{0:T(128)} %copy-done.68) | copy-start | bytes 1540
  3205.4 1304.9 %reduce-scatter.13.cloned.1.call-start = ((), (), s32[]{:S(2)}) async-start(), calls=%async_computation.19 | async-start | bytes 7077888 | tf_op jit(solution)/shard_map/reduce_scatter | solution.py:380
  3413.8 1096.5 %copy-start.79 = (u32[32]{0:T(128)S(1)}, u32[32]{0:T(128)}, u32[]{:S(2)}) copy-start(u32[32]{0:T(128)} %constant.326) | copy-start | bytes 388
  3413.8 1097.7 %copy-start.13 = (f32[128,1024]{1,0:T(8,128)S(1)}, f32[128,1024]{1,0:T(8,128)}, u32[]{:S(2)}) copy-start(f32[128,1024]{1,0:T(8,128)} %copy-done.11) | copy-start | bytes 1572868
  3413.9 1247.0 %all-reduce.7.cloned.1.call-start = ((), (), s32[]{:S(2)}) async-start(), calls=%async_computation.27 | async-start | bytes 5767168 | tf_op jit(solution)/shard_map/psum | solution.py:404
  4514.3 64.9 %copy-start.74 = (f32[128]{0:T(128)S(1)}, f32[128]{0:T(128)}, u32[]{:S(2)}) copy-start(f32[128]{0:T(128)} %copy-done.73) | copy-start | bytes 1540
  4660.9 7.1 copy-start.59
  4660.9 7.9 copy-start.58
  4660.9 8.8 copy-start.57
  (40 other events, 68.1 us)
Sparse Core Ops, SparseCore 0:
  483.5 152.8 all-gather.10
  1624.5 385.5 all-gather.12
  2012.2 28.5 all-gather.14
  2042.3 28.5 all-gather.16
  2072.4 81.5 all-gather.18
  2155.4 27.6 all-gather.20
  2184.7 28.5 all-gather.22
  2214.9 28.6 all-gather.24
  3188.7 125.4 reduce-scatter.26
  3316.3 91.7 reduce-scatter.24
  3411.0 211.2 reduce-scatter.14
  3624.4 153.1 reduce-scatter.18
  3779.8 183.7 reduce-scatter.20
  3965.7 110.8 reduce-scatter.22
  4079.3 236.5 reduce-scatter.16
  4318.1 192.1 reduce-scatter.12
  4513.8 146.9 all-reduce.6
where the time goes:
time: 5090 us; the launch traced here: 5060 us
  waiting for transfers between devices  1620 us (32%)
  blocking collectives  1560 us (31%)
  local copies, waits for them, and re-layouts  1180 us (23%)
  matrix products  551 us (11%)
  other arithmetic  78.8 us (2%)
    all_gather x1, blocking collectives, per_device(): lax.all_gather(attn_gain, 'mem', axis=0, tiled=True)  1140 us
    all_gather x1, blocking collectives, per_device(): lax.all_gather(mem_gain, 'mem', axis=0, tiled=True)  367 us
    gather x1, local copies, waits for them, and re-layouts, per_device(): returned.reshape(slots_total, width)[slot_of]  300 us
    scatter x2, local copies, waits for them, and re-layouts, per_device(): send_back = jnp.zeros((slots_total, width), jnp.bfloat16).at[slot_of].set...  256 us
    dot_general x16, matrix products, accumulate(): jnp.einsum('sr,sd->rd', one_hot, grads_block, preferred_element_type=jnp....  242 us
    reduce_scatter x1, waiting for transfers between devices, per_device(): lax.psum_scatter(query_w_grad.astype(jnp.bfloat16), 'mem', scatter_dimens...  239 us
    reduce_scatter x1, waiting for transfers between devices, per_device(): lax.psum_scatter(proj_grad.astype(jnp.bfloat16), 'mem', scatter_dimension...  208 us
    unnamed x19, waiting for transfers between devices  206 us
  transfers between devices with their start and end apart: 20, of which 15 were waited for; matrix products, arithmetic and copies ran while one was open for 16% of the time, Pallas kernels for 0%

commit v1 on v0

v1 whole, which is shorter than its diff:
```python
import functools

import jax
import jax.numpy as jnp
from jax import lax
from jax.experimental import pallas as pl
from jax.experimental.pallas import tpu as pltpu
from jax.sharding import PartitionSpec as P

HEADS = 16
HDIM = 64
MHEADS = 4
NK = 256
HALF = 512
TOPK = 32
EPS = 1e-05
LANES = 128
ALL = ("grp", "mem")
BF = jnp.bfloat16
F32 = jnp.float32
NEG = -1e30


def dot(left, right, dims=((1,), (0,))):
    return lax.dot_general(left, right, (dims, ((), ())), preferred_element_type=F32)


NT = ((1,), (1,))
TN = ((0,), (0,))


def iota(shape, dim):
    return lax.broadcasted_iota(jnp.int32, shape, dim)


def lane_halves(rows):
    first = iota((rows, LANES), 1) < HDIM
    return first


def half_masks():
    lane = iota((1, LANES), 1)
    return ((lane < HDIM).astype(BF), (lane >= HDIM).astype(BF))


def attn_fwd_kernel(rows, win, pos_ref, q_ref, k_ref, v_ref, qseg_ref, kseg_ref, out_ref, lse_ref):
    pair = pl.program_id(0)
    row0 = pos_ref[0] * rows
    start = pl.multiple_of(jnp.maximum(row0 + rows - win, 0), LANES)
    keys = k_ref[pl.ds(start, win), :]
    values = v_ref[pl.ds(start, win), :]
    key_pos = start + iota((rows, win), 1)
    query_pos = row0 + iota((rows, win), 0)
    allowed = (key_pos <= query_pos) & (kseg_ref[:, pl.ds(start, win)] == qseg_ref[...])
    lane = iota((rows, LANES), 1)
    masks = half_masks()
    outs = []
    lse = jnp.where(pair == 0, jnp.zeros((rows, LANES), F32), lse_ref[...])
    for half in range(2):
        scores = dot(q_ref[...] * masks[half], keys, NT) * 0.125
        scores = jnp.where(allowed, scores, NEG)
        top = jnp.max(scores, axis=1, keepdims=True)
        weights = jnp.exp(scores - top)
        total = jnp.sum(weights, axis=1, keepdims=True)
        probs = weights * (1.0 / total)
        outs.append(dot(probs.astype(BF), values))
        lse = jnp.where(lane == pair * 2 + half, top + jnp.log(total), lse)
    out_ref[...] = jnp.where(lane < HDIM, outs[0], outs[1])
    lse_ref[...] = lse


def attn_fwd(pos, qkv, seg_row, seg_col, rows):
    group_len, width = qkv.shape[0], qkv.shape[1] // 3
    pairs = width // LANES
    win = min(group_len, group_len // 2 + rows)
    return pl.pallas_call(
        functools.partial(attn_fwd_kernel, rows, win),
        grid_spec=pltpu.PrefetchScalarGridSpec(
            num_scalar_prefetch=1,
            grid=(pairs,),
            in_specs=[
                pl.BlockSpec((rows, LANES), lambda h, p: (p[0], h)),
                pl.BlockSpec((group_len, LANES), lambda h, p: (0, pairs + h)),
                pl.BlockSpec((group_len, LANES), lambda h, p: (0, 2 * pairs + h)),
                pl.BlockSpec((rows, 1), lambda h, p: (p[0], 0)),
                pl.BlockSpec((1, group_len), lambda h, p: (0, 0)),
            ],
            out_specs=[
                pl.BlockSpec((rows, LANES), lambda h, p: (0, h)),
                pl.BlockSpec((rows, LANES), lambda h, p: (0, 0)),
            ],
        ),
        out_shape=[
            jax.ShapeDtypeStruct((rows, width), F32),
            jax.ShapeDtypeStruct((rows, LANES), F32),
        ],
        cost_estimate=pl.CostEstimate(
            flops=4 * rows * win * width,
            bytes_accessed=group_len * width * 4,
            transcendentals=rows * win * HEADS,
        ),
        name="attn_fwd",
    )(pos, qkv, qkv, qkv, seg_col, seg_row)


def attn_bwd_kernel(
    rows, win, pairs, pos_ref, q_ref, k_ref, v_ref, da_ref, stat_ref, segc_ref, segr_ref, out_ref
):
    pair = pl.program_id(0)
    group_len = k_ref.shape[0]
    row0 = pl.multiple_of(pos_ref[0] * rows, LANES)
    start = pl.multiple_of(jnp.maximum(row0 + rows - win, 0), LANES)
    qstart = pl.multiple_of(jnp.minimum(row0, group_len - win), LANES)
    own, back, ahead = pl.ds(row0, rows), pl.ds(start, win), pl.ds(qstart, win)
    masks = half_masks()
    lane = iota((rows, LANES), 1)

    def stat(where, index, count):
        table = stat_ref[where, :]
        return jnp.sum(
            jnp.where(iota((count, table.shape[1]), 1) == index, table, 0.0),
            axis=1,
            keepdims=True,
        )

    allowed = (start + iota((rows, win), 1) <= row0 + iota((rows, win), 0)) & (
        segr_ref[:, back] == segc_ref[own, :]
    )
    allowed_two = (row0 + iota((win, rows), 1) <= qstart + iota((win, rows), 0)) & (
        segr_ref[:, own] == segc_ref[ahead, :]
    )
    dqs, dks, dvs = [], [], []
    for half in range(2):
        head = pair * 2 + half
        lse, delta = stat(own, head, rows), stat(own, HEADS + head, rows)
        keys = k_ref[back, :]
        scores = dot(q_ref[own, :] * masks[half], keys, NT) * 0.125
        probs = jnp.exp(jnp.where(allowed, scores - lse, NEG))
        dprobs = dot(da_ref[own, :] * masks[half], v_ref[back, :], NT)
        grads = (probs * (dprobs - delta)).astype(BF)
        dqs.append(dot(grads, keys))
        lse, delta = stat(ahead, head, win), stat(ahead, HEADS + head, win)
        queries, douts = q_ref[ahead, :], da_ref[ahead, :]
        scores = dot(queries * masks[half], k_ref[own, :], NT) * 0.125
        probs = jnp.exp(jnp.where(allowed_two, scores - lse, NEG))
        dprobs = dot(douts * masks[half], v_ref[own, :], NT)
        grads = (probs * (dprobs - delta)).astype(BF)
        dks.append(dot(grads, queries, TN))
        dvs.append(dot(probs.astype(BF), douts, TN))
    width = pairs * LANES
    for i, (parts, scale) in enumerate(((dqs, 0.125), (dks, 0.125), (dvs, 1.0))):
        column = pl.multiple_of(i * width + pair * LANES, LANES)
        out_ref[:, pl.ds(column, LANES)] = (
            jnp.where(lane < HDIM, parts[0], parts[1]) * scale
        ).astype(BF)


def attn_bwd(pos, qkv, douts, stats, seg_row, seg_col, rows):
    group_len, width = douts.shape
    pairs = width // LANES
    win = min(group_len, group_len // 2 + rows)
    return pl.pallas_call(
        functools.partial(attn_bwd_kernel, rows, win, pairs),
        grid_spec=pltpu.PrefetchScalarGridSpec(
            num_scalar_prefetch=1,
            grid=(pairs,),
            in_specs=[
                pl.BlockSpec((group_len, LANES), lambda h, p: (0, h)),
                pl.BlockSpec((group_len, LANES), lambda h, p: (0, pairs + h)),
                pl.BlockSpec((group_len, LANES), lambda h, p: (0, 2 * pairs + h)),
                pl.BlockSpec((group_len, LANES), lambda h, p: (0, h)),
                pl.BlockSpec(stats.shape, lambda h, p: (0, 0)),
                pl.BlockSpec((group_len, 1), lambda h, p: (0, 0)),
                pl.BlockSpec((1, group_len), lambda h, p: (0, 0)),
            ],
            out_specs=pl.BlockSpec((rows, 3 * width), lambda h, p: (0, 0)),
        ),
        out_shape=jax.ShapeDtypeStruct((rows, 3 * width), BF),
        cost_estimate=pl.CostEstimate(
            flops=14 * rows * win * width,
            bytes_accessed=group_len * width * 8,
            transcendentals=2 * rows * win * HEADS,
        ),
        name="attn_bwd",
    )(pos, qkv, qkv, qkv, douts, stats, seg_col, seg_row)


def by_head(lane, reduce, fill, values):
    spread = jnp.zeros_like(values)
    for c in range(MHEADS):
        inside = lane // TOPK == c
        spread = jnp.where(
            inside, reduce(jnp.where(inside, values, fill), axis=1, keepdims=True), spread
        )
    return spread


def pick_fwd_kernel(scores_ref, picks_ref, weight_ref, low_ref):
    rows = picks_ref.shape[0]
    lane = iota((rows, LANES), 1)
    picks = picks_ref[...]
    index = (picks // NK, picks % NK)
    total = jnp.zeros((rows, LANES), F32)
    for c in range(MHEADS):
        both = jnp.zeros((rows, LANES), F32)
        for e in range(2):
            base = (c * 2 + e) * NK
            for part in range(NK // LANES):
                table = scores_ref[:, base + part * LANES : base + (part + 1) * LANES]
                found = jnp.take_along_axis(table, index[e] % LANES, axis=1)
                both = both + jnp.where(index[e] // LANES == part, found, 0.0)
        total = jnp.where(lane // TOPK == c, both, total)
    top = by_head(lane, jnp.max, NEG, total)
    weights = jnp.exp(total - top)
    weights = weights / by_head(lane, jnp.sum, 0.0, weights)
    weight_ref[...] = weights
    low_ref[...] = weights.astype(BF)


def pick_fwd(half_scores, picks):
    rows = picks.shape[0]
    return pl.pallas_call(
        pick_fwd_kernel,
        out_shape=[
            jax.ShapeDtypeStruct((rows, LANES), F32),
            jax.ShapeDtypeStruct((rows, LANES), BF),
        ],
        name="pick_fwd",
    )(half_scores, picks)


def pick_bwd_kernel(weight_ref, grad_ref, picks_ref, out_ref):
    rows = picks_ref.shape[0]
    lane = iota((rows, LANES), 1)
    weights, grads, picks = weight_ref[...], grad_ref[...], picks_ref[...]
    score = (weights * (grads - by_head(lane, jnp.sum, 0.0, weights * grads))).astype(BF)
    score = score.astype(F32)
    index = (picks // NK, picks % NK)
    key = iota((rows, NK), 1)
    for c in range(MHEADS):
        totals = [jnp.zeros((rows, NK), F32) for _ in range(2)]
        for j in range(TOPK):
            column = slice(c * TOPK + j, c * TOPK + j + 1)
            for e in range(2):
                totals[e] = totals[e] + jnp.where(
                    key == index[e][:, column], score[:, column], 0.0
                )
        for e in range(2):
            base = (c * 2 + e) * NK
            out_ref[:, base : base + NK] = totals[e].astype(BF)


def pick_bwd(weights, grads, picks):
    rows = picks.shape[0]
    block = 32
    spec = pl.BlockSpec((block, LANES), lambda i: (i, 0))
    return pl.pallas_call(
        pick_bwd_kernel,
        grid=(rows // block,),
        in_specs=[spec, spec, spec],
        out_specs=pl.BlockSpec((block, MHEADS * 2 * NK), lambda i: (i, 0)),
        out_shape=jax.ShapeDtypeStruct((rows, MHEADS * 2 * NK), BF),
        name="pick_bwd",
    )(weights, grads, picks)


def owner_kernel(
    his, flat_bits, local_rows, keys_ref, sent_ref, values_ref, part_ref, spread_ref
):
    rows = part_ref.shape[0]
    width = values_ref.shape[1]
    slots = keys_ref.shape[-1]
    low_rows = local_rows // his
    key = keys_ref[0]
    flat = key & ((1 << flat_bits) - 1)
    dummy = ((key >> flat_bits) & 1) == 1
    row = (key >> (flat_bits + 1)) % local_rows
    token = flat // LANES
    pick = flat % LANES
    token = jnp.where(dummy, -1, token)
    block = jnp.where(dummy, -1, (row // low_rows) * rows + token)
    low_row = row % low_rows
    grad = sent_ref[:, :width]
    weights = sent_ref[:, width:]
    is_token = iota((rows, slots), 0) == token
    is_pick = iota((LANES, slots), 0) == pick
    token_hot = is_token.astype(F32).astype(BF)
    found = dot(weights, token_hot, TN)
    weight = jnp.sum(jnp.where(is_pick, found, 0.0), axis=0, keepdims=True)
    is_block = iota((his * rows, slots), 0) == block
    is_low = iota((low_rows, slots), 0) == low_row
    low_hot = is_low.astype(F32).astype(BF)
    spread = dot(jnp.where(is_block, weight, 0.0).astype(BF), low_hot, NT).astype(BF)
    total = jnp.zeros((rows, width), F32)
    products = []
    for h in range(his):
        table = values_ref[h * low_rows : (h + 1) * low_rows, :]
        piece = spread[h * rows : (h + 1) * rows, :]
        spread_ref[h] = piece
        total = total + dot(piece, table)
        products.append(dot(grad, table, NT).astype(BF))
    picked = dot(jnp.concatenate(products, axis=0), is_block.astype(F32).astype(BF), TN)
    picked = jnp.sum(jnp.where(is_low, picked, 0.0), axis=0, keepdims=True)
    part_ref[:, :width] = total.astype(BF)
    part_ref[:, width:] = dot(
        jnp.where(is_token, picked, 0.0).astype(BF), is_pick.astype(F32).astype(BF), NT
    ).astype(BF)


def owner_call(keys, sent, values, flat_bits):
    owners, slots = keys.shape
    rows = sent.shape[0] // owners
    local_rows, width = values.shape
    his = 4
    low_rows = local_rows // his
    return pl.pallas_call(
        functools.partial(owner_kernel, his, flat_bits, local_rows),
        grid=(owners,),
        in_specs=[
            pl.BlockSpec((1, 1, slots), lambda s: (s, 0, 0)),
            pl.BlockSpec((rows, width + LANES), lambda s: (s, 0)),
            pl.BlockSpec((local_rows, width), lambda s: (0, 0)),
        ],
        out_specs=[
            pl.BlockSpec((rows, width + LANES), lambda s: (s, 0)),
            pl.BlockSpec((his, rows, low_rows), lambda s: (0, s, 0)),
        ],
        out_shape=[
            jax.ShapeDtypeStruct((owners * rows, width + LANES), BF),
            jax.ShapeDtypeStruct((his, owners * rows, low_rows), BF),
        ],
        compiler_params=pltpu.CompilerParams(vmem_limit_bytes=48 * 1024 * 1024),
        cost_estimate=pl.CostEstimate(
            flops=2 * owners * rows * local_rows * (2 * slots + 2 * width),
            bytes_accessed=owners * rows * (2 * width + local_rows) * 2,
            transcendentals=0,
        ),
        name="owner",
    )(keys.reshape(owners, 1, slots), sent, values)


def route(picks, owners, local_rows, capacity, flat_bits):
    total = picks.size
    rows_of = picks.reshape(total)
    flat = jnp.arange(total, dtype=jnp.int32)
    each = jnp.arange(owners, dtype=jnp.int32)
    counts = jnp.sum((rows_of[:, None] // local_rows == each[None, :]).astype(jnp.int32), axis=0)
    ends = jnp.cumsum(capacity - counts)
    spares = owners * capacity - total
    spare_owner = jnp.sum(
        (jnp.arange(spares, dtype=jnp.int32)[:, None] >= ends[None, :]).astype(jnp.int32), axis=1
    )
    real = (rows_of << (flat_bits + 1)) + flat
    spare = ((spare_owner * local_rows + local_rows - 1) << (flat_bits + 1)) + (1 << flat_bits)
    keys = lax.sort(jnp.concatenate([real, spare]))
    return keys.reshape(owners, capacity)


def rms_scale(values):
    return lax.rsqrt(jnp.mean(values * values, axis=-1, keepdims=True) + EPS)


def rms_back(values, scale, gain, grad):
    scaled = grad * gain
    inner = jnp.mean(values * scaled, axis=-1, keepdims=True)
    gain_grad = jnp.sum(grad * values * scale, axis=0)
    return scale * scaled - values * (scale * scale * scale * inner), gain_grad


def per_device(
    tokens,
    segment_ids,
    picks,
    attn_gain,
    qkv_weight,
    attn_proj,
    mem_gain,
    query_weight,
    half_keys,
    memory_values,
    gate_weight,
    out_weight,
    out_cotangent,
):
    rows, width = tokens.shape
    owners = lax.axis_size("grp") * lax.axis_size("mem")
    local_rows = memory_values.shape[0]
    total_picks = rows * MHEADS * TOPK
    flat_bits = (total_picks - 1).bit_length()
    capacity = 2 * total_picks // owners
    group_len = segment_ids.shape[0]
    position = lax.axis_index("mem").astype(jnp.int32)
    pos = position.reshape(1)

    def gather(x, axes="mem"):
        return lax.all_gather(x, axes, axis=0, tiled=True)

    gains = lax.all_gather(jnp.stack([attn_gain, mem_gain]), "mem", axis=1, tiled=True)
    gains = gains.astype(F32)
    gain_one, gain_two = gains[0:1], gains[1:2]
    tokens_all = gather(tokens)
    qkv_full = gather(qkv_weight)
    proj_full = gather(attn_proj)
    query_full = gather(query_weight)
    keys_full = gather(half_keys)
    gate_full = gather(gate_weight)
    output_full = gather(out_weight)

    requests = route(picks, owners, local_rows, capacity, flat_bits)
    arrived = lax.all_to_all(requests, ALL, split_axis=0, concat_axis=0, tiled=True)

    inputs_all = tokens_all.astype(F32)
    first_all = (inputs_all * rms_scale(inputs_all) * gain_one).astype(BF)
    qkv_all = dot(first_all, qkv_full).astype(BF)
    seg_row, seg_col = segment_ids.reshape(1, group_len), segment_ids.reshape(group_len, 1)
    attn_sum, lse = attn_fwd(pos, qkv_all, seg_row, seg_col, rows)
    attended = attn_sum.astype(BF)
    inputs = tokens.astype(F32)
    residual = inputs + dot(attended, proj_full)
    scale_two = rms_scale(residual)
    second = (residual * scale_two * gain_two).astype(BF)
    mem_query = dot(second, query_full).astype(BF)
    gate_pre = dot(second, gate_full)
    mixed_grad = dot(out_cotangent, output_full, NT)
    sig = jax.nn.sigmoid(gate_pre)
    gate_act = gate_pre * sig
    memory_grad = (mixed_grad * gate_act).astype(BF)
    key_table = keys_full.reshape(MHEADS * 2, NK, HALF)
    half_scores = jnp.einsum(
        "tcf,cnf->tcn",
        mem_query.reshape(rows, MHEADS * 2, HALF),
        key_table,
        preferred_element_type=F32,
    ).reshape(rows, MHEADS * 2 * NK)
    flat_picks = picks.reshape(rows, MHEADS * TOPK)
    pick_weights, weights_low = pick_fwd(half_scores, flat_picks)

    sent = gather(jnp.concatenate([memory_grad, weights_low], axis=1), ALL)
    part, spread = owner_call(arrived, sent, memory_values, flat_bits)
    back = lax.psum_scatter(part, "grp", scatter_dimension=0, tiled=True)
    back = lax.psum_scatter(back, "mem", scatter_dimension=0, tiled=True)
    values_grad = jnp.einsum(
        "hkl,kd->hld", spread, sent[:, :width], preferred_element_type=F32
    ).reshape(local_rows, width)

    memory_out = back[:, :width].astype(F32)
    weight_grad = back[:, width:].astype(F32)
    mixed = (memory_out * gate_act).astype(BF)
    block_out = (residual + dot(mixed, output_full)).astype(BF)
    out_w_grad = dot(mixed, out_cotangent, TN)
    gate_grad = (mixed_grad * memory_out * (sig * (1.0 + gate_pre * (1.0 - sig)))).astype(BF)
    gate_w_grad = dot(second, gate_grad, TN)
    half_grad = pick_bwd(pick_weights, weight_grad, flat_picks)
    half_cube = half_grad.reshape(rows, MHEADS * 2, NK)
    query_grad = (
        jnp.einsum("tcn,cnf->tcf", half_cube, key_table, preferred_element_type=F32)
        .astype(BF)
        .reshape(rows, MHEADS * 2 * HALF)
    )
    keys_grad = jnp.einsum(
        "tcn,tcf->cnf",
        half_cube,
        mem_query.reshape(rows, MHEADS * 2, HALF),
        preferred_element_type=F32,
    ).reshape(MHEADS * 2 * NK, HALF)
    query_w_grad = dot(second, query_grad, TN)
    second_grad = dot(gate_grad, gate_full, NT) + dot(query_grad, query_full, NT)
    resid_from_norm, gain_two_grad = rms_back(residual, scale_two, gain_two, second_grad)
    resid_grad = out_cotangent.astype(F32) + resid_from_norm
    resid_low = resid_grad.astype(BF)
    proj_grad = dot(attended, resid_low, TN)
    attn_grad = dot(resid_low, proj_full, NT).astype(BF)
    delta = jnp.sum(
        (attn_grad.astype(F32) * attn_sum).reshape(rows, HEADS, HDIM), axis=-1
    )
    stats = jnp.concatenate([lse[:, :HEADS], delta], axis=1)
    stats_high = lax.reduce_precision(stats, 8, 7)
    stats_low = stats - stats_high
    shared = gather(
        jnp.concatenate(
            [
                resid_low,
                stats_high.astype(BF),
                stats_low.astype(BF),
                jnp.zeros((rows, LANES - 4 * HEADS), BF),
            ],
            axis=1,
        )
    )
    stats_all = shared[:, width : width + 2 * HEADS].astype(F32) + shared[
        :, width + 2 * HEADS : width + 4 * HEADS
    ].astype(F32)
    attn_grad_all = dot(shared[:, :width], proj_full, NT).astype(BF)
    qkv_rows = attn_bwd(pos, qkv_all, attn_grad_all, stats_all, seg_row, seg_col, rows)
    scale_one = rms_scale(inputs)
    first_low = (inputs * scale_one * gain_one).astype(BF)
    qkv_w_grad = dot(first_low, qkv_rows, TN)
    first_grad = dot(qkv_rows, qkv_full, NT)
    input_from_norm, gain_one_grad = rms_back(inputs, scale_one, gain_one, first_grad)
    tokens_grad = resid_grad + input_from_norm

    def scatter(x):
        return lax.psum_scatter(x.astype(BF), "mem", scatter_dimension=0, tiled=True)

    shares = [
        scatter(x) for x in (out_w_grad, gate_w_grad, keys_grad, query_w_grad, proj_grad, qkv_w_grad)
    ]
    shares = lax.psum(tuple(shares), "grp")
    gain_sums = lax.psum(jnp.stack([gain_one_grad, gain_two_grad]), ALL)
    gain_sums = lax.dynamic_slice_in_dim(
        gain_sums, position * attn_gain.shape[0], attn_gain.shape[0], axis=1
    )
    out_share, gate_share, keys_share, query_share, proj_share, qkv_share = (
        x.astype(F32) for x in shares
    )
    return (
        block_out,
        tokens_grad,
        gain_sums[0],
        qkv_share,
        proj_share,
        gain_sums[1],
        query_share,
        keys_share,
        values_grad,
        gate_share,
        out_share,
    )


def solution(mesh):
    placed = (
        P(ALL, None),
        P("grp"),
        P(ALL, None, None),
        P("mem"),
        P("mem", None),
        P("mem", None),
        P("mem"),
        P("mem", None),
        P("mem", None),
        P(ALL, None),
        P("mem", None),
        P("mem", None),
        P(ALL, None),
    )
    return jax.shard_map(
        per_device,
        mesh=mesh,
        in_specs=placed,
        out_specs=(
            P(ALL, None),
            P(ALL, None),
            P("mem"),
            P("mem", None),
            P("mem", None),
            P("mem"),
            P("mem", None),
            P("mem", None),
            P(ALL, None),
            P("mem", None),
            P("mem", None),
        ),
        check_vma=False,
    )
```

time: 5090 us -> 1130 us (0.22)
  blocking collectives: 1560 us -> 63.7 us
  local copies, waits for them, and re-layouts: 1180 us -> 14.2 us
  waiting for transfers between devices: 1620 us -> 750 us
  matrix products: 551 us -> 95.3 us
  Pallas kernels: 0 us -> 155 us
    all_gather x2 -> x1, blocking collectives: 1500 us -> 13.5 us  [per_device(): lax.all_gather(jnp.stack([attn_gain, mem_gain]), 'mem', axis=1, tiled=True)]
    gather x10 -> x0, local copies, waits for them, and re-layouts: 707 us -> none  [the longest x1 300 us: per_device(): returned.reshape(slots_total, width)[slot_of]]
    reduce_scatter x6 -> x8, waiting for transfers between devices: 1100 us -> 406 us  [the longest x6 274 us: scatter(): lax.psum_scatter(x.astype(BF), 'mem', scatter_dimension=0, tiled=True)]
    dot_general x63 -> x20, matrix products: 551 us -> 95.3 us  [the longest x16 62.5 us: dot(): lax.dot_general(left, right, (dims, ((), ())), preferred_element_type=F32)]
    scatter x4 -> x0, local copies, waits for them, and re-layouts: 377 us -> none  [the longest x2 256 us: per_device(): send_back = jnp.zeros((slots_total, width), jnp.bfloat16).at[slot_of].set...]
    all_gather x8 -> x9, waiting for transfers between devices: 106 us -> 322 us  [gather(): return lax.all_gather(x, axes, axis=0, tiled=True)]
    unnamed x19 -> x18, waiting for transfers between devices: 206 us -> 4.51 us
    pallas_call x0 -> x5, Pallas kernels: none -> 155 us  [the longest x1 118 us: owner_call(): pl.pallas_call(functools.partial(owner_kernel, his, flat_bits, local_rows...]
  transfers between devices with their start and end apart: 20 -> 18, of which waited for: 15 -> 18; matrix products, arithmetic and copies ran while one was open for 16% -> 9% of each run, Pallas kernels for 0% -> 2%
where the time goes in v1:
time: 1130 us
  waiting for transfers between devices  750 us (66%)
  Pallas kernels  155 us (14%)
  matrix products  95.3 us (8%)
  blocking collectives  63.7 us (6%)
  other arithmetic  32.8 us (3%)
  between operations  15 us (1%)
  local copies, waits for them, and re-layouts  14.2 us (1%)
    all_gather x9, waiting for transfers between devices, gather(): return lax.all_gather(x, axes, axis=0, tiled=True)  322 us
    reduce_scatter x6, waiting for transfers between devices, scatter(): lax.psum_scatter(x.astype(BF), 'mem', scatter_dimension=0, tiled=True)  274 us
    pallas_call x1, Pallas kernels, owner_call(): pl.pallas_call(functools.partial(owner_kernel, his, flat_bits, local_rows...  118 us
    reduce_scatter x1, waiting for transfers between devices, per_device(): back = lax.psum_scatter(part, 'grp', scatter_dimension=0, tiled=True)  93.7 us
    dot_general x16, matrix products, dot(): lax.dot_general(left, right, (dims, ((), ())), preferred_element_type=F32)  62.5 us
    reduce_scatter x1, waiting for transfers between devices, per_device(): back = lax.psum_scatter(back, 'mem', scatter_dimension=0, tiled=True)  38.4 us
    psum x1, blocking collectives, per_device(): gain_sums = lax.psum(jnp.stack([gain_one_grad, gain_two_grad]), ALL)  38 us
    dot_general x1, matrix products, per_device(): jnp.einsum('hkl,kd->hld', spread, sent[:, :width], preferred_element_type...  24.2 us
  transfers between devices with their start and end apart: 18, of which 18 were waited for; matrix products, arithmetic and copies ran while one was open for 9% of the time, Pallas kernels for 2%

profile of v1, /device:TPU:0, one launch (start us, length us, event | category | flops | bytes accessed | tf_op | source)
XLA Modules:
  0.0 1127.6 jit_solution(18223657266551676436)
XLA Ops:
  12.0 13.5 %all_gather.31 = bf16[2,1024]{1,0:T(2,128)(2,1)S(1)} all-gather(bf16[2,128]{1,0:T(2,128)(2,1)S(1)} %pad_maximum_fusion.3), channel_id=1, replica_groups=mesh['grp'=4,'mem'=8] {'mem'}, dimensions={1}, use_global_device_ids=true | all-gather | bytes 4608 | tf_op jit(solution)/shard_map/all_gather | solution.py:398
  25.5 1.0 copy.78.qseg_ref.segc_ref
  27.3 14.2 %all-gather.10.cloned.1.call-done = bf16[1024,1024]{1,0:T(8,128)(2,1)} async-done(((bf16[128,1024]{1,0:T(8,128)(2,1)}), bf16[1024,1024]{1,0:T(8,128)(2,1)}) %all-gather.10.cloned.1.call-update) | async-done | bytes 2097168 | tf_op jit(solution)/shard_map/all_gather | solution.py:396
  41.5 2.2 fusion.1
  43.7 63.7 %all-gather.12.cloned.1.call-done = bf16[1024,3072]{1,0:T(8,128)(2,1)} async-done(((bf16[128,3072]{1,0:T(8,128)(2,1)}), bf16[1024,3072]{1,0:T(8,128)(2,1)}) %all-gather.12.cloned.1.call-update) | async-done | bytes 6291472 | tf_op jit(solution)/shard_map/all_gather | solution.py:396
  107.4 11.6 %convolution_convert_fusion.2.q_ref.k_ref.v_ref = bf16[1024,3072]{1,0:T(8,128)(2,1)} fusion(bf16[1024,3072]{1,0:T(8,128)(2,1)} %all-gather.12.cloned.1.call-done, bf16[1024,1024]{1,0:T(8,128)(2,1)S(1)} %copy-done.10, f32[1024]{0:T(1024)S(1)} %bitcast.83, f32[1024]{0:T(1024)S(1)} %add_rsqrt_fusion), kind=kOutput, calls=%fused_computation.4 | convolution fusion | flops 6449790976 | bytes 14688256 | tf_op jit(solution)/shard_map/dot_general | solution.py:25
  119.0 10.2 attn_fwd.1
  129.2 7.6 all-gather.14.cloned.1.call-done
  136.8 2.3 multiply_reduce_fusion.2
  139.3 27.6 %all-gather.18.cloned.1.call-done = bf16[1024,1024]{1,0:T(8,128)(2,1)} async-done(((bf16[128,1024]{1,0:T(8,128)(2,1)}), bf16[1024,1024]{1,0:T(8,128)(2,1)}) %all-gather.18.cloned.1.call-update) | async-done | bytes 2097168 | tf_op jit(solution)/shard_map/all_gather | solution.py:396
  166.9 2.0 fusion.46
  168.9 28.0 %all-gather.16.cloned.1.call-done = bf16[1024,1024]{1,0:T(8,128)(2,1)} async-done(((bf16[128,1024]{1,0:T(8,128)(2,1)}), bf16[1024,1024]{1,0:T(8,128)(2,1)}) %all-gather.16.cloned.1.call-update) | async-done | bytes 2097168 | tf_op jit(solution)/shard_map/all_gather | solution.py:396
  197.0 3.2 multiply_convert_fusion
  200.2 79.8 %all-gather.20.cloned.1.call-done = bf16[1024,4096]{1,0:T(8,128)(2,1)} async-done(((bf16[128,4096]{1,0:T(8,128)(2,1)}), bf16[1024,4096]{1,0:T(8,128)(2,1)}) %all-gather.20.cloned.1.call-update) | async-done | bytes 8388624 | tf_op jit(solution)/shard_map/all_gather | solution.py:396
  280.0 4.6 convolution_convert_fusion.3
  284.7 24.6 %all-gather.22.cloned.1.call-done = bf16[2048,512]{1,0:T(8,128)(2,1)} async-done(((bf16[256,512]{1,0:T(8,128)(2,1)}), bf16[2048,512]{1,0:T(8,128)(2,1)}) %all-gather.22.cloned.1.call-update) | async-done | bytes 2097168 | tf_op jit(solution)/shard_map/all_gather | solution.py:396
  309.3 2.4 convolution_bitcast_fusion
  311.7 1.1 copy.96
  312.8 3.0 pick_fwd.1
  315.7 1.5 pad_maximum_fusion
  318.9 11.2 sort.14
  330.0 12.3 %all_to_all.9.keys_ref = s32[32,1,1024]{2,1,0:T(1,128)S(1)} all-to-all(s32[32,1,1024]{2,1,0:T(1,128)S(1)} %bitcast.87), channel_id=1, replica_groups=mesh['grp'=4,'mem'=8] {'grp','mem'}, dimensions={0} | all-to-all | bytes 262144 | tf_op jit(solution)/shard_map/all_to_all | solution.py:410
  342.3 58.3 %all-gather.24.cloned.1.call-done.sent_ref = bf16[4096,1152]{1,0:T(8,128)(2,1)} async-done(((bf16[128,1152]{1,0:T(8,128)(2,1)}), bf16[4096,1152]{1,0:T(8,128)(2,1)}) %all-gather.24.cloned.1.call-update) | async-done | bytes 9437200 | tf_op jit(solution)/shard_map/all_gather | solution.py:396
  400.6 2.2 copy-done
  402.8 118.2 %owner.1 = (bf16[4096,1152]{1,0:T(8,128)(2,1)}, bf16[4,4096,512]{2,1,0:T(8,128)(2,1)}) custom-call(s32[32,1,1024]{2,1,0:T(1,128)S(1)} %all_to_all.9.keys_ref, bf16[4096,1152]{1,0:T(8,128)(2,1)} %all-gather.24.cloned.1.call-done.sent_ref, bf16[2048,1024]{1,0:T(8,128)(2,1)S(1)} %copy-done), custom_call_target="tpu_custom_call" | custom-call | flops 68719476736 | bytes 33554432 | tf_op jit(solution)/shard_map/owner/pallas_call | solution.py:316
  521.1 93.7 %reduce-scatter.9.cloned.1.call-done = bf16[1024,1152]{1,0:T(8,128)(2,1)} async-done(((bf16[4096,1152]{1,0:T(8,128)(2,1)}), bf16[1024,1152]{1,0:T(8,128)(2,1)}) %reduce-scatter.9.cloned.1.call-update) | async-done | bytes 2359312 | tf_op jit(solution)/shard_map/reduce_scatter | solution.py:440
  614.9 38.4 %reduce-scatter.11.cloned.1.call-done = bf16[128,1152]{1,0:T(8,128)(2,1)} async-done(((bf16[1024,1152]{1,0:T(8,128)(2,1)}), bf16[128,1152]{1,0:T(8,128)(2,1)}) %reduce-scatter.11.cloned.1.call-update) | async-done | bytes 294928 | tf_op jit(solution)/shard_map/reduce_scatter | solution.py:441
  653.3 1.4 slice_convert_fusion.grad_ref
  654.6 9.1 pick_bwd.1
  663.7 1.3 copy.94
  665.8 3.1 fusion.12
  669.0 1.6 copy.86
  670.6 1.4 fusion.22
  672.0 6.4 fusion.47
  678.5 1.0 multiply_reduce_fusion
  680.5 1.6 fusion.14
  682.1 2.0 copy.87
  684.2 1.1 bitcast_reduce_fusion
  685.4 0.9 fusion.37
  687.2 3.0 convolution_convert_fusion.6
  690.3 3.1 convolution_convert_fusion.7
  693.4 3.1 convolution_convert_fusion.4
  697.6 2.1 convolution_convert_fusion.5
  699.9 18.4 %all-gather.26.cloned.1.call-done = bf16[1024,1152]{1,0:T(8,128)(2,1)} async-done(((bf16[128,1152]{1,0:T(8,128)(2,1)}), bf16[1024,1152]{1,0:T(8,128)(2,1)}) %all-gather.26.cloned.1.call-update) | async-done | bytes 2359312 | tf_op jit(solution)/shard_map/all_gather | solution.py:396
  718.3 2.0 convert_add_fusion.stat_ref
  720.3 5.9 fusion.9.da_ref
  726.2 15.0 %attn_bwd.1 = bf16[128,3072]{1,0:T(8,128)(2,1)} custom-call(s32[1]{0:T(128)} %bitcast.pos_ref, bf16[1024,3072]{1,0:T(8,128)(2,1)} %convolution_convert_fusion.2.q_ref.k_ref.v_ref, bf16[1024,3072]{1,0:T(8,128)(2,1)} %convolution_convert_fusion.2.q_ref.k_ref.v_ref, bf16[1024,3072]{1,0:T(8,128)(2,1)} %convolution_convert_fusion.2.q_ref.k_ref.v_ref, ...), custom_call_target="tpu_custom_call" | custom-call | flops 1174405120 | bytes 8388608 | tf_op jit(solution)/shard_map/attn_bwd/pallas_call | solution.py:162
  741.2 5.7 convolution_convert_fusion.1
  746.9 5.8 convolution_convert_fusion
  753.0 2.5 reduce-scatter.21.cloned.1.call-done
  755.5 36.6 %reduce-scatter.15.cloned.1.call-done = bf16[128,1024]{1,0:T(8,128)(2,1)} async-done(((bf16[1024,1024]{1,0:T(8,128)(2,1)}), bf16[128,1024]{1,0:T(8,128)(2,1)}) %reduce-scatter.15.cloned.1.call-update) | async-done | bytes 262160 | tf_op jit(solution)/shard_map/reduce_scatter | solution.py:503
  792.1 36.7 %reduce-scatter.19.cloned.1.call-done = bf16[256,512]{1,0:T(8,128)(2,1)} async-done(((bf16[2048,512]{1,0:T(8,128)(2,1)}), bf16[256,512]{1,0:T(8,128)(2,1)}) %reduce-scatter.19.cloned.1.call-update) | async-done | bytes 262160 | tf_op jit(solution)/shard_map/reduce_scatter | solution.py:503
  828.8 36.6 %reduce-scatter.23.cloned.1.call-done = bf16[128,1024]{1,0:T(8,128)(2,1)} async-done(((bf16[1024,1024]{1,0:T(8,128)(2,1)}), bf16[128,1024]{1,0:T(8,128)(2,1)}) %reduce-scatter.23.cloned.1.call-update) | async-done | bytes 262160 | tf_op jit(solution)/shard_map/reduce_scatter | solution.py:503
  865.4 70.6 %reduce-scatter.13.cloned.1.call-done = bf16[128,3072]{1,0:T(8,128)(2,1)} async-done(((bf16[1024,3072]{1,0:T(8,128)(2,1)}), bf16[128,3072]{1,0:T(8,128)(2,1)}) %reduce-scatter.13.cloned.1.call-update) | async-done | bytes 786448 | tf_op jit(solution)/shard_map/reduce_scatter | solution.py:503
  936.0 90.7 %reduce-scatter.17.cloned.1.call-done = bf16[128,4096]{1,0:T(8,128)(2,1)} async-done(((bf16[1024,4096]{1,0:T(8,128)(2,1)}), bf16[128,4096]{1,0:T(8,128)(2,1)}) %reduce-scatter.17.cloned.1.call-update) | async-done | bytes 1048592 | tf_op jit(solution)/shard_map/reduce_scatter | solution.py:503
  1026.8 24.2 %fusion = f32[4,512,1024]{2,1,0:T(8,128)} fusion(bf16[4,4096,512]{2,1,0:T(8,128)(2,1)} %get-tuple-element.25, bf16[4096,1152]{1,0:T(8,128)(2,1)} %all-gather.24.cloned.1.call-done.sent_ref), kind=kOutput, calls=%fused_computation.1 | convolution fusion | flops 17179869184 | bytes 33554432 | tf_op jit(solution)/shard_map/hkl,kd->hld/dot_general | solution.py:442
  1051.0 1.2 fusion.15
  1052.2 3.0 fusion.28
  1055.2 38.0 %psum.49 = f32[2,1024]{1,0:T(2,128)S(1)} all-reduce(f32[2,1024]{1,0:T(2,128)S(1)} %pad_maximum_fusion.2), channel_id=1, replica_groups=mesh['grp'=4,'mem'=8] {'grp','mem'}, use_global_device_ids=true, to_apply=%region_14.15 | all-reduce | flops 2048 | bytes 16384 | tf_op jit(solution)/shard_map/psum | solution.py:509
  1093.7 2.2 fusion.26
  1096.0 17.0 %all-reduce.3.cloned.1.call-done = (bf16[128,3072]{1,0:T(8,128)(2,1)}, bf16[128,1024]{1,0:T(8,128)(2,1)}, bf16[128,4096]{1,0:T(8,128)(2,1)}, bf16[256,512]{1,0:T...) async-done(((bf16[128,3072]{1,0:T(8,128)(2,1)}, bf16[128,1024]{1,0:T(8,128)(2,1)}, bf16[128,4096]{1,0:T(8,128)(2,1)}, bf16[256,512]{1,0:T(8,128)(2,1)}, ...) | async-done | bytes 2883600 | tf_op jit(solution)/shard_map/psum | solution.py:508
  1113.0 2.8 convert_element_type.156
  1115.9 1.3 convert_element_type.152
  1118.0 0.9 convert_element_type.159
  (136 shorter events, 14.9 us)
Async XLA Ops:
  7.2 4.8 copy-start.31
  7.2 4.8 copy-start.30
  7.2 18.3 %copy-start.26 = (s32[1024]{0:T(1024)S(1)}, s32[1024]{0:T(1024)}, u32[]{:S(2)}) copy-start(s32[1024]{0:T(1024)} %param.14) | copy-start | bytes 12292
  7.2 19.3 %copy-start.25 = (s32[128,4,32]{0,2,1:T(8,128)S(1)}, s32[128,4,32]{0,2,1:T(8,128)}, u32[]{:S(2)}) copy-start(s32[128,4,32]{0,2,1:T(8,128)} %param.15) | copy-start | bytes 196612
  7.2 34.3 %all-gather.10.cloned.1.call-start = ((), (), s32[]{:S(2)}) async-start(), calls=%async_computation.9 | async-start | bytes 2359296 | tf_op jit(solution)/shard_map/all_gather | solution.py:396
  8.0 99.5 %all-gather.12.cloned.1.call-start = ((), (), s32[]{:S(2)}) async-start(), calls=%async_computation.10 | async-start | bytes 7077888 | tf_op jit(solution)/shard_map/all_gather | solution.py:396
  8.7 128.1 %all-gather.14.cloned.1.call-start = ((), (), s32[]{:S(2)}) async-start(), calls=%async_computation.11 | async-start | bytes 2359296 | tf_op jit(solution)/shard_map/all_gather | solution.py:396
  9.4 157.5 %all-gather.18.cloned.1.call-start = ((), (), s32[]{:S(2)}) async-start(), calls=%async_computation.13 | async-start | bytes 2359296 | tf_op jit(solution)/shard_map/all_gather | solution.py:396
  10.0 187.0 %all-gather.16.cloned.1.call-start = ((), (), s32[]{:S(2)}) async-start(), calls=%async_computation.12 | async-start | bytes 2359296 | tf_op jit(solution)/shard_map/all_gather | solution.py:396
  10.6 269.4 %all-gather.20.cloned.1.call-start = ((), (), s32[]{:S(2)}) async-start(), calls=%async_computation.14 | async-start | bytes 9437184 | tf_op jit(solution)/shard_map/all_gather | solution.py:396
  11.2 298.1 %all-gather.22.cloned.1.call-start = ((), (), s32[]{:S(2)}) async-start(), calls=%async_computation.15 | async-start | bytes 2359296 | tf_op jit(solution)/shard_map/all_gather | solution.py:396
  11.9 388.6 %all-gather.24.cloned.1.call-start = ((), (), s32[]{:S(2)}) async-start(), calls=%async_computation.16 | async-start | bytes 9732096 | tf_op jit(solution)/shard_map/all_gather | solution.py:396
  41.5 65.9 %copy-start.10 = (bf16[1024,1024]{1,0:T(8,128)(2,1)S(1)}, bf16[1024,1024]{1,0:T(8,128)(2,1)}, u32[]{:S(2)}) copy-start(bf16[1024,1024]{1,0:T(8,128)(2,1)} %all-gather.10.cloned.1.call-done) | copy-start | bytes 6291460
  119.0 17.8 %copy-start.1 = (bf16[128,1024]{1,0:T(8,128)(2,1)S(1)}, bf16[128,1024]{1,0:T(8,128)(2,1)}, u32[]{:S(2)}) copy-start(bf16[128,1024]{1,0:T(8,128)(2,1)} %param.13) | copy-start | bytes 786436
  139.1 57.9 %copy-start.14 = (bf16[128,1024]{1,0:T(8,128)(2,1)S(1)}, bf16[128,1024]{1,0:T(8,128)(2,1)}, u32[]{:S(2)}) copy-start(bf16[128,1024]{1,0:T(8,128)(2,1)} %param.25) | copy-start | bytes 786436
  168.9 31.3 %copy-start.11 = (f32[128,1024]{1,0:T(8,128)}, f32[128,1024]{1,0:T(8,128)S(1)}, u32[]{:S(2)}) copy-start(f32[128,1024]{1,0:T(8,128)S(1)} %fusion.46) | copy-start | bytes 1572868
  317.2 297.6 %reduce-scatter.9.cloned.1.call-start = ((), (), s32[]{:S(2)}) async-start(), calls=%async_computation.17 | async-start | bytes 11796480 | tf_op jit(solution)/shard_map/reduce_scatter | solution.py:440
  400.6 2.2 copy-start
  521.0 132.2 %reduce-scatter.11.cloned.1.call-start = ((), (), s32[]{:S(2)}) async-start(), calls=%async_computation.18 | async-start | bytes 2654208 | tf_op jit(solution)/shard_map/reduce_scatter | solution.py:441
  614.8 103.5 %all-gather.26.cloned.1.call-start = ((), (), s32[]{:S(2)}) async-start(), calls=%async_computation.19 | async-start | bytes 2654208 | tf_op jit(solution)/shard_map/all_gather | solution.py:396
  665.0 0.8 copy-start.5
  665.8 4.7 copy-start.18
  672.0 6.5 copy-start.9
  672.0 6.5 copy-start.3
  678.5 1.8 copy-start.15
  678.5 2.0 copy-start.2
  678.5 2.0 copy-start.8
  679.5 0.8 copy-start.6
  679.5 2.6 copy-start.27
  687.2 68.3 %reduce-scatter.21.cloned.1.call-start = ((), (), s32[]{:S(2)}) async-start(), calls=%async_computation.24 | async-start | bytes 2359296 | tf_op jit(solution)/shard_map/reduce_scatter | solution.py:503
  690.2 101.9 %reduce-scatter.15.cloned.1.call-start = ((), (), s32[]{:S(2)}) async-start(), calls=%async_computation.21 | async-start | bytes 2359296 | tf_op jit(solution)/shard_map/reduce_scatter | solution.py:503
  693.4 3.6 copy-start.16
  693.4 135.4 %reduce-scatter.19.cloned.1.call-start = ((), (), s32[]{:S(2)}) async-start(), calls=%async_computation.23 | async-start | bytes 2359296 | tf_op jit(solution)/shard_map/reduce_scatter | solution.py:503
  696.5 1.0 copy-start.12
  696.5 1.1 copy-start.19
  696.6 168.9 %reduce-scatter.23.cloned.1.call-start = ((), (), s32[]{:S(2)}) async-start(), calls=%async_computation.25 | async-start | bytes 2359296 | tf_op jit(solution)/shard_map/reduce_scatter | solution.py:503
  699.7 236.3 %reduce-scatter.13.cloned.1.call-start = ((), (), s32[]{:S(2)}) async-start(), calls=%async_computation.20 | async-start | bytes 7077888 | tf_op jit(solution)/shard_map/reduce_scatter | solution.py:503
  746.9 279.8 %reduce-scatter.17.cloned.1.call-start = ((), (), s32[]{:S(2)}) async-start(), calls=%async_computation.22 | async-start | bytes 9437184 | tf_op jit(solution)/shard_map/reduce_scatter | solution.py:503
  752.7 299.4 %slice-start = ((s8[6291456]{0:T(1024)(128)(4,1)}), s8[2097152]{0:T(1024)(128)(4,1)S(1)}, s32[]{:S(2)}) async-start(s8[6291456]{0:T(1024)(128)(4,1)} %bitcast.77), calls=%async_computation.27 | async-start | bytes 4194304
  752.8 360.2 %all-reduce.3.cloned.1.call-start = ((), (), s32[]{:S(2)}) async-start(), calls=%async_computation.26 | async-start | bytes 5767168 | tf_op jit(solution)/shard_map/psum | solution.py:508
  1026.7 24.2 %copy-start.13 = (f32[128,1024]{1,0:T(8,128)S(1)}, f32[128,1024]{1,0:T(8,128)}, u32[]{:S(2)}) copy-start(f32[128,1024]{1,0:T(8,128)} %copy-done.11) | copy-start | bytes 1572868
  1026.7 24.2 %copy-start.20 = (bf16[128,1152]{1,0:T(8,128)(2,1)S(1)}, bf16[128,1152]{1,0:T(8,128)(2,1)}, u32[]{:S(2)}) copy-start(bf16[128,1152]{1,0:T(8,128)(2,1)} %reduce-scatter.11.cloned.1.call-done) | copy-start | bytes 884740
  1026.7 24.2 %copy-start.29 = (bf16[1024,1024]{1,0:T(8,128)(2,1)S(1)}, bf16[1024,1024]{1,0:T(8,128)(2,1)}, u32[]{:S(2)}) copy-start(bf16[1024,1024]{1,0:T(8,128)(2,1)} %all-gather.16.cloned.1.call-done) | copy-start | bytes 6291460
  1026.8 25.4 %slice-start.1 = ((s8[6291456]{0:T(1024)(128)(4,1)}), s8[4194304]{0:T(1024)(128)(4,1)S(1)}, s32[]{:S(2)}) async-start(s8[6291456]{0:T(1024)(128)(4,1)} %bitcast.77), calls=%async_computation.28 | async-start | bytes 8388608
  1051.0 1.2 copy-start.4
  1052.2 41.6 %copy-start.7 = (f32[128,1024]{1,0:T(8,128)S(1)}, f32[128,1024]{1,0:T(8,128)}, u32[]{:S(2)}) copy-start(f32[128,1024]{1,0:T(8,128)} %copy-done.6) | copy-start | bytes 1572868
  1052.2 41.6 %copy-start.28 = (f32[128]{0:T(128)S(1)}, f32[128]{0:T(128)}, u32[]{:S(2)}) copy-start(f32[128]{0:T(128)} %copy-done.27) | copy-start | bytes 1540
  1113.0 2.9 copy-start.17
  1113.0 4.2 copy-start.24
  1115.8 2.2 copy-start.23
  1115.8 3.0 copy-start.22
  1115.8 3.9 copy-start.21
Sparse Core Ops, SparseCore 0:
  9.7 31.7 all-gather.9
  43.1 64.2 all-gather.11
  109.0 27.7 all-gather.13
  138.3 28.5 all-gather.17
  168.3 28.5 all-gather.15
  198.4 81.5 all-gather.19
  281.6 27.6 all-gather.21
  317.4 83.1 all-gather.23
  521.1 93.6 reduce-scatter.8
  617.0 36.2 reduce-scatter.10
  687.3 30.9 all-gather.25
  720.4 35.0 reduce-scatter.20
  757.8 34.2 reduce-scatter.14
  794.3 34.4 reduce-scatter.18
  830.9 34.4 reduce-scatter.22
  867.6 68.3 reduce-scatter.12
  938.7 87.9 reduce-scatter.16
  1030.3 82.6 all-reduce.2

commit v2 on v1

--- a/solution.py
+++ b/solution.py
@@ -307,7 +307,7 @@
     ).astype(BF)
 
 
-def owner_call(keys, sent, values, flat_bits):
+def owner_call(keys, sent, values, flat_bits, order):
     owners, slots = keys.shape
     rows = sent.shape[0] // owners
     local_rows, width = values.shape
@@ -322,7 +322,7 @@
             pl.BlockSpec((local_rows, width), lambda s: (0, 0)),
         ],
         out_specs=[
-            pl.BlockSpec((rows, width + LANES), lambda s: (s, 0)),
+            pl.BlockSpec((rows, width + LANES), lambda s: (order(s), 0)),
             pl.BlockSpec((his, rows, low_rows), lambda s: (0, s, 0)),
         ],
         out_shape=[
@@ -354,6 +354,248 @@
     spare = ((spare_owner * local_rows + local_rows - 1) << (flat_bits + 1)) + (1 << flat_bits)
     keys = lax.sort(jnp.concatenate([real, spare]))
     return keys.reshape(owners, capacity)
+
+
+MESH = pl.DeviceIdType.MESH
+
+
+def places():
+    g, m = lax.axis_index("grp"), lax.axis_index("mem")
+    across = g + 1 - 2 * (g % 2)
+    along = (g + 2) % 4
+    sibling = m + 1 - 2 * (m % 2)
+    return g, m, across, along, sibling
+
+
+def enter(peers):
+    barrier = pltpu.get_barrier_semaphore()
+    for peer in peers:
+        pl.semaphore_signal(barrier, inc=1, device_id=peer, device_id_type=MESH)
+    pl.semaphore_wait(barrier, len(peers))
+
+
+def push(src, dst, send, recv, peer):
+    copy = pltpu.make_async_remote_copy(
+        src_ref=src, dst_ref=dst, send_sem=send, recv_sem=recv, device_id=peer, device_id_type=MESH
+    )
+    copy.start()
+    return copy
+
+
+def reduce_planes(held, ready, x1, y1, x2, y2, zin, send, recv):
+    g, m, across, along, _ = places()
+    diagonal = 3 - g
+    half = held.shape[2] // 2
+    low, high = pl.ds(0, half), pl.ds(half, half)
+    to_x, to_y = (across, m), (along, m)
+    sent, ones, twos, threes = [], [], [], []
+    for k in range(4):
+        ready(k)
+        a = push(held.at[k, diagonal, low], x1.at[k], send.at[0, k], recv.at[0, k], to_x)
+        b = push(held.at[k, diagonal, high], y1.at[k], send.at[1, k], recv.at[1, k], to_y)
+        ones.append((a, b))
+    for k in range(4):
+        a, b = ones[k]
+        a.wait_recv()
+        b.wait_recv()
+        held[k, along, low] = held[k, along, low] + x1[k]
+        held[k, across, high] = held[k, across, high] + y1[k]
+        a = push(held.at[k, across], x2.at[k], send.at[2, k], recv.at[2, k], to_x)
+        b = push(held.at[k, along], y2.at[k], send.at[3, k], recv.at[3, k], to_y)
+        twos.append((a, b))
+    total = None
+    for k in range(4):
+        a, b = twos[k]
+        a.wait_recv()
+        b.wait_recv()
+        total = held[k, g].astype(F32) + x2[k].astype(F32) + y2[k].astype(F32)
+        if k < 3:
+            held[k, g] = total.astype(BF)
+            peer = (g, (m + 2 * (3 - k)) % 8)
+            threes.append(push(held.at[k, g], zin.at[k], send.at[4, k], recv.at[4, k], peer))
+    for k in range(3):
+        threes[k].wait_recv()
+        total = total + zin[k].astype(F32)
+    for pair in ones + twos:
+        sent.extend(pair)
+    for copy in sent + threes:
+        copy.wait_send()
+    return total
+
+
+def plane_peers():
+    g, m, across, along, sibling = places()
+    return [(across, m), (along, m), (g, sibling)] + [(g, (m + 2 * d) % 8) for d in (1, 2, 3)]
+
+
+def return_kernel(part_ref, out_ref, held, sib, x1, y1, x2, y2, zin, local_sem, send, recv):
+    g, m, _, _, sibling = places()
+    core, z = m % 2, m // 2
+    enter(plane_peers())
+    locals_, remotes = [], []
+    for k in range(4):
+        level = (z + 3 - k) % 4
+        copy = pltpu.make_async_copy(part_ref.at[core, level], held.at[k], local_sem.at[k])
+        copy.start()
+        locals_.append(copy)
+        remotes.append(
+            push(
+                part_ref.at[1 - core, level], sib.at[k], send.at[5, k], recv.at[5, k], (g, sibling)
+            )
+        )
+
+    def ready(k):
+        locals_[k].wait()
+        remotes[k].wait_recv()
+        for i in range(4):
+            held[k, i] = held[k, i] + sib[k, i]
+
+    out_ref[...] = reduce_planes(held, ready, x1, y1, x2, y2, zin, send, recv)
+    for copy in remotes:
+        copy.wait_send()
+
+
+def plane_scratch(rows, columns):
+    return [
+        pltpu.VMEM((4, rows // 2, columns), BF),
+        pltpu.VMEM((4, rows // 2, columns), BF),
+        pltpu.VMEM((4, rows, columns), BF),
+        pltpu.VMEM((4, rows, columns), BF),
+        pltpu.VMEM((3, rows, columns), BF),
+    ]
+
+
+def return_rows(part, rows):
+    columns = part.shape[1]
+    return pl.pallas_call(
+        return_kernel,
+        in_specs=[pl.BlockSpec(memory_space=pl.ANY)],
+        out_specs=pl.BlockSpec(memory_space=pltpu.VMEM),
+        out_shape=jax.ShapeDtypeStruct((rows, columns), F32),
+        scratch_shapes=[
+            pltpu.VMEM((4, 4, rows, columns), BF),
+            pltpu.VMEM((4, 4, rows, columns), BF),
+            *plane_scratch(rows, columns),
+            pltpu.SemaphoreType.DMA((4,)),
+            pltpu.SemaphoreType.DMA((6, 4)),
+            pltpu.SemaphoreType.DMA((6, 4)),
+        ],
+        compiler_params=pltpu.CompilerParams(
+            collective_id=1, has_side_effects=True, vmem_limit_bytes=48 * 1024 * 1024
+        ),
+        name="return_rows",
+    )(part.reshape(2, 4, 4, rows, columns))
+
+
+WIDTH = HEADS * HDIM
+KEYS = MHEADS * 2 * NK
+QUERIES = MHEADS * 2 * HALF
+F_MIXED, F_SECOND, F_ATTENDED, F_FIRST, F_COT, F_GATE, F_RESID = (i * WIDTH for i in range(7))
+F_HALF = 7 * WIDTH
+F_QKV = F_HALF + KEYS
+F_QUERY = F_QKV + 3 * WIDTH
+F_ALL = F_QUERY + QUERIES
+G_OUT, G_GATE, G_PROJ, G_HALF = 0, WIDTH, 2 * WIDTH, 3 * WIDTH
+G_QKV = G_HALF + KEYS
+G_KEYS = G_QKV + 3 * WIDTH
+G_GAIN = G_KEYS + 2 * HALF
+G_ALL = G_GAIN + LANES
+PRODUCTS = (
+    (F_MIXED, F_COT, WIDTH, G_OUT),
+    (F_SECOND, F_GATE, WIDTH, G_GATE),
+    (F_ATTENDED, F_RESID, WIDTH, G_PROJ),
+    (F_SECOND, F_HALF, KEYS, G_HALF),
+    (F_FIRST, F_QKV, 3 * WIDTH, G_QKV),
+)
+
+
+def grads_kernel(
+    fact_ref, gain_ref, out_ref, fact, gains, held, x1, y1, x2, y2, zin, quarter, local_sem, send, recv
+):
+    g, m, across, along, sibling = places()
+    core, z = m % 2, m // 2
+    rows = fact_ref.shape[0]
+    enter(plane_peers())
+    copies = []
+    for i, (src, dst, count) in enumerate(((fact_ref, fact, rows), (gain_ref, gains, 16))):
+        near = pltpu.make_async_copy(src, dst.at[pl.ds(0, count)], local_sem.at[i])
+        near.start()
+        far = push(
+            src, dst.at[pl.ds(count, count)], send.at[5, i], recv.at[5, i], (g, sibling)
+        )
+        copies.append((near, far))
+    for near, far in copies:
+        near.wait()
+        far.wait_recv()
+    row = iota((32, LANES), 0) % 16
+    column = iota((32, LANES), 1)
+    select = ((row < 4) & (row // 2 == column)).astype(F32).astype(BF)
+    chunk = WIDTH
+
+    def ready(k):
+        block = (z + 3 - k) % 4 * 2 + core
+
+        def store(value, at):
+            for i in range(4):
+                held[k, i, :, at : at + value.shape[1]] = value[i * 32 : (i + 1) * 32].astype(BF)
+
+        for left, right, count, at in PRODUCTS:
+            lhs = fact[:, pl.ds(pl.multiple_of(left + block * LANES, LANES), LANES)]
+            for j in range(0, count, chunk):
+                store(dot(lhs, fact[:, right + j : right + j + chunk], TN), at + j)
+        lhs = fact[:, pl.ds(pl.multiple_of(F_HALF + block * NK, LANES), NK)]
+        rhs = fact[:, pl.ds(pl.multiple_of(F_QUERY + block * HALF, LANES), HALF)]
+        value = dot(lhs, rhs, TN)
+        for i in range(4):
+            for h in range(2):
+                first = i * 64 + h * 32
+                held[k, i, :, G_KEYS + h * HALF : G_KEYS + (h + 1) * HALF] = value[
+                    first : first + 32
+                ].astype(BF)
+        lhs = gains[:, pl.ds(pl.multiple_of(block * LANES, LANES), LANES)]
+        store(dot(lhs, select, TN), G_GAIN)
+
+    total = reduce_planes(held, ready, x1, y1, x2, y2, zin, send, recv)
+    quarter[g] = total.astype(BF)
+    to_x, to_y = (across, m), (along, m)
+    low, high = pl.ds(0, 16), pl.ds(16, 16)
+    a = push(quarter.at[g], quarter.at[g], send.at[6, 0], recv.at[6, 0], to_x)
+    b = push(quarter.at[g], quarter.at[g], send.at[6, 1], recv.at[6, 1], to_y)
+    a.wait_recv()
+    c = push(quarter.at[across, low], quarter.at[across, low], send.at[6, 2], recv.at[6, 2], to_y)
+    b.wait_recv()
+    d = push(quarter.at[along, high], quarter.at[along, high], send.at[6, 3], recv.at[6, 3], to_x)
+    c.wait_recv()
+    d.wait_recv()
+    for copy in (a, b, c, d):
+        copy.wait_send()
+    for _, far in copies:
+        far.wait_send()
+    out_ref[...] = quarter[...]
+
+
+def reduce_grads(factors, gains):
+    rows = factors.shape[0]
+    return pl.pallas_call(
+        grads_kernel,
+        in_specs=[pl.BlockSpec(memory_space=pl.ANY)] * 2,
+        out_specs=pl.BlockSpec(memory_space=pltpu.VMEM),
+        out_shape=jax.ShapeDtypeStruct((4, 32, G_ALL), BF),
+        scratch_shapes=[
+            pltpu.VMEM((2 * rows, F_ALL), BF),
+            pltpu.VMEM((32, WIDTH), BF),
+            pltpu.VMEM((4, 4, 32, G_ALL), BF),
+            *plane_scratch(32, G_ALL),
+            pltpu.VMEM((4, 32, G_ALL), BF),
+            pltpu.SemaphoreType.DMA((2,)),
+            pltpu.SemaphoreType.DMA((7, 4)),
+            pltpu.SemaphoreType.DMA((7, 4)),
+        ],
+        compiler_params=pltpu.CompilerParams(
+            collective_id=2, has_side_effects=True, vmem_limit_bytes=56 * 1024 * 1024
+        ),
+        name="reduce_grads",
+    )(factors, gains).reshape(4 * 32, G_ALL)
 
 
 def rms_scale(values):
@@ -389,6 +631,7 @@
     flat_bits = (total_picks - 1).bit_length()
     capacity = 2 * total_picks // owners
     group_len = segment_ids.shape[0]
+    linked = (lax.axis_size("grp"), lax.axis_size("mem"), rows) == (4, 8, LANES)
     position = lax.axis_index("mem").astype(jnp.int32)
     pos = position.reshape(1)
 
@@ -436,9 +679,15 @@
     pick_weights, weights_low = pick_fwd(half_scores, flat_picks)
 
     sent = gather(jnp.concatenate([memory_grad, weights_low], axis=1), ALL)
-    part, spread = owner_call(arrived, sent, memory_values, flat_bits)
-    back = lax.psum_scatter(part, "grp", scatter_dimension=0, tiled=True)
-    back = lax.psum_scatter(back, "mem", scatter_dimension=0, tiled=True)
+    if linked:
+        part, spread = owner_call(
+            arrived, sent, memory_values, flat_bits, lambda s: s % 2 * 16 + s // 2 % 4 * 4 + s // 8
+        )
+        back = return_rows(part, rows)
+    else:
+        part, spread = owner_call(arrived, sent, memory_values, flat_bits, lambda s: s)
+        back = lax.psum_scatter(part, "grp", scatter_dimension=0, tiled=True)
+        back = lax.psum_scatter(back, "mem", scatter_dimension=0, tiled=True)
     values_grad = jnp.einsum(
         "hkl,kd->hld", spread, sent[:, :width], preferred_element_type=F32
     ).reshape(local_rows, width)
@@ -447,9 +696,7 @@
     weight_grad = back[:, width:].astype(F32)
     mixed = (memory_out * gate_act).astype(BF)
     block_out = (residual + dot(mixed, output_full)).astype(BF)
-    out_w_grad = dot(mixed, out_cotangent, TN)
     gate_grad = (mixed_grad * memory_out * (sig * (1.0 + gate_pre * (1.0 - sig)))).astype(BF)
-    gate_w_grad = dot(second, gate_grad, TN)
     half_grad = pick_bwd(pick_weights, weight_grad, flat_picks)
     half_cube = half_grad.reshape(rows, MHEADS * 2, NK)
     query_grad = (
@@ -457,18 +704,10 @@
         .astype(BF)
         .reshape(rows, MHEADS * 2 * HALF)
     )
-    keys_grad = jnp.einsum(
-        "tcn,tcf->cnf",
-        half_cube,
-        mem_query.reshape(rows, MHEADS * 2, HALF),
-        preferred_element_type=F32,
-    ).reshape(MHEADS * 2 * NK, HALF)
-    query_w_grad = dot(second, query_grad, TN)
     second_grad = dot(gate_grad, gate_full, NT) + dot(query_grad, query_full, NT)
     resid_from_norm, gain_two_grad = rms_back(residual, scale_two, gain_two, second_grad)
     resid_grad = out_cotangent.astype(F32) + resid_from_norm
     resid_low = resid_grad.astype(BF)
-    proj_grad = dot(attended, resid_low, TN)
     attn_grad = dot(resid_low, proj_full, NT).astype(BF)
     delta = jnp.sum(
         (attn_grad.astype(F32) * attn_sum).reshape(rows, HEADS, HDIM), axis=-1
@@ -494,25 +733,75 @@
     qkv_rows = attn_bwd(pos, qkv_all, attn_grad_all, stats_all, seg_row, seg_col, rows)
     scale_one = rms_scale(inputs)
     first_low = (inputs * scale_one * gain_one).astype(BF)
-    qkv_w_grad = dot(first_low, qkv_rows, TN)
     first_grad = dot(qkv_rows, qkv_full, NT)
     input_from_norm, gain_one_grad = rms_back(inputs, scale_one, gain_one, first_grad)
     tokens_grad = resid_grad + input_from_norm
 
-    def scatter(x):
-        return lax.psum_scatter(x.astype(BF), "mem", scatter_dimension=0, tiled=True)
-
-    shares = [
-        scatter(x) for x in (out_w_grad, gate_w_grad, keys_grad, query_w_grad, proj_grad, qkv_w_grad)
-    ]
-    shares = lax.psum(tuple(shares), "grp")
-    gain_sums = lax.psum(jnp.stack([gain_one_grad, gain_two_grad]), ALL)
-    gain_sums = lax.dynamic_slice_in_dim(
-        gain_sums, position * attn_gain.shape[0], attn_gain.shape[0], axis=1
-    )
-    out_share, gate_share, keys_share, query_share, proj_share, qkv_share = (
-        x.astype(F32) for x in shares
-    )
+    if linked:
+        factors = jnp.concatenate(
+            [
+                mixed,
+                second,
+                attended,
+                first_low,
+                out_cotangent,
+                gate_grad,
+                resid_low,
+                half_grad,
+                qkv_rows,
+                mem_query,
+            ],
+            axis=1,
+        )
+        sums = jnp.stack([gain_one_grad, gain_two_grad])
+        sums_high = lax.reduce_precision(sums, 8, 7)
+        gain_rows = jnp.stack([sums_high, sums - sums_high], axis=1).reshape(4, width)
+        gain_rows = jnp.concatenate([gain_rows.astype(BF), jnp.zeros((12, width), BF)])
+        reduced = reduce_grads(factors, gain_rows).astype(F32)
+        out_share = reduced[:, G_OUT : G_OUT + width]
+        gate_share = reduced[:, G_GATE : G_GATE + width]
+        proj_share = reduced[:, G_PROJ : G_PROJ + width]
+        qkv_share = reduced[:, G_QKV : G_QKV + 3 * width]
+        keys_share = (
+            reduced[:, G_KEYS : G_KEYS + 2 * HALF]
+            .reshape(4, 32, 2, HALF)
+            .transpose(0, 2, 1, 3)
+            .reshape(half_keys.shape)
+        )
+        query_share = jnp.einsum(
+            "rcn,cnf->rcf",
+            reduced[:, G_HALF : G_HALF + KEYS].astype(BF).reshape(rows, MHEADS * 2, NK),
+            key_table,
+            preferred_element_type=F32,
+        ).reshape(rows, QUERIES)
+        gain_sums = reduced[:, G_GAIN : G_GAIN + 2].T
+    else:
+        keys_grad = jnp.einsum(
+            "tcn,tcf->cnf",
+            half_cube,
+            mem_query.reshape(rows, MHEADS * 2, HALF),
+            preferred_element_type=F32,
+        ).reshape(KEYS, HALF)
+        partials = (
+            dot(mixed, out_cotangent, TN),
+            dot(second, gate_grad, TN),
+            keys_grad,
+            dot(second, query_grad, TN),
+            dot(attended, resid_low, TN),
+            dot(first_low, qkv_rows, TN),
+        )
+        shares = [
+            lax.psum_scatter(x.astype(BF), "mem", scatter_dimension=0, tiled=True)
+            for x in partials
+        ]
+        shares = lax.psum(tuple(shares), "grp")
+        gain_sums = lax.psum(jnp.stack([gain_one_grad, gain_two_grad]), ALL)
+        gain_sums = lax.dynamic_slice_in_dim(
+            gain_sums, position * attn_gain.shape[0], attn_gain.shape[0], axis=1
+        )
+        out_share, gate_share, keys_share, query_share, proj_share, qkv_share = (
+            x.astype(F32) for x in shares
+        )
     return (
         block_out,
         tokens_grad,

time: 1130 us -> 834 us (0.74)
  waiting for transfers between devices: 750 us -> 315 us
  Pallas kernels: 155 us -> 339 us
  blocking collectives: 63.7 us -> 13.4 us
  local copies, waits for them, and re-layouts: 14.2 us -> 31.9 us
  matrix products: 95.3 us -> 79.5 us
    reduce_scatter x8 -> x0, waiting for transfers between devices: 406 us -> none  [the longest x6 274 us: scatter(): lax.psum_scatter(x.astype(BF), 'mem', scatter_dimension=0, tiled=True)]
    pallas_call x0 -> x2, Pallas kernels: none -> 182 us  [the longest x1 128 us: reduce_grads(): pl.pallas_call(grads_kernel, in_specs=[pl.BlockSpec(memory_space=pl.ANY)]...]
    psum x1 -> x0, blocking collectives: 38 us -> none  [per_device(): gain_sums = lax.psum(jnp.stack([gain_one_grad, gain_two_grad]), ALL)]
    all_gather x9, waiting for transfers between devices: 322 us -> 302 us  [gather(): return lax.all_gather(x, axes, axis=0, tiled=True)]
    psum x1 -> x0, waiting for transfers between devices: 17 us -> none  [per_device(): shares = lax.psum(tuple(shares), 'grp')]
    dot_general x16 -> x11, matrix products: 62.5 us -> 48.4 us  [dot(): lax.dot_general(left, right, (dims, ((), ())), preferred_element_type=F32)]
    all_to_all x1 -> x0, blocking collectives: 12.3 us -> none  [per_device(): lax.all_to_all(requests, ALL, split_axis=0, concat_axis=0, tiled=True)]
  transfers between devices with their start and end apart: 18 -> 10, of which waited for: 18 -> 10; matrix products, arithmetic and copies ran while one was open for 9% -> 9% of each run, Pallas kernels for 2% -> 1%
where the time goes in v2:
time: 834 us; the launch traced here: 829 us
  Pallas kernels  339 us (41%)
  waiting for transfers between devices  315 us (38%)
  matrix products  79.5 us (10%)
  local copies, waits for them, and re-layouts  31.9 us (4%)
  other arithmetic  31.1 us (4%)
  between operations  14.7 us (2%)
  blocking collectives  13.4 us (2%)
    all_gather x9, waiting for transfers between devices, gather(): return lax.all_gather(x, axes, axis=0, tiled=True)  302 us
    pallas_call x1, Pallas kernels, reduce_grads(): pl.pallas_call(grads_kernel, in_specs=[pl.BlockSpec(memory_space=pl.ANY)]...  128 us
    pallas_call x1, Pallas kernels, owner_call(): pl.pallas_call(functools.partial(owner_kernel, his, flat_bits, local_rows...  119 us
    pallas_call x1, Pallas kernels, return_rows(): pl.pallas_call(return_kernel, in_specs=[pl.BlockSpec(memory_space=pl.ANY)...  54.4 us
    dot_general x11, matrix products, dot(): lax.dot_general(left, right, (dims, ((), ())), preferred_element_type=F32)  48.4 us
    dot_general x1, matrix products, per_device(): jnp.einsum('hkl,kd->hld', spread, sent[:, :width], preferred_element_type...  24.4 us
  transfers between devices with their start and end apart: 10, of which 10 were waited for; matrix products, arithmetic and copies ran while one was open for 9% of the time, Pallas kernels for 1%

profile of v2, /device:TPU:0, one launch (start us, length us, event | category | flops | bytes accessed | tf_op | source)
XLA Modules:
  0.0 829.1 jit_solution(2071587784366164569)
XLA Ops:
  12.6 13.4 %all_gather.31 = bf16[2,1024]{1,0:T(2,128)(2,1)S(1)} all-gather(bf16[2,128]{1,0:T(2,128)(2,1)S(1)} %pad_maximum_fusion.4), channel_id=1, replica_groups=mesh['grp'=4,'mem'=8] {'mem'}, dimensions={1}, use_global_device_ids=true | all-gather | bytes 4608 | tf_op jit(solution)/shard_map/all_gather | solution.py:641
  26.0 1.7 copy.86.qseg_ref.segc_ref
  27.7 1.6 copy.91.picks_ref
  29.3 12.2 %all-gather.10.cloned.1.call-done = bf16[1024,1024]{1,0:T(8,128)(2,1)} async-done(((bf16[128,1024]{1,0:T(8,128)(2,1)}), bf16[1024,1024]{1,0:T(8,128)(2,1)}) %all-gather.10.cloned.1.call-update) | async-done | bytes 2097168 | tf_op jit(solution)/shard_map/all_gather | solution.py:639
  41.5 2.1 fusion.1
  43.5 63.8 %all-gather.12.cloned.1.call-done = bf16[1024,3072]{1,0:T(8,128)(2,1)} async-done(((bf16[128,3072]{1,0:T(8,128)(2,1)}), bf16[1024,3072]{1,0:T(8,128)(2,1)}) %all-gather.12.cloned.1.call-update) | async-done | bytes 6291472 | tf_op jit(solution)/shard_map/all_gather | solution.py:639
  107.4 11.9 %convolution_convert_fusion.q_ref.k_ref.v_ref = bf16[1024,3072]{1,0:T(8,128)(2,1)} fusion(bf16[1024,3072]{1,0:T(8,128)(2,1)} %all-gather.12.cloned.1.call-done, bf16[1024,1024]{1,0:T(8,128)(2,1)} %all-gather.10.cloned.1.call-done, f32[1024]{0:T(1024)S(1)} %bitcast.91, f32[1024]{0:T(1024)S(1)} %add_rsqrt_fusion), kind=kOutput, calls=%fused_computation.2 | convolution fusion | flops 6449790976 | bytes 14688256 | tf_op jit(solution)/shard_map/dot_general | solution.py:25
  119.3 10.6 %attn_fwd.1 = (f32[128,1024]{1,0:T(8,128)}, f32[128,128]{1,0:T(8,128)}) custom-call(s32[1]{0:T(128)} %bitcast.pos_ref, bf16[1024,3072]{1,0:T(8,128)(2,1)} %convolution_convert_fusion.q_ref.k_ref.v_ref, bf16[1024,3072]{1,0:T(8,128)(2,1)} %convolution_convert_fusion.q_ref.k_ref.v_ref, bf16[1024,3072]{1,0:T(8,128)(2,1)} %convolution_convert_fusion.q_ref.k_ref.v_ref, ...), custom_call_target="tpu_custom_call" | custom-call | flops 335544320 | bytes 4194304 | tf_op jit(solution)/shard_map/attn_fwd/pallas_call | solution.py:76
  129.9 6.8 all-gather.14.cloned.1.call-done
  136.8 2.3 multiply_reduce_fusion.2
  139.1 27.8 %all-gather.18.cloned.1.call-done = bf16[1024,1024]{1,0:T(8,128)(2,1)} async-done(((bf16[128,1024]{1,0:T(8,128)(2,1)}), bf16[1024,1024]{1,0:T(8,128)(2,1)}) %all-gather.18.cloned.1.call-update) | async-done | bytes 2097168 | tf_op jit(solution)/shard_map/all_gather | solution.py:639
  166.9 2.1 fusion.41
  168.9 28.0 %all-gather.16.cloned.1.call-done = bf16[1024,1024]{1,0:T(8,128)(2,1)} async-done(((bf16[128,1024]{1,0:T(8,128)(2,1)}), bf16[1024,1024]{1,0:T(8,128)(2,1)}) %all-gather.16.cloned.1.call-update) | async-done | bytes 2097168 | tf_op jit(solution)/shard_map/all_gather | solution.py:639
  196.9 3.2 multiply_convert_fusion.2
  200.2 79.8 %all-gather.20.cloned.1.call-done = bf16[1024,4096]{1,0:T(8,128)(2,1)} async-done(((bf16[128,4096]{1,0:T(8,128)(2,1)}), bf16[1024,4096]{1,0:T(8,128)(2,1)}) %all-gather.20.cloned.1.call-update) | async-done | bytes 8388624 | tf_op jit(solution)/shard_map/all_gather | solution.py:639
  280.0 4.7 convolution_convert_fusion.1
  284.7 24.5 %all-gather.22.cloned.1.call-done = bf16[2048,512]{1,0:T(8,128)(2,1)} async-done(((bf16[256,512]{1,0:T(8,128)(2,1)}), bf16[2048,512]{1,0:T(8,128)(2,1)}) %all-gather.22.cloned.1.call-update) | async-done | bytes 2097168 | tf_op jit(solution)/shard_map/all_gather | solution.py:639
  309.2 2.4 convolution_bitcast_fusion.1
  311.6 1.1 copy.109
  312.7 3.0 pick_fwd.1
  315.7 1.5 pad_maximum_fusion
  318.6 11.4 %sort.14 = (s32[32768]{0:T(1024)}, s32[32768]{0:T(1024)}) sort(s32[32768]{0:T(1024)S(1)} %pad_add_fusion, s32[32768]{0:T(1024)S(1)} %iota.15), dimensions={0}, to_apply=%region_4.5 | sort | flops 491520 | bytes 524288 | tf_op jit(solution)/shard_map/sort | solution.py:355
  330.0 4.1 all-to-all-start
  334.3 8.0 all-to-all-done.keys_ref
  342.3 58.3 %all-gather.24.cloned.1.call-done.sent_ref = bf16[4096,1152]{1,0:T(8,128)(2,1)} async-done(((bf16[128,1152]{1,0:T(8,128)(2,1)}), bf16[4096,1152]{1,0:T(8,128)(2,1)}) %all-gather.24.cloned.1.call-update) | async-done | bytes 9437200 | tf_op jit(solution)/shard_map/all_gather | solution.py:639
  400.5 2.2 copy-done
  402.7 119.0 %owner.1 = (bf16[4096,1152]{1,0:T(8,128)(2,1)}, bf16[4,4096,512]{2,1,0:T(8,128)(2,1)}) custom-call(s32[32,1,1024]{2,1,0:T(1,128)S(1)} %all-to-all-done.keys_ref, bf16[4096,1152]{1,0:T(8,128)(2,1)} %all-gather.24.cloned.1.call-done.sent_ref, bf16[2048,1024]{1,0:T(8,128)(2,1)S(1)} %copy-done), custom_call_target="tpu_custom_call" | custom-call | flops 68719476736 | bytes 33554432 | tf_op jit(solution)/shard_map/owner/pallas_call | solution.py:316
  521.8 54.4 %return_rows.1 = f32[128,1152]{1,0:T(8,128)S(1)} custom-call(bf16[2,4,4,128,1152]{4,3,2,1,0:T(8,128)(2,1)} %bitcast.75), custom_call_target="tpu_custom_call" | custom-call | tf_op jit(solution)/shard_map/return_rows/pallas_call | solution.py:470
  576.2 1.0 constant_dynamic-update-slice_fusion.7
  577.8 0.8 constant_dynamic-update-slice_fusion.6
  579.3 0.9 fusion.29
  580.2 0.8 constant_dynamic-update-slice_fusion.5
  581.0 9.1 %pick_bwd.1 = bf16[128,2048]{1,0:T(8,128)(2,1)} custom-call(f32[128,128]{1,0:T(8,128)} %get-tuple-element.23.weight_ref, f32[128,128]{1,0:T(8,128)} %slice.58.grad_ref, s32[128,128]{1,0:T(8,128)} %copy.91.picks_ref), custom_call_target="tpu_custom_call" | custom-call | tf_op jit(solution)/shard_map/pick_bwd/pallas_call | solution.py:257
  590.1 2.5 fusion.12
  592.6 2.4 copy.94
  595.0 2.1 constant_dynamic-update-slice_fusion.4
  597.2 6.8 fusion.42
  604.0 1.0 multiply_reduce_fusion
  605.0 0.9 constant_dynamic-update-slice_fusion.3
  606.6 1.6 fusion.14
  608.2 2.0 copy.95
  610.3 1.1 bitcast_reduce_fusion
  611.4 0.9 fusion.31
  612.4 1.8 concatenate.38
  614.2 1.9 constant_dynamic-update-slice_fusion.2
  616.1 2.8 fusion.15
  618.9 24.4 %fusion = f32[4,512,1024]{2,1,0:T(8,128)} fusion(bf16[4,4096,512]{2,1,0:T(8,128)(2,1)} %get-tuple-element.25, bf16[4096,1152]{1,0:T(8,128)(2,1)} %all-gather.24.cloned.1.call-done.sent_ref), kind=kOutput, calls=%fused_computation.1 | convolution fusion | flops 17179869184 | bytes 33554432 | tf_op jit(solution)/shard_map/hkl,kd->hld/dot_general | solution.py:691
  643.3 1.3 all-gather.26.cloned.1.call-done
  644.5 5.9 fusion.9.da_ref
  650.4 2.1 convert_add_fusion.stat_ref
  652.5 15.3 %attn_bwd.1 = bf16[128,3072]{1,0:T(8,128)(2,1)} custom-call(s32[1]{0:T(128)} %bitcast.pos_ref, bf16[1024,3072]{1,0:T(8,128)(2,1)} %convolution_convert_fusion.q_ref.k_ref.v_ref, bf16[1024,3072]{1,0:T(8,128)(2,1)} %convolution_convert_fusion.q_ref.k_ref.v_ref, bf16[1024,3072]{1,0:T(8,128)(2,1)} %convolution_convert_fusion.q_ref.k_ref.v_ref, ...), custom_call_target="tpu_custom_call" | custom-call | flops 1174405120 | bytes 8388608 | tf_op jit(solution)/shard_map/attn_bwd/pallas_call | solution.py:162
  667.8 6.1 fusion.25
  674.6 2.1 constant_dynamic-update-slice_fusion.1
  676.7 2.3 constant_dynamic-update-slice_fusion.fact_ref
  679.0 127.9 %reduce_grads.1 = bf16[4,32,9344]{2,1,0:T(8,128)(2,1)} custom-call(bf16[128,16384]{1,0:T(8,128)(2,1)} %constant_dynamic-update-slice_fusion.fact_ref, bf16[16,1024]{1,0:T(8,128)(2,1)} %concatenate.40.gain_ref), custom_call_target="tpu_custom_call" | custom-call | tf_op jit(solution)/shard_map/reduce_grads/pallas_call | solution.py:579
  806.9 2.1 bitcast_convert_fusion
  809.0 1.3 slice.80
  810.4 1.8 fusion.39
  812.1 1.5 reshape.309
  813.6 0.9 copy.101
  814.5 1.1 slice.83
  815.8 1.8 convolution_bitcast_fusion
  817.7 1.9 copy.100
  819.6 1.8 copy.103
  (94 shorter events, 10.9 us)
Async XLA Ops:
  7.2 34.3 %all-gather.10.cloned.1.call-start = ((), (), s32[]{:S(2)}) async-start(), calls=%async_computation.1 | async-start | bytes 2359296 | tf_op jit(solution)/shard_map/all_gather | solution.py:639
  7.9 99.5 %all-gather.12.cloned.1.call-start = ((), (), s32[]{:S(2)}) async-start(), calls=%async_computation.2 | async-start | bytes 7077888 | tf_op jit(solution)/shard_map/all_gather | solution.py:639
  8.7 128.1 %all-gather.14.cloned.1.call-start = ((), (), s32[]{:S(2)}) async-start(), calls=%async_computation.3 | async-start | bytes 2359296 | tf_op jit(solution)/shard_map/all_gather | solution.py:639
  9.4 157.5 %all-gather.18.cloned.1.call-start = ((), (), s32[]{:S(2)}) async-start(), calls=%async_computation.5 | async-start | bytes 2359296 | tf_op jit(solution)/shard_map/all_gather | solution.py:639
  10.0 187.0 %all-gather.16.cloned.1.call-start = ((), (), s32[]{:S(2)}) async-start(), calls=%async_computation.4 | async-start | bytes 2359296 | tf_op jit(solution)/shard_map/all_gather | solution.py:639
  10.6 269.4 %all-gather.20.cloned.1.call-start = ((), (), s32[]{:S(2)}) async-start(), calls=%async_computation.6 | async-start | bytes 9437184 | tf_op jit(solution)/shard_map/all_gather | solution.py:639
  11.1 298.1 %all-gather.22.cloned.1.call-start = ((), (), s32[]{:S(2)}) async-start(), calls=%async_computation.7 | async-start | bytes 2359296 | tf_op jit(solution)/shard_map/all_gather | solution.py:639
  11.9 388.6 %all-gather.24.cloned.1.call-start = ((), (), s32[]{:S(2)}) async-start(), calls=%async_computation.8 | async-start | bytes 9732096 | tf_op jit(solution)/shard_map/all_gather | solution.py:639
  119.3 17.5 %copy-start.2 = (bf16[128,1024]{1,0:T(8,128)(2,1)S(1)}, bf16[128,1024]{1,0:T(8,128)(2,1)}, u32[]{:S(2)}) copy-start(bf16[128,1024]{1,0:T(8,128)(2,1)} %param.13) | copy-start | bytes 786436
  129.9 67.0 %copy-start.10 = (bf16[128,1024]{1,0:T(8,128)(2,1)S(1)}, bf16[128,1024]{1,0:T(8,128)(2,1)}, u32[]{:S(2)}) copy-start(bf16[128,1024]{1,0:T(8,128)(2,1)} %param.25) | copy-start | bytes 786436
  168.9 31.2 %copy-start.6 = (f32[128,1024]{1,0:T(8,128)}, f32[128,1024]{1,0:T(8,128)S(1)}, u32[]{:S(2)}) copy-start(f32[128,1024]{1,0:T(8,128)S(1)} %fusion.41) | copy-start | bytes 1572868
  284.7 32.7 %copy-start.3 = (bf16[128,4096]{1,0:T(8,128)(2,1)}, bf16[128,4096]{1,0:T(8,128)(2,1)S(1)}, u32[]{:S(2)}) copy-start(bf16[128,4096]{1,0:T(8,128)(2,1)S(1)} %convolution_convert_fusion.1) | copy-start | bytes 3145732
  284.7 32.5 %copy-start.16 = (s32[128,4,32]{0,2,1:T(8,128)S(1)}, s32[128,4,32]{0,2,1:T(8,128)}, u32[]{:S(2)}) copy-start(s32[128,4,32]{0,2,1:T(8,128)} %param.15) | copy-start | bytes 196612
  330.0 12.3 %all-to-all-start = ((s32[32,1,1024]{2,1,0:T(1,128)}), s32[32,1,1024]{2,1,0:T(1,128)S(1)}, u32[]{:S(2)}, u32[]{:S(2)}) async-start(s32[32,1,1024]{2,1,0:T(1,128)} %bitcast.7), calls=%async_computation | async-start | bytes 262144 | tf_op jit(solution)/shard_map/all_to_all | solution.py:653
  334.1 310.4 %all-gather.26.cloned.1.call-start = ((), (), s32[]{:S(2)}) async-start(), calls=%async_computation.9 | async-start | bytes 2654208 | tf_op jit(solution)/shard_map/all_gather | solution.py:639
  334.3 187.5 %copy-start.21 = (f32[128]{0:T(128)}, f32[128]{0:T(128)S(1)}, u32[]{:S(2)}) copy-start(f32[128]{0:T(128)S(1)} %fusion.18) | copy-start | bytes 1540
  334.3 245.1 %copy-start.17 = (f32[128]{0:T(128)}, f32[128]{0:T(128)S(1)}, u32[]{:S(2)}) copy-start(f32[128]{0:T(128)S(1)} %add_rsqrt_fusion.1) | copy-start | bytes 1540
  400.5 2.2 copy-start
  521.7 54.4 %copy-start.7 = (f32[128,1024]{1,0:T(8,128)S(1)}, f32[128,1024]{1,0:T(8,128)}, u32[]{:S(2)}) copy-start(f32[128,1024]{1,0:T(8,128)} %copy-done.6) | copy-start | bytes 1572868
  521.7 56.9 %copy-start.8 = (f32[128,1024]{1,0:T(8,128)S(1)}, f32[128,1024]{1,0:T(8,128)}, u32[]{:S(2)}) copy-start(f32[128,1024]{1,0:T(8,128)} %get-tuple-element.19) | copy-start | bytes 1572868
  521.7 58.5 %copy-start.11 = (bf16[128,1024]{1,0:T(8,128)(2,1)S(1)}, bf16[128,1024]{1,0:T(8,128)(2,1)}, u32[]{:S(2)}) copy-start(bf16[128,1024]{1,0:T(8,128)(2,1)} %param.25) | copy-start | bytes 786436
  576.1 14.0 %copy-start.1 = (bf16[2048,512]{1,0:T(8,128)(2,1)S(1)}, bf16[2048,512]{1,0:T(8,128)(2,1)}, u32[]{:S(2)}) copy-start(bf16[2048,512]{1,0:T(8,128)(2,1)} %all-gather.22.cloned.1.call-done) | copy-start | bytes 6291460
  597.2 6.8 copy-start.5
  597.2 7.8 copy-start.12
  603.9 2.7 copy-start.4
  603.9 2.6 copy-start.9
  605.0 5.3 copy-start.19
  605.9 0.7 copy-start.14
  652.5 15.3 %copy-start.18 = (f32[128]{0:T(128)S(1)}, f32[128]{0:T(128)}, u32[]{:S(2)}) copy-start(f32[128]{0:T(128)} %copy-done.17) | copy-start | bytes 1540
  806.9 3.4 copy-start.22
  806.9 3.4 copy-start.13
  806.9 3.4 copy-start.15
  806.9 3.4 copy-start.20
Sparse Core Ops, SparseCore 0:
  9.6 31.7 all-gather.9
  43.1 64.2 all-gather.11
  109.0 27.7 all-gather.13
  138.2 28.5 all-gather.17
  168.3 28.5 all-gather.15
  198.4 81.5 all-gather.19
  281.6 27.6 all-gather.21
  317.3 83.1 all-gather.23
  614.3 30.1 all-gather.25

commit v3 on v2

--- a/solution.py
+++ b/solution.py
@@ -487,6 +487,172 @@
     )(part.reshape(2, 4, 4, rows, columns))
 
 
+def gather_kernel(pieces, count, *refs):
+    sources, targets = refs[:count], refs[count : 2 * count]
+    local_sem, send, recv = refs[2 * count :]
+    g, m, across, along, sibling = places()
+    z = m // 2
+    to_x, to_y, to_s = (across, m), (along, m), (g, sibling)
+    enter(plane_peers())
+    total = range(len(pieces))
+    ways = [(sign, hop) for hop in (1, 2, 3) for sign in (1, -1)]
+
+    def view(piece, owner, quarter=None, part=None):
+        array, first, columns, _ = pieces[piece]
+        ref = targets[array]
+        size = ref.shape[0] // 8
+        start = owner * size
+        if quarter is not None:
+            size = size // 4
+            start = start + quarter * size
+        if part is not None:
+            size = size // 2
+            start = start + part * size
+        return ref.at[pl.ds(start, size), pl.ds(first, columns)]
+
+    def copy(piece, index, block, peer, src=None):
+        return pltpu.make_async_remote_copy(
+            src_ref=block if src is None else src,
+            dst_ref=block,
+            send_sem=send.at[piece, index],
+            recv_sem=recv.at[piece, index],
+            device_id=peer,
+            device_id_type=MESH,
+        )
+
+    def line(p, way, owner, src=None):
+        block = view(p, owner, g if pieces[p][3] else None)
+        peer = (g, (m + 8 + 2 * ways[way][0]) % 8)
+        return copy(p, way, block, peer, src)
+
+    def has(way, hop=None):
+        sign, distance = ways[way]
+        distance = distance if hop is None else hop
+        return z >= distance if sign > 0 else z + distance <= 3
+
+    def more(way):
+        return z <= 2 if ways[way][0] > 0 else z >= 1
+
+    def origin(way):
+        sign, distance = ways[way]
+        return (m + 8 - 2 * sign * distance) % 8
+
+    def planes(p, way):
+        block = view(p, origin(way), g)
+        return copy(p, 6 + way, block, to_x), copy(p, 12 + way, block, to_y)
+
+    def corners(p, way):
+        owner = origin(way)
+        return (
+            copy(p, 18 + way, view(p, owner, across, 0), to_y),
+            copy(p, 24 + way, view(p, owner, along, 1), to_x),
+        )
+
+    def core(p, way):
+        return copy(p, 30 + way, view(p, origin(way)), to_s)
+
+    def first(p):
+        array, start, columns, shared = pieces[p]
+        ref = sources[array]
+        whole = ref.at[:, pl.ds(start, columns)]
+        src = whole
+        if shared:
+            quarter = ref.shape[0] // 4
+            src = ref.at[pl.ds(g * quarter, quarter), pl.ds(start, columns)]
+        return (
+            [line(p, way, m, src) for way in (0, 1)],
+            pltpu.make_async_copy(whole, view(p, m), local_sem.at[p]),
+            copy(p, 36, view(p, m), to_s, whole),
+        )
+
+    for p in total:
+        out, near, side = first(p)
+        for way in (0, 1):
+            pl.when(more(way))(out[way].start)
+        near.start()
+        side.start()
+
+    def arrive(p, hop):
+        for way in (2 * hop - 2, 2 * hop - 1):
+
+            @pl.when(has(way))
+            def _():
+                line(p, way, origin(way)).wait_recv()
+                if hop < 3:
+                    pl.when(more(way))(line(p, way + 2, origin(way)).start)
+                if pieces[p][3]:
+                    for item in planes(p, way):
+                        item.start()
+                else:
+                    core(p, way).start()
+
+    def turn(p, hop):
+        for way in (2 * hop - 2, 2 * hop - 1):
+
+            @pl.when(has(way))
+            def _():
+                for item, after in zip(planes(p, way), corners(p, way), strict=True):
+                    item.wait_recv()
+                    after.start()
+
+    def cross(p, hop):
+        for way in (2 * hop - 2, 2 * hop - 1):
+
+            @pl.when(has(way))
+            def _():
+                for item in corners(p, way):
+                    item.wait_recv()
+                core(p, way).start()
+
+    shared = [p for p in total if pieces[p][3]]
+    for hop in range(1, 6):
+        for p in total:
+            if hop <= 3:
+                arrive(p, hop)
+            if p in shared and 1 <= hop - 1 <= 3:
+                turn(p, hop - 1)
+            if p in shared and 1 <= hop - 2 <= 3:
+                cross(p, hop - 2)
+    for p in total:
+        out, near, side = first(p)
+        near.wait()
+        side.wait()
+        for way in (0, 1):
+            pl.when(more(way))(out[way].wait_send)
+        for way in range(6):
+
+            @pl.when(has(way))
+            def _():
+                core(p, way).wait()
+                if ways[way][1] < 3:
+                    pl.when(more(way))(line(p, way + 2, origin(way)).wait_send)
+                if pieces[p][3]:
+                    for item in planes(p, way) + corners(p, way):
+                        item.wait_send()
+
+
+def gather_weights(arrays, chunk, own_count):
+    pieces = []
+    for i, x in enumerate(arrays):
+        columns = x.shape[1]
+        for first in range(0, columns, chunk):
+            pieces.append((i, first, min(chunk, columns - first), i >= own_count))
+    count = len(arrays)
+    return pl.pallas_call(
+        functools.partial(gather_kernel, tuple(pieces), count),
+        in_specs=[pl.BlockSpec(memory_space=pl.ANY)] * count,
+        out_specs=[pl.BlockSpec(memory_space=pl.ANY)] * count,
+        out_shape=[jax.ShapeDtypeStruct((8 * x.shape[0], x.shape[1]), x.dtype) for x in arrays],
+        scratch_shapes=[
+            pltpu.SemaphoreType.DMA((len(pieces),)),
+            pltpu.SemaphoreType.DMA((len(pieces), 37)),
+            pltpu.SemaphoreType.DMA((len(pieces), 37)),
+        ],
+        compiler_params=pltpu.CompilerParams(collective_id=3, has_side_effects=True),
+        name="gather_weights",
+    )(*arrays)
+
+
 WIDTH = HEADS * HDIM
 KEYS = MHEADS * 2 * NK
 QUERIES = MHEADS * 2 * HALF
@@ -638,16 +804,45 @@
     def gather(x, axes="mem"):
         return lax.all_gather(x, axes, axis=0, tiled=True)
 
-    gains = lax.all_gather(jnp.stack([attn_gain, mem_gain]), "mem", axis=1, tiled=True)
+    if linked:
+        gain_block = jnp.concatenate(
+            [attn_gain[None], mem_gain[None], jnp.zeros((14, LANES), BF)]
+        )
+        (
+            tokens_all,
+            gains,
+            qkv_full,
+            proj_full,
+            keys_full,
+            query_full,
+            gate_full,
+            output_full,
+        ) = gather_weights(
+            (
+                tokens,
+                gain_block,
+                qkv_weight,
+                attn_proj,
+                half_keys,
+                query_weight,
+                gate_weight,
+                out_weight,
+            ),
+            2 * width,
+            2,
+        )
+        gains = gains.reshape(8, 16, LANES)[:, :2].transpose(1, 0, 2).reshape(2, width)
+    else:
+        gains = lax.all_gather(jnp.stack([attn_gain, mem_gain]), "mem", axis=1, tiled=True)
+        tokens_all = gather(tokens)
+        qkv_full = gather(qkv_weight)
+        proj_full = gather(attn_proj)
+        query_full = gather(query_weight)
+        keys_full = gather(half_keys)
+        gate_full = gather(gate_weight)
+        output_full = gather(out_weight)
     gains = gains.astype(F32)
     gain_one, gain_two = gains[0:1], gains[1:2]
-    tokens_all = gather(tokens)
-    qkv_full = gather(qkv_weight)
-    proj_full = gather(attn_proj)
-    query_full = gather(query_weight)
-    keys_full = gather(half_keys)
-    gate_full = gather(gate_weight)
-    output_full = gather(out_weight)
 
     requests = route(picks, owners, local_rows, capacity, flat_bits)
     arrived = lax.all_to_all(requests, ALL, split_axis=0, concat_axis=0, tiled=True)

time: 834 us -> 684 us (0.82)
  waiting for transfers between devices: 315 us -> 61.3 us
  Pallas kernels: 339 us -> 448 us
  blocking collectives: 13.4 us -> 0 us
    all_gather x9 -> x2, waiting for transfers between devices: 302 us -> 53.3 us  [gather(): return lax.all_gather(x, axes, axis=0, tiled=True)]
    pallas_call x0 -> x1, Pallas kernels: none -> 108 us  [gather_weights(): pl.pallas_call(functools.partial(gather_kernel, tuple(pieces), count), in...]
    all_gather x1 -> x0, blocking collectives: 13.4 us -> none  [per_device(): lax.all_gather(jnp.stack([attn_gain, mem_gain]), 'mem', axis=1, tiled=True)]
  transfers between devices with their start and end apart: 10 -> 3, of which waited for: 10 -> 3; matrix products, arithmetic and copies ran while one was open for 9% -> 7% of each run, Pallas kernels for 1% -> 0%
where the time goes in v3:
time: 684 us; the launch traced here: 675 us
  Pallas kernels  448 us (65%)
  matrix products  78.7 us (12%)
  waiting for transfers between devices  61.3 us (9%)
  local copies, waits for them, and re-layouts  35.3 us (5%)
  other arithmetic  34.3 us (5%)
  between operations  14.9 us (2%)
    pallas_call x1, Pallas kernels, reduce_grads(): pl.pallas_call(grads_kernel, in_specs=[pl.BlockSpec(memory_space=pl.ANY)]...  128 us
    pallas_call x1, Pallas kernels, owner_call(): pl.pallas_call(functools.partial(owner_kernel, his, flat_bits, local_rows...  119 us
    pallas_call x1, Pallas kernels, gather_weights(): pl.pallas_call(functools.partial(gather_kernel, tuple(pieces), count), in...  108 us
    pallas_call x1, Pallas kernels, return_rows(): pl.pallas_call(return_kernel, in_specs=[pl.BlockSpec(memory_space=pl.ANY)...  54.3 us
    all_gather x2, waiting for transfers between devices, gather(): return lax.all_gather(x, axes, axis=0, tiled=True)  53.3 us
    dot_general x11, matrix products, dot(): lax.dot_general(left, right, (dims, ((), ())), preferred_element_type=F32)  47.5 us
    dot_general x1, matrix products, per_device(): jnp.einsum('hkl,kd->hld', spread, sent[:, :width], preferred_element_type...  24.4 us
    unnamed x62, local copies, waits for them, and re-layouts  16.3 us
  transfers between devices with their start and end apart: 3, of which 3 were waited for; matrix products, arithmetic and copies ran while one was open for 7% of the time, Pallas kernels for 0%

profile of v3, /device:TPU:0, one launch (start us, length us, event | category | flops | bytes accessed | tf_op | source)
XLA Modules:
  0.0 675.3 jit_solution(5032954146723637331)
XLA Ops:
  7.3 1.3 maximum_maximum_fusion.refs_1_
  8.7 108.3 %gather_weights.1 = (bf16[1024,1024]{1,0:T(8,128)(2,1)}, bf16[128,128]{1,0:T(8,128)(2,1)}, bf16[1024,3072]{1,0:T(8,128)(2,1)}, bf16[1024,1024]{1,0:T(8,128)(2,1)...) custom-call(bf16[128,1024]{1,0:T(8,128)(2,1)} %refs_0_.1, ...), custom_call_target="tpu_custom_call" | custom-call | tf_op jit(solution)/shard_map/gather_weights/pallas_call | solution.py:641
  117.0 0.7 convert_bitcast_fusion
  117.7 2.1 fusion.1
  119.8 1.0 copy.93.qseg_ref.segc_ref
  120.8 11.9 %convolution_convert_fusion.q_ref.k_ref.v_ref = bf16[1024,3072]{1,0:T(8,128)(2,1)} fusion(bf16[1024,3072]{1,0:T(8,128)(2,1)} %get-tuple-element.29, bf16[1024,1024]{1,0:T(8,128)(2,1)} %get-tuple-element.27, f32[1024]{0:T(1024)S(1)} %bitcast.96, f32[1024]{0:T(1024)S(1)} %add_rsqrt_fusion), kind=kOutput, calls=%fused_computation.2 | convolution fusion | flops 6449790976 | bytes 14688256 | tf_op jit(solution)/shard_map/dot_general | solution.py:25
  132.8 10.7 %attn_fwd.1 = (f32[128,1024]{1,0:T(8,128)}, f32[128,128]{1,0:T(8,128)}) custom-call(s32[1]{0:T(128)} %bitcast.pos_ref, bf16[1024,3072]{1,0:T(8,128)(2,1)} %convolution_convert_fusion.q_ref.k_ref.v_ref, bf16[1024,3072]{1,0:T(8,128)(2,1)} %convolution_convert_fusion.q_ref.k_ref.v_ref, bf16[1024,3072]{1,0:T(8,128)(2,1)} %convolution_convert_fusion.q_ref.k_ref.v_ref, ...), custom_call_target="tpu_custom_call" | custom-call | flops 335544320 | bytes 4194304 | tf_op jit(solution)/shard_map/attn_fwd/pallas_call | solution.py:76
  143.4 1.6 multiply_reduce_fusion.2
  145.5 4.8 convolution_convert_fusion.1
  150.4 0.9 copy-done.4
  151.4 1.7 fusion.15
  153.1 2.5 copy.117.scores_ref
  155.6 0.7 copy.99.picks_ref
  156.3 2.1 fusion.41
  158.4 3.1 pick_fwd.1
  161.5 3.2 multiply_convert_fusion.2
  164.8 0.7 pad_maximum_fusion
  165.5 0.8 copy.94
  166.4 1.1 reshape.307
  169.2 0.9 pad_add_fusion
  170.7 12.3 %sort.14 = (s32[32768]{0:T(1024)}, s32[32768]{0:T(1024)}) sort(s32[32768]{0:T(1024)S(1)} %pad_add_fusion, s32[32768]{0:T(1024)} %iota.15), dimensions={0}, to_apply=%region_4.5 | sort | flops 491520 | bytes 524288 | tf_op jit(solution)/shard_map/sort | solution.py:355
  183.0 2.8 all-to-all-start
  186.0 8.0 %all-to-all-done.keys_ref = s32[32,1,1024]{2,1,0:T(1,128)S(1)} async-done(((s32[32,1,1024]{2,1,0:T(1,128)}), s32[32,1,1024]{2,1,0:T(1,128)S(1)}, u32[]{:S(2)}, u32[]{:S(2)}) %all-to-all-start) | async-done | bytes 131104 | tf_op jit(solution)/shard_map/all_to_all | solution.py:848
  194.0 52.0 %all-gather.3.cloned.1.call-done.sent_ref = bf16[4096,1152]{1,0:T(8,128)(2,1)} async-done(((bf16[128,1152]{1,0:T(8,128)(2,1)}), bf16[4096,1152]{1,0:T(8,128)(2,1)}) %all-gather.3.cloned.1.call-update) | async-done | bytes 9437200 | tf_op jit(solution)/shard_map/all_gather | solution.py:805
  246.0 2.2 copy-done
  248.2 119.1 %owner.1 = (bf16[4096,1152]{1,0:T(8,128)(2,1)}, bf16[4,4096,512]{2,1,0:T(8,128)(2,1)}) custom-call(s32[32,1,1024]{2,1,0:T(1,128)S(1)} %all-to-all-done.keys_ref, bf16[4096,1152]{1,0:T(8,128)(2,1)} %all-gather.3.cloned.1.call-done.sent_ref, bf16[2048,1024]{1,0:T(8,128)(2,1)S(1)} %copy-done), custom_call_target="tpu_custom_call" | custom-call | flops 68719476736 | bytes 33554432 | tf_op jit(solution)/shard_map/owner/pallas_call | solution.py:316
  367.3 54.3 %return_rows.1 = f32[128,1152]{1,0:T(8,128)S(1)} custom-call(bf16[2,4,4,128,1152]{4,3,2,1,0:T(8,128)(2,1)} %bitcast.79), custom_call_target="tpu_custom_call" | custom-call | tf_op jit(solution)/shard_map/return_rows/pallas_call | solution.py:470
  422.2 1.0 constant_dynamic-update-slice_fusion.7
  423.2 9.3 %pick_bwd.1 = bf16[128,2048]{1,0:T(8,128)(2,1)} custom-call(f32[128,128]{1,0:T(8,128)} %get-tuple-element.39.weight_ref, f32[128,128]{1,0:T(8,128)} %slice.64.grad_ref, s32[128,128]{1,0:T(8,128)} %copy.99.picks_ref), custom_call_target="tpu_custom_call" | custom-call | tf_op jit(solution)/shard_map/pick_bwd/pallas_call | solution.py:257
  432.5 1.9 convolution_convert_fusion.2
  434.4 6.4 fusion.42
  440.9 0.8 constant_dynamic-update-slice_fusion.6
  441.7 0.8 convert_dynamic-update-slice_fusion
  442.5 0.9 fusion.29
  443.4 0.8 constant_dynamic-update-slice_fusion.5
  444.2 1.0 constant_dynamic-update-slice_fusion.4
  445.2 1.0 multiply_reduce_fusion
  446.2 0.9 constant_dynamic-update-slice_fusion.3
  447.1 0.7 copy-done.14
  447.8 1.6 fusion.13
  449.4 2.0 copy.103
  451.4 1.1 bitcast_reduce_fusion
  452.6 0.9 fusion.31
  453.6 1.8 concatenate.42
  455.4 1.9 constant_dynamic-update-slice_fusion.2
  457.3 2.8 fusion.14
  460.1 24.4 %fusion = f32[4,512,1024]{2,1,0:T(8,128)} fusion(bf16[4,4096,512]{2,1,0:T(8,128)(2,1)} %get-tuple-element.41, bf16[4096,1152]{1,0:T(8,128)(2,1)} %all-gather.3.cloned.1.call-done.sent_ref), kind=kOutput, calls=%fused_computation.1 | convolution fusion | flops 17179869184 | bytes 33554432 | tf_op jit(solution)/shard_map/hkl,kd->hld/dot_general | solution.py:886
  484.5 1.3 all-gather.5.cloned.1.call-done
  485.7 5.9 fusion.9.da_ref
  491.7 2.0 convert_add_fusion.stat_ref
  493.7 15.3 %attn_bwd.1 = bf16[128,3072]{1,0:T(8,128)(2,1)} custom-call(s32[1]{0:T(128)} %bitcast.pos_ref, bf16[1024,3072]{1,0:T(8,128)(2,1)} %convolution_convert_fusion.q_ref.k_ref.v_ref, bf16[1024,3072]{1,0:T(8,128)(2,1)} %convolution_convert_fusion.q_ref.k_ref.v_ref, bf16[1024,3072]{1,0:T(8,128)(2,1)} %convolution_convert_fusion.q_ref.k_ref.v_ref, ...), custom_call_target="tpu_custom_call" | custom-call | flops 1174405120 | bytes 8388608 | tf_op jit(solution)/shard_map/attn_bwd/pallas_call | solution.py:162
  509.0 6.1 fusion.25
  515.7 2.1 constant_dynamic-update-slice_fusion.1
  517.8 2.3 constant_dynamic-update-slice_fusion.fact_ref
  520.1 127.9 %reduce_grads.1 = bf16[4,32,9344]{2,1,0:T(8,128)(2,1)} custom-call(bf16[128,16384]{1,0:T(8,128)(2,1)} %constant_dynamic-update-slice_fusion.fact_ref, bf16[16,1024]{1,0:T(8,128)(2,1)} %concatenate.44.gain_ref), custom_call_target="tpu_custom_call" | custom-call | tf_op jit(solution)/shard_map/reduce_grads/pallas_call | solution.py:745
  648.0 2.0 bitcast_convert_fusion
  650.0 1.4 slice.87
  651.4 1.2 copy-done.2
  652.7 1.9 slice.90
  654.6 2.0 copy.118
  656.6 3.3 fusion.43
  659.9 3.0 copy.111
  662.9 3.1 fusion.39
  666.4 0.9 copy.109
  (84 shorter events, 5.9 us)
Async XLA Ops:
  7.2 112.6 %copy-start.18 = (s32[1024]{0:T(1024)S(1)}, s32[1024]{0:T(1024)}, u32[]{:S(2)}) copy-start(s32[1024]{0:T(1024)} %param.14) | copy-start | bytes 12292
  7.2 238.9 %all-gather.3.cloned.1.call-start = ((), (), s32[]{:S(2)}) async-start(), calls=%async_computation.1 | async-start | bytes 9732096 | tf_op jit(solution)/shard_map/all_gather | solution.py:805
  132.8 10.7 %copy-start.3 = (bf16[128,1024]{1,0:T(8,128)(2,1)S(1)}, bf16[128,1024]{1,0:T(8,128)(2,1)}, u32[]{:S(2)}) copy-start(bf16[128,1024]{1,0:T(8,128)(2,1)} %refs_0_.1) | copy-start | bytes 786436
  132.8 10.7 %copy-start.5 = (bf16[1024,1024]{1,0:T(8,128)(2,1)S(1)}, bf16[1024,1024]{1,0:T(8,128)(2,1)}, u32[]{:S(2)}) copy-start(bf16[1024,1024]{1,0:T(8,128)(2,1)} %get-tuple-element.31) | copy-start | bytes 6291460
  145.0 0.5 copy-start.26
  145.5 5.8 copy-start.1
  150.4 1.0 copy-start.4
  150.4 5.2 copy-start.17
  158.4 12.3 %copy-start.8 = (f32[128,1024]{1,0:T(8,128)}, f32[128,1024]{1,0:T(8,128)S(1)}, u32[]{:S(2)}) copy-start(f32[128,1024]{1,0:T(8,128)S(1)} %fusion.41) | copy-start | bytes 1572868
  161.5 3.2 copy-start.19
  183.0 11.0 %all-to-all-start = ((s32[32,1,1024]{2,1,0:T(1,128)}), s32[32,1,1024]{2,1,0:T(1,128)S(1)}, u32[]{:S(2)}, u32[]{:S(2)}) async-start(s32[32,1,1024]{2,1,0:T(1,128)} %bitcast.95), calls=%async_computation | async-start | bytes 262144 | tf_op jit(solution)/shard_map/all_to_all | solution.py:848
  185.8 299.9 %all-gather.5.cloned.1.call-start = ((), (), s32[]{:S(2)}) async-start(), calls=%async_computation.2 | async-start | bytes 2654208 | tf_op jit(solution)/shard_map/all_gather | solution.py:805
  186.0 181.3 %copy-start.24 = (f32[128]{0:T(128)}, f32[128]{0:T(128)S(1)}, u32[]{:S(2)}) copy-start(f32[128]{0:T(128)S(1)} %fusion.18) | copy-start | bytes 1540
  186.0 256.5 %copy-start.20 = (f32[128]{0:T(128)}, f32[128]{0:T(128)S(1)}, u32[]{:S(2)}) copy-start(f32[128]{0:T(128)S(1)} %add_rsqrt_fusion.1) | copy-start | bytes 1540
  246.0 2.2 copy-start
  367.3 55.0 %copy-start.9 = (f32[128,1024]{1,0:T(8,128)S(1)}, f32[128,1024]{1,0:T(8,128)}, u32[]{:S(2)}) copy-start(f32[128,1024]{1,0:T(8,128)} %copy-done.8) | copy-start | bytes 1572868
  434.4 7.4 %copy-start.11 = (f32[128,1024]{1,0:T(8,128)S(1)}, f32[128,1024]{1,0:T(8,128)}, u32[]{:S(2)}) copy-start(f32[128,1024]{1,0:T(8,128)} %get-tuple-element.30) | copy-start | bytes 1572868
  434.4 9.1 %copy-start.12 = (bf16[128,1024]{1,0:T(8,128)(2,1)S(1)}, bf16[128,1024]{1,0:T(8,128)(2,1)}, u32[]{:S(2)}) copy-start(bf16[128,1024]{1,0:T(8,128)(2,1)} %param.25) | copy-start | bytes 786436
  434.4 9.8 %copy-start.10 = (f32[128,1024]{1,0:T(8,128)S(1)}, f32[128,1024]{1,0:T(8,128)}, u32[]{:S(2)}) copy-start(f32[128,1024]{1,0:T(8,128)} %copy-done.8) | copy-start | bytes 1572868
  434.4 9.8 %copy-start.16 = (f32[128,1024]{1,0:T(8,128)S(1)}, f32[128,1024]{1,0:T(8,128)}, u32[]{:S(2)}) copy-start(f32[128,1024]{1,0:T(8,128)} %get-tuple-element.124) | copy-start | bytes 1572868
  440.9 4.3 copy-start.7
  440.9 5.2 copy-start.27
  443.4 4.3 copy-start.6
  446.2 5.3 copy-start.22
  447.1 0.7 copy-start.14
  493.7 15.3 %copy-start.21 = (f32[128]{0:T(128)S(1)}, f32[128]{0:T(128)}, u32[]{:S(2)}) copy-start(f32[128]{0:T(128)} %copy-done.20) | copy-start | bytes 1540
  650.0 2.7 copy-start.2
  656.6 6.2 copy-start.25
  656.6 6.2 copy-start.23
  659.9 3.0 copy-start.13
  659.9 3.0 copy-start.15
Sparse Core Ops, SparseCore 0:
  165.7 80.3 all-gather.2
  455.5 30.2 all-gather.4

commit v4 on v3

--- a/solution.py
+++ b/solution.py
@@ -307,7 +307,7 @@
     ).astype(BF)
 
 
-def owner_call(keys, sent, values, flat_bits, order):
+def owner_call(keys, sent, values, flat_bits):
     owners, slots = keys.shape
     rows = sent.shape[0] // owners
     local_rows, width = values.shape
@@ -322,7 +322,7 @@
             pl.BlockSpec((local_rows, width), lambda s: (0, 0)),
         ],
         out_specs=[
-            pl.BlockSpec((rows, width + LANES), lambda s: (order(s), 0)),
+            pl.BlockSpec((rows, width + LANES), lambda s: (s, 0)),
             pl.BlockSpec((his, rows, low_rows), lambda s: (0, s, 0)),
         ],
         out_shape=[
@@ -428,33 +428,6 @@
     return [(across, m), (along, m), (g, sibling)] + [(g, (m + 2 * d) % 8) for d in (1, 2, 3)]
 
 
-def return_kernel(part_ref, out_ref, held, sib, x1, y1, x2, y2, zin, local_sem, send, recv):
-    g, m, _, _, sibling = places()
-    core, z = m % 2, m // 2
-    enter(plane_peers())
-    locals_, remotes = [], []
-    for k in range(4):
-        level = (z + 3 - k) % 4
-        copy = pltpu.make_async_copy(part_ref.at[core, level], held.at[k], local_sem.at[k])
-        copy.start()
-        locals_.append(copy)
-        remotes.append(
-            push(
-                part_ref.at[1 - core, level], sib.at[k], send.at[5, k], recv.at[5, k], (g, sibling)
-            )
-        )
-
-    def ready(k):
-        locals_[k].wait()
-        remotes[k].wait_recv()
-        for i in range(4):
-            held[k, i] = held[k, i] + sib[k, i]
-
-    out_ref[...] = reduce_planes(held, ready, x1, y1, x2, y2, zin, send, recv)
-    for copy in remotes:
-        copy.wait_send()
-
-
 def plane_scratch(rows, columns):
     return [
         pltpu.VMEM((4, rows // 2, columns), BF),
@@ -465,26 +438,289 @@
     ]
 
 
-def return_rows(part, rows):
-    columns = part.shape[1]
+def memory_kernel(
+    flat_bits,
+    payload_ref,
+    keys_ref,
+    picks_ref,
+    values_ref,
+    out_ref,
+    spread_ref,
+    sent_ref,
+    sent,
+    parts,
+    sibs,
+    x1,
+    y1,
+    x2,
+    y2,
+    zin,
+    held,
+    spread,
+    own_sem,
+    spread_sem,
+    sent_sem,
+    send,
+    recv,
+):
+    g, m, across, along, sibling = places()
+    core, z = m % 2, m // 2
+    to_x, to_y, to_s = (across, m), (along, m), (g, sibling)
+    rows, columns = payload_ref.shape
+    width = columns - LANES
+    local_rows = values_ref.shape[0]
+    slots = keys_ref.shape[1]
+    his = spread.shape[1]
+    low_rows = local_rows // his
+    low, high = pl.ds(0, rows // 2), pl.ds(rows // 2, rows // 2)
+    enter(plane_peers())
+
+    def copy(kind, index, src, dst, peer):
+        return pltpu.make_async_remote_copy(
+            src_ref=src,
+            dst_ref=dst,
+            send_sem=send.at[kind, index],
+            recv_sem=recv.at[kind, index],
+            device_id=peer,
+            device_id_type=MESH,
+        )
+
+    def mine(i):
+        return payload_ref if i == 0 else sent.at[i, core]
+
+    def to_sibling(i):
+        return copy(0, i, mine(i), sent.at[i, core], to_s)
+
+    def plane_x(k):
+        return copy(1, k, mine(4 * k), sent.at[4 * k + 1, core], to_x)
+
+    def plane_y(k):
+        return copy(2, k, mine(4 * k), sent.at[4 * k + 2, core], to_y)
+
+    def line(k):
+        return copy(3, k, payload_ref, sent.at[4 * k, core], (g, (m + 2 * k) % 8))
+
+    def corner_y(k):
+        return copy(4, k, sent.at[4 * k + 1, core, low], sent.at[4 * k + 3, core, low], to_y)
+
+    def corner_x(k):
+        return copy(5, k, sent.at[4 * k + 2, core, high], sent.at[4 * k + 3, core, high], to_x)
+
+    def part_sibling(i):
+        return copy(6, i, parts.at[i, 1 - core], sibs.at[i], to_s)
+
+    def one_x(k):
+        return copy(7, k, parts.at[4 * k + 3, core, low], x1.at[k], to_x)
+
+    def one_y(k):
+        return copy(8, k, parts.at[4 * k + 3, core, high], y1.at[k], to_y)
+
+    def two_x(k):
+        return copy(9, k, parts.at[4 * k + 1, core], x2.at[k], to_x)
+
+    def two_y(k):
+        return copy(10, k, parts.at[4 * k + 2, core], y2.at[k], to_y)
+
+    def three(k):
+        return copy(11, k, parts.at[4 * k, core], zin.at[k - 1], (g, (m + 8 - 2 * k) % 8))
+
+    def from_line(k):
+        line(k).wait_recv()
+        plane_x(k).start()
+        plane_y(k).start()
+        to_sibling(4 * k).start()
+
+    def from_plane(k):
+        plane_x(k).wait_recv()
+        corner_y(k).start()
+        to_sibling(4 * k + 1).start()
+        plane_y(k).wait_recv()
+        corner_x(k).start()
+        to_sibling(4 * k + 2).start()
+
+    def from_corner(k):
+        corner_x(k).wait_recv()
+        corner_y(k).wait_recv()
+        to_sibling(4 * k + 3).start()
+
+    def pair_sum(k):
+        for i in (4 * k + 3, 4 * k + 1, 4 * k + 2, 4 * k):
+            part_sibling(i).wait_recv()
+            parts[i, core] = parts[i, core] + sibs[i]
+            if i == 4 * k + 3:
+                one_x(k).start()
+                one_y(k).start()
+
+    def corner_sum(k):
+        one_x(k).wait_recv()
+        parts[4 * k + 2, core, low] = parts[4 * k + 2, core, low] + x1[k]
+        two_y(k).start()
+        one_y(k).wait_recv()
+        parts[4 * k + 1, core, high] = parts[4 * k + 1, core, high] + y1[k]
+        two_x(k).start()
+
+    def plane_sum(k):
+        two_x(k).wait_recv()
+        two_y(k).wait_recv()
+        total = parts[4 * k, core].astype(F32) + x2[k].astype(F32) + y2[k].astype(F32)
+        if k == 0:
+            held[...] = total
+        else:
+            parts[4 * k, core] = total.astype(BF)
+            three(k).start()
+
+    own = pltpu.make_async_copy(payload_ref, sent.at[0, core], own_sem)
+    own.start()
+    to_sibling(0).start()
+    plane_x(0).start()
+    plane_y(0).start()
+    for k in (1, 2, 3):
+        line(k).start()
+    own.wait()
+
+    tasks = {
+        1: [lambda: from_plane(0)],
+        2: [lambda: from_line(1)],
+        3: [lambda: from_corner(0), lambda: from_line(2)],
+        4: [lambda: from_line(3), lambda: pair_sum(0)],
+        5: [lambda: from_plane(1)],
+        6: [lambda: corner_sum(0)],
+        7: [lambda: from_corner(1)],
+        8: [lambda: from_plane(2), lambda: pair_sum(1)],
+        9: [lambda: plane_sum(0)],
+        10: [lambda: from_corner(2), lambda: corner_sum(1)],
+        11: [lambda: from_plane(3)],
+        12: [lambda: pair_sum(2), lambda: plane_sum(1)],
+        13: [lambda: from_corner(3)],
+        14: [lambda: corner_sum(2)],
+    }
+
+    def spread_copy(i, buffer):
+        return pltpu.make_async_copy(
+            spread.at[buffer],
+            spread_ref.at[:, pl.ds(pl.multiple_of(i * 2 * rows, 2 * rows), 2 * rows), :],
+            spread_sem.at[buffer],
+        )
+
+    def step(i, _):
+        for when, todo in tasks.items():
+
+            @pl.when(i == when)
+            def _():
+                for task in todo:
+                    task()
+
+        copy(0, i, sent.at[i, core], sent.at[i, 1 - core], to_s).wait_recv()
+        pltpu.make_async_copy(sent.at[i], sent_ref.at[i], sent_sem.at[i]).start()
+        buffer = i % 2
+        pl.when(i >= 2)(lambda: spread_copy(i - 2, buffer).wait())
+        k, j = i // 4, i % 4
+        grp = (g // 2 + j // 2) % 2 * 2 + (g % 2 + j % 2) % 2
+        base = grp * 8 + (z + 4 - k) % 4 * 2
+        local = picks_ref[pl.ds(pl.multiple_of(base * rows, 2 * rows), 2 * rows), :]
+        local = local - (g * 8 + m) * local_rows
+        lane, tile = local % LANES, local // LANES
+        for c in range(2):
+            key = keys_ref[pl.ds(base + c, 1), :]
+            flat = key & ((1 << flat_bits) - 1)
+            dummy = ((key >> flat_bits) & 1) == 1
+            row = (key >> (flat_bits + 1)) % local_rows
+            token = jnp.where(dummy, -1, flat // LANES)
+            block = jnp.where(dummy, -1, (row // low_rows) * rows + token)
+            is_token = iota((rows, slots), 0) == token
+            is_pick = iota((LANES, slots), 0) == flat % LANES
+            weights = sent[i, c, :, width:]
+            found = dot(weights, is_token.astype(F32).astype(BF), TN)
+            weight = jnp.sum(jnp.where(is_pick, found, 0.0), axis=0, keepdims=True)
+            is_block = iota((his * rows, slots), 0) == block
+            is_low = iota((low_rows, slots), 0) == row % low_rows
+            piece = dot(
+                jnp.where(is_block, weight, 0.0).astype(BF), is_low.astype(F32).astype(BF), NT
+            ).astype(BF)
+            for h in range(his):
+                spread[buffer, h, c * rows : (c + 1) * rows, :] = piece[h * rows : (h + 1) * rows]
+        grads = sent[i, :, :, :width].reshape(2 * rows, width)
+        total = jnp.zeros((2 * rows, width), F32)
+        picked = jnp.zeros((2 * rows, LANES), F32)
+        for h in range(his):
+            table = values_ref[h * low_rows : (h + 1) * low_rows, :]
+            total = total + dot(spread[buffer, h], table)
+            products = dot(grads, table, NT)
+            for b in range(low_rows // LANES):
+                found = jnp.take_along_axis(
+                    products[:, b * LANES : (b + 1) * LANES], lane, axis=1
+                )
+                picked = jnp.where(tile == h * (low_rows // LANES) + b, found, picked)
+        parts[i, :, :, :width] = total.astype(BF).reshape(2, rows, width)
+        parts[i, :, :, width:] = picked.astype(BF).reshape(2, rows, LANES)
+        part_sibling(i).start()
+        spread_copy(i, buffer).start()
+        return 0
+
+    lax.fori_loop(0, 16, step, 0)
+    plane_sum(2)
+    pair_sum(3)
+    corner_sum(3)
+    plane_sum(3)
+    total = held[...]
+    for k in (1, 2, 3):
+        three(k).wait_recv()
+        total = total + zin[k - 1].astype(F32)
+    out_ref[...] = total
+    for k in range(4):
+        todo = [plane_x(k), plane_y(k), corner_x(k), corner_y(k)]
+        todo += [one_x(k), one_y(k), two_x(k), two_y(k)]
+        if k:
+            todo += [line(k), three(k)]
+        for j in range(4):
+            todo += [to_sibling(4 * k + j), part_sibling(4 * k + j)]
+        for item in todo:
+            item.wait_send()
+    for i in (14, 15):
+        spread_copy(i, i % 2).wait()
+    for i in range(16):
+        pltpu.make_async_copy(sent.at[i], sent_ref.at[i], sent_sem.at[i]).wait()
+
+
+def memory_call(payload, keys, picks, values, flat_bits):
+    rows, columns = payload.shape
+    local_rows = values.shape[0]
+    his = 4
+    half = (4, rows // 2, columns)
+    full = (4, rows, columns)
+    vmem = pl.BlockSpec(memory_space=pltpu.VMEM)
+    hbm = pl.BlockSpec(memory_space=pl.ANY)
     return pl.pallas_call(
-        return_kernel,
-        in_specs=[pl.BlockSpec(memory_space=pl.ANY)],
-        out_specs=pl.BlockSpec(memory_space=pltpu.VMEM),
-        out_shape=jax.ShapeDtypeStruct((rows, columns), F32),
+        functools.partial(memory_kernel, flat_bits),
+        in_specs=[hbm, vmem, vmem, vmem],
+        out_specs=[vmem, hbm, hbm],
+        out_shape=[
+            jax.ShapeDtypeStruct((rows, columns), F32),
+            jax.ShapeDtypeStruct((his, 32 * rows, local_rows // his), BF),
+            jax.ShapeDtypeStruct((16, 2, rows, columns), BF),
+        ],
         scratch_shapes=[
-            pltpu.VMEM((4, 4, rows, columns), BF),
-            pltpu.VMEM((4, 4, rows, columns), BF),
-            *plane_scratch(rows, columns),
-            pltpu.SemaphoreType.DMA((4,)),
-            pltpu.SemaphoreType.DMA((6, 4)),
-            pltpu.SemaphoreType.DMA((6, 4)),
+            pltpu.VMEM((16, 2, rows, columns), BF),
+            pltpu.VMEM((16, 2, rows, columns), BF),
+            pltpu.VMEM((16, rows, columns), BF),
+            pltpu.VMEM(half, BF),
+            pltpu.VMEM(half, BF),
+            pltpu.VMEM(full, BF),
+            pltpu.VMEM(full, BF),
+            pltpu.VMEM((3, rows, columns), BF),
+            pltpu.VMEM((rows, columns), F32),
+            pltpu.VMEM((2, his, 2 * rows, local_rows // his), BF),
+            pltpu.SemaphoreType.DMA,
+            pltpu.SemaphoreType.DMA((2,)),
+            pltpu.SemaphoreType.DMA((16,)),
+            pltpu.SemaphoreType.DMA((12, 16)),
+            pltpu.SemaphoreType.DMA((12, 16)),
         ],
         compiler_params=pltpu.CompilerParams(
-            collective_id=1, has_side_effects=True, vmem_limit_bytes=48 * 1024 * 1024
+            collective_id=1, has_side_effects=True, vmem_limit_bytes=60 * 1024 * 1024
         ),
-        name="return_rows",
-    )(part.reshape(2, 4, 4, rows, columns))
+        name="memory",
+    )(payload, keys, picks, values)
 
 
 def gather_kernel(pieces, count, *refs):
@@ -804,7 +1040,9 @@
     def gather(x, axes="mem"):
         return lax.all_gather(x, axes, axis=0, tiled=True)
 
+    flat_picks = picks.reshape(rows, MHEADS * TOPK)
     if linked:
+        picks_all = gather(flat_picks, ALL)
         gain_block = jnp.concatenate(
             [attn_gain[None], mem_gain[None], jnp.zeros((14, LANES), BF)]
         )
@@ -870,17 +1108,15 @@
         key_table,
         preferred_element_type=F32,
     ).reshape(rows, MHEADS * 2 * NK)
-    flat_picks = picks.reshape(rows, MHEADS * TOPK)
     pick_weights, weights_low = pick_fwd(half_scores, flat_picks)
 
-    sent = gather(jnp.concatenate([memory_grad, weights_low], axis=1), ALL)
+    payload = jnp.concatenate([memory_grad, weights_low], axis=1)
     if linked:
-        part, spread = owner_call(
-            arrived, sent, memory_values, flat_bits, lambda s: s % 2 * 16 + s // 2 % 4 * 4 + s // 8
-        )
-        back = return_rows(part, rows)
+        back, spread, sent = memory_call(payload, arrived, picks_all, memory_values, flat_bits)
+        sent = sent.reshape(owners * rows, width + LANES)
     else:
-        part, spread = owner_call(arrived, sent, memory_values, flat_bits, lambda s: s)
+        sent = gather(payload, ALL)
+        part, spread = owner_call(arrived, sent, memory_values, flat_bits)
         back = lax.psum_scatter(part, "grp", scatter_dimension=0, tiled=True)
         back = lax.psum_scatter(back, "mem", scatter_dimension=0, tiled=True)
     values_grad = jnp.einsum(

time: 684 us -> 572 us (0.84)
  waiting for transfers between devices: 61.3 us -> 1.37 us
  Pallas kernels: 448 us -> 394 us
  starting transfers between devices: 2.9 us -> 17.4 us
    pallas_call x2 -> x1, Pallas kernels: 173 us -> 121 us  [memory_call(): pl.pallas_call(functools.partial(memory_kernel, flat_bits), in_specs=[hbm...]
    all_gather x2, waiting for transfers between devices: 53.3 us -> 1.33 us  [gather(): return lax.all_gather(x, axes, axis=0, tiled=True)]
    all_gather x2, starting transfers between devices: 0.08 us -> 10.1 us  [gather(): return lax.all_gather(x, axes, axis=0, tiled=True)]
    all_to_all x1, waiting for transfers between devices: 7.97 us -> 0.01 us  [per_device(): lax.all_to_all(requests, ALL, split_axis=0, concat_axis=0, tiled=True)]
    unnamed x62 -> x65, local copies, waits for them, and re-layouts: 16.3 us -> 12.8 us
  transfers between devices with their start and end apart: 3 -> 3, of which waited for: 3 -> 1; matrix products, arithmetic and copies ran while one was open for 7% -> 11% of each run, Pallas kernels for 0% -> 21%
where the time goes in v4:
time: 572 us; the launch traced here: 567 us
  Pallas kernels  394 us (69%)
  matrix products  75.9 us (13%)
  local copies, waits for them, and re-layouts  31.9 us (6%)
  other arithmetic  31.6 us (6%)
  starting transfers between devices  17.4 us (3%)
  between operations  14.7 us (3%)
    pallas_call x1, Pallas kernels, reduce_grads(): pl.pallas_call(grads_kernel, in_specs=[pl.BlockSpec(memory_space=pl.ANY)]...  128 us
    pallas_call x1, Pallas kernels, memory_call(): pl.pallas_call(functools.partial(memory_kernel, flat_bits), in_specs=[hbm...  121 us
    pallas_call x1, Pallas kernels, gather_weights(): pl.pallas_call(functools.partial(gather_kernel, tuple(pieces), count), in...  107 us
    dot_general x11, matrix products, dot(): lax.dot_general(left, right, (dims, ((), ())), preferred_element_type=F32)  44.8 us
    dot_general x1, matrix products, per_device(): jnp.einsum('hkl,kd->hld', spread, sent[:, :width], preferred_element_type...  24.4 us
    pallas_call x1, Pallas kernels, attn_bwd(): pl.pallas_call(functools.partial(attn_bwd_kernel, rows, win, pairs), grid...  15.2 us
    unnamed x65, local copies, waits for them, and re-layouts  12.8 us
  transfers between devices with their start and end apart: 3, of which 1 were waited for; matrix products, arithmetic and copies ran while one was open for 11% of the time, Pallas kernels for 21%

profile of v4, /device:TPU:0, one launch (start us, length us, event | category | flops | bytes accessed | tf_op | source)
XLA Modules:
  0.0 567.0 jit_solution(9740981614897861033)
XLA Ops:
  7.2 1.0 copy.101
  9.5 11.2 %sort.14 = (s32[32768]{0:T(1024)}, s32[32768]{0:T(1024)}) sort(s32[32768]{0:T(1024)S(1)} %pad_add_fusion, s32[32768]{0:T(1024)S(1)} %iota.15), dimensions={0}, to_apply=%region_5.6 | sort | flops 491520 | bytes 524288 | tf_op jit(solution)/shard_map/sort | solution.py:355
  20.6 7.3 %all-to-all-start = ((s32[32,1,1024]{2,1,0:T(1,128)}), s32[32,1,1024]{2,1,0:T(1,128)S(1)}, u32[]{:S(2)}, u32[]{:S(2)}) async-start(s32[32,1,1024]{2,1,0:T(1,128)} %bitcast.15), calls=%async_computation | async-start | bytes 262144 | tf_op jit(solution)/shard_map/all_to_all | solution.py:1086
  28.0 1.6 copy.100.picks_ref
  29.6 10.1 %all-gather.5.cloned.1.call-start = ((), (), s32[]{:S(2)}) async-start(), calls=%async_computation.2 | async-start | bytes 2654208 | tf_op jit(solution)/shard_map/all_gather | solution.py:1041
  39.8 1.3 maximum_maximum_fusion.refs_1_
  41.1 107.2 %gather_weights.1 = (bf16[1024,1024]{1,0:T(8,128)(2,1)}, bf16[128,128]{1,0:T(8,128)(2,1)}, bf16[1024,3072]{1,0:T(8,128)(2,1)}, bf16[1024,1024]{1,0:T(8,128)(2,1)...) custom-call(bf16[128,1024]{1,0:T(8,128)(2,1)} %refs_0_.1, ...), custom_call_target="tpu_custom_call" | custom-call | tf_op jit(solution)/shard_map/gather_weights/pallas_call | solution.py:877
  148.3 0.7 convert_bitcast_fusion
  149.1 2.1 fusion.1
  151.2 1.0 copy.96.qseg_ref.segc_ref
  152.2 12.0 %convolution_convert_fusion.q_ref.k_ref.v_ref = bf16[1024,3072]{1,0:T(8,128)(2,1)} fusion(bf16[1024,3072]{1,0:T(8,128)(2,1)} %get-tuple-element.30, bf16[1024,1024]{1,0:T(8,128)(2,1)} %get-tuple-element.28, f32[1024]{0:T(1024)S(1)} %bitcast.98, f32[1024]{0:T(1024)S(1)} %add_rsqrt_fusion), kind=kOutput, calls=%fused_computation.2 | convolution fusion | flops 6449790976 | bytes 14688256 | tf_op jit(solution)/shard_map/dot_general | solution.py:25
  164.2 10.2 %attn_fwd.1 = (f32[128,1024]{1,0:T(8,128)}, f32[128,128]{1,0:T(8,128)}) custom-call(s32[1]{0:T(128)} %bitcast.pos_ref, bf16[1024,3072]{1,0:T(8,128)(2,1)} %convolution_convert_fusion.q_ref.k_ref.v_ref, bf16[1024,3072]{1,0:T(8,128)(2,1)} %convolution_convert_fusion.q_ref.k_ref.v_ref, bf16[1024,3072]{1,0:T(8,128)(2,1)} %convolution_convert_fusion.q_ref.k_ref.v_ref, ...), custom_call_target="tpu_custom_call" | custom-call | flops 335544320 | bytes 4194304 | tf_op jit(solution)/shard_map/attn_fwd/pallas_call | solution.py:76
  174.6 1.7 multiply_reduce_fusion.2
  176.3 0.5 fusion.41
  176.8 4.8 convolution_convert_fusion.1
  181.7 1.7 fusion.15
  183.4 0.7 copy-done.16
  184.1 1.7 multiply_convert_fusion.2
  185.8 2.5 copy.121.scores_ref
  188.4 2.9 pick_fwd.1
  191.3 1.7 pad_maximum_fusion.payload_ref
  193.0 0.7 copy.135
  193.7 121.2 %memory.1 = (f32[128,1152]{1,0:T(8,128)}, bf16[4,4096,512]{2,1,0:T(8,128)(2,1)}, bf16[16,2,128,1152]{3,2,1,0:T(8,128)(2,1)}) custom-call(bf16[128,1152]{1,0:T(8,128)(2,1)} %pad_maximum_fusion.payload_ref, s32[32,1024]{1,0:T(8,128)} %bitcast.89, s32[4096,128]{1,0:T(8,128)} %all-gather.3.cloned.1.call-done.picks_ref, bf16[2048,1024]{1,0:T(8,128)(2,1)} %values_ref.1), custom_call_target="tpu_custom_call" | custom-call | tf_op jit(solution)/shard_map/memory/pallas_call | solution.py:693
  314.9 2.0 constant_dynamic-update-slice_fusion.7
  317.0 1.5 slice.64.grad_ref
  318.4 0.8 constant_dynamic-update-slice_fusion.6
  319.3 0.8 convert_dynamic-update-slice_fusion
  320.0 0.9 fusion.29
  320.9 1.7 constant_dynamic-update-slice_fusion.5
  322.6 9.5 %pick_bwd.1 = bf16[128,2048]{1,0:T(8,128)(2,1)} custom-call(f32[128,128]{1,0:T(8,128)} %get-tuple-element.40.weight_ref, f32[128,128]{1,0:T(8,128)} %slice.64.grad_ref, s32[128,128]{1,0:T(8,128)} %copy.100.picks_ref), custom_call_target="tpu_custom_call" | custom-call | tf_op jit(solution)/shard_map/pick_bwd/pallas_call | solution.py:257
  332.1 1.9 convolution_convert_fusion.2
  334.0 6.5 %fusion.42 = f32[128,1024]{1,0:T(8,128)S(1)} fusion(bf16[128,4096]{0,1:T(8,128)(2,1)S(1)} %bitcast.85, bf16[1024,4096]{1,0:T(8,128)(2,1)} %get-tuple-element.36), kind=kOutput, calls=%fused_computation.107 | convolution fusion | flops 1073741824 | bytes 9961472 | tf_op jit(solution)/shard_map/dot_general | solution.py:25
  340.5 0.9 constant_dynamic-update-slice_fusion.4
  341.5 1.0 multiply_reduce_fusion
  342.5 0.9 constant_dynamic-update-slice_fusion.3
  343.4 0.7 copy-done.14
  344.1 1.6 fusion.13
  345.7 2.0 copy.107
  347.8 1.1 bitcast_reduce_fusion
  349.0 0.9 fusion.31
  349.9 1.8 concatenate.42
  351.7 1.9 constant_dynamic-update-slice_fusion.2
  353.6 2.8 fusion.14
  356.5 24.4 %fusion = f32[4,512,1024]{2,1,0:T(8,128)} fusion(bf16[4,4096,512]{2,1,0:T(8,128)(2,1)} %get-tuple-element.42, bf16[4096,1152]{1,0:T(8,128)(2,1)} %bitcast.111), kind=kOutput, calls=%fused_computation.1 | convolution fusion | flops 17179869184 | bytes 33554432 | tf_op jit(solution)/shard_map/hkl,kd->hld/dot_general | solution.py:1122
  380.8 1.3 all-gather.5.cloned.1.call-done
  382.2 5.9 %fusion.9.da_ref = bf16[1024,1024]{1,0:T(8,128)(2,1)} fusion(bf16[1024,1024]{1,0:T(8,128)(2,1)} %get-tuple-element.32, bf16[1024,1152]{1,0:T(8,128)(2,1)} %all-gather.5.cloned.1.call-done), kind=kOutput, calls=%fused_computation.17 | convolution fusion | flops 2148532224 | bytes 6291456 | tf_op jit(solution)/shard_map/dot_general | solution.py:25
  388.1 2.0 convert_add_fusion.stat_ref
  390.1 15.2 %attn_bwd.1 = bf16[128,3072]{1,0:T(8,128)(2,1)} custom-call(s32[1]{0:T(128)} %bitcast.pos_ref, bf16[1024,3072]{1,0:T(8,128)(2,1)} %convolution_convert_fusion.q_ref.k_ref.v_ref, bf16[1024,3072]{1,0:T(8,128)(2,1)} %convolution_convert_fusion.q_ref.k_ref.v_ref, bf16[1024,3072]{1,0:T(8,128)(2,1)} %convolution_convert_fusion.q_ref.k_ref.v_ref, ...), custom_call_target="tpu_custom_call" | custom-call | flops 1174405120 | bytes 8388608 | tf_op jit(solution)/shard_map/attn_bwd/pallas_call | solution.py:162
  405.3 6.2 %fusion.25 = (f32[1024]{0:T(1024)S(1)}, f32[128]{0:T(128)S(1)}, f32[128,1024]{1,0:T(8,128)}) fusion(bf16[128,1024]{1,0:T(8,128)(2,1)S(1)} %copy-done.1, f32[128]{0:T(128)S(1)} %copy-done.22, f32[1024]{0:T(1024)S(1)} %bitcast.100, bf16[128,3072]{1,0:T(8,128)(2,1)} %attn_bwd.1, bf16[1024,3072]{1,0:T(8,128)(2,1)} %get-tuple-element.30), kind=kOutput, calls=%fused_computation.42 | convolution fusion | flops 806222720 | bytes 7873536 | tf_op jit(solution)/shard_map/dot_general | solution.py:25
  411.5 0.9 constant_dynamic-update-slice_fusion.1
  412.4 1.1 constant_dynamic-update-slice_fusion.fact_ref
  413.5 0.6 concatenate.44.gain_ref
  414.2 127.8 %reduce_grads.1 = bf16[4,32,9344]{2,1,0:T(8,128)(2,1)} custom-call(bf16[128,16384]{1,0:T(8,128)(2,1)} %constant_dynamic-update-slice_fusion.fact_ref, bf16[16,1024]{1,0:T(8,128)(2,1)} %concatenate.44.gain_ref), custom_call_target="tpu_custom_call" | custom-call | tf_op jit(solution)/shard_map/reduce_grads/pallas_call | solution.py:981
  542.0 2.0 bitcast_convert_fusion
  544.0 1.3 slice.87
  545.3 1.4 fusion.39
  546.7 0.7 slice_reduce_fusion
  547.4 1.9 slice.90
  549.3 2.0 copy.123
  551.3 3.2 fusion.43
  554.5 3.0 copy.115
  557.5 0.4 reshape.316
  558.0 0.9 copy.113
  558.9 1.1 fusion.21
  (86 shorter events, 1.8 us)
Async XLA Ops:
  7.2 144.0 %copy-start.20 = (s32[1024]{0:T(1024)S(1)}, s32[1024]{0:T(1024)}, u32[]{:S(2)}) copy-start(s32[1024]{0:T(1024)} %param.14) | copy-start | bytes 12292
  20.6 172.4 %all-to-all-start = ((s32[32,1,1024]{2,1,0:T(1,128)}), s32[32,1,1024]{2,1,0:T(1,128)S(1)}, u32[]{:S(2)}, u32[]{:S(2)}) async-start(s32[32,1,1024]{2,1,0:T(1,128)} %bitcast.15), calls=%async_computation | async-start | bytes 262144 | tf_op jit(solution)/shard_map/all_to_all | solution.py:1086
  27.9 165.8 %all-gather.3.cloned.1.call-start = ((), (), s32[]{:S(2)}) async-start(), calls=%async_computation.1 | async-start | bytes 2162688 | tf_op jit(solution)/shard_map/all_gather | solution.py:1041
  29.6 352.6 %all-gather.5.cloned.1.call-start = ((), (), s32[]{:S(2)}) async-start(), calls=%async_computation.2 | async-start | bytes 2654208 | tf_op jit(solution)/shard_map/all_gather | solution.py:1041
  164.2 10.2 %copy-start.1 = (bf16[128,1024]{1,0:T(8,128)(2,1)S(1)}, bf16[128,1024]{1,0:T(8,128)(2,1)}, u32[]{:S(2)}) copy-start(bf16[128,1024]{1,0:T(8,128)(2,1)} %refs_0_.1) | copy-start | bytes 786436
  164.2 10.4 %copy-start.4 = (bf16[1024,1024]{1,0:T(8,128)(2,1)S(1)}, bf16[1024,1024]{1,0:T(8,128)(2,1)}, u32[]{:S(2)}) copy-start(bf16[1024,1024]{1,0:T(8,128)(2,1)} %get-tuple-element.32) | copy-start | bytes 6291460
  174.4 1.9 copy-start.6
  174.6 2.3 copy-start.25
  176.3 0.6 copy-start.27
  176.3 143.8 %copy-start.21 = (f32[128]{0:T(128)}, f32[128]{0:T(128)S(1)}, u32[]{:S(2)}) copy-start(f32[128]{0:T(128)S(1)} %get-tuple-element.129) | copy-start | bytes 1540
  176.8 4.9 copy-start
  181.7 4.2 copy-start.2
  181.7 1.7 copy-start.11
  181.7 2.4 copy-start.16
  193.7 125.6 %copy-start.9 = (f32[128,1024]{1,0:T(8,128)S(1)}, f32[128,1024]{1,0:T(8,128)}, u32[]{:S(2)}) copy-start(f32[128,1024]{1,0:T(8,128)} %get-tuple-element.31) | copy-start | bytes 1572868
  333.9 6.6 %copy-start.15 = (f32[128,1152]{1,0:T(8,128)S(1)}, f32[128,1152]{1,0:T(8,128)}, u32[]{:S(2)}) copy-start(f32[128,1152]{1,0:T(8,128)} %get-tuple-element.39) | copy-start | bytes 1769476
  334.0 6.6 %copy-start.19 = (f32[128,1024]{1,0:T(8,128)S(1)}, f32[128,1024]{1,0:T(8,128)}, u32[]{:S(2)}) copy-start(f32[128,1024]{1,0:T(8,128)} %get-tuple-element.126) | copy-start | bytes 1572868
  334.0 7.5 %copy-start.7 = (bf16[1024,1024]{1,0:T(8,128)(2,1)S(1)}, bf16[1024,1024]{1,0:T(8,128)(2,1)}, u32[]{:S(2)}) copy-start(bf16[1024,1024]{1,0:T(8,128)(2,1)} %get-tuple-element.34) | copy-start | bytes 6291460
  340.4 2.0 copy-start.28
  340.5 2.0 copy-start.12
  340.5 3.6 copy-start.5
  340.5 3.6 copy-start.10
  342.5 5.3 copy-start.23
  343.4 0.7 copy-start.14
  390.1 15.2 %copy-start.22 = (f32[128]{0:T(128)S(1)}, f32[128]{0:T(128)}, u32[]{:S(2)}) copy-start(f32[128]{0:T(128)} %copy-done.21) | copy-start | bytes 1540
  405.3 6.2 %copy-start.8 = (bf16[128,3072]{1,0:T(8,128)(2,1)S(1)}, bf16[128,3072]{1,0:T(8,128)(2,1)}, u32[]{:S(2)}) copy-start(bf16[128,3072]{1,0:T(8,128)(2,1)} %attn_bwd.1) | copy-start | bytes 2359300
  405.3 7.2 %copy-start.3 = (bf16[128,4096]{1,0:T(8,128)(2,1)S(1)}, bf16[128,4096]{1,0:T(8,128)(2,1)}, u32[]{:S(2)}) copy-start(bf16[128,4096]{1,0:T(8,128)(2,1)} %copy-done.2) | copy-start | bytes 3145732
  544.0 2.7 copy-start.26
  554.5 3.0 copy-start.18
  554.5 4.3 copy-start.13
  554.5 4.3 copy-start.17
  554.5 4.3 copy-start.24
Sparse Core Ops, SparseCore 0:
  31.8 61.6 all-gather.2
  351.8 30.2 all-gather.4

commit v5 on v4

--- a/solution.py
+++ b/solution.py
@@ -103,12 +103,8 @@
     )(pos, qkv, qkv, qkv, seg_col, seg_row)
 
 
-def attn_bwd_kernel(
-    rows, win, pairs, pos_ref, q_ref, k_ref, v_ref, da_ref, stat_ref, segc_ref, segr_ref, out_ref
-):
-    pair = pl.program_id(0)
-    group_len = k_ref.shape[0]
-    row0 = pl.multiple_of(pos_ref[0] * rows, LANES)
+def attn_bwd_pair(rows, win, pair, position, group_len, load, stat_ref, segc_ref, segr_ref):
+    row0 = pl.multiple_of(position * rows, LANES)
     start = pl.multiple_of(jnp.maximum(row0 + rows - win, 0), LANES)
     qstart = pl.multiple_of(jnp.minimum(row0, group_len - win), LANES)
     own, back, ahead = pl.ds(row0, rows), pl.ds(start, win), pl.ds(qstart, win)
@@ -133,26 +129,45 @@
     for half in range(2):
         head = pair * 2 + half
         lse, delta = stat(own, head, rows), stat(own, HEADS + head, rows)
-        keys = k_ref[back, :]
-        scores = dot(q_ref[own, :] * masks[half], keys, NT) * 0.125
+        keys = load(1, back)
+        scores = dot(load(0, own) * masks[half], keys, NT) * 0.125
         probs = jnp.exp(jnp.where(allowed, scores - lse, NEG))
-        dprobs = dot(da_ref[own, :] * masks[half], v_ref[back, :], NT)
+        dprobs = dot(load(3, own) * masks[half], load(2, back), NT)
         grads = (probs * (dprobs - delta)).astype(BF)
         dqs.append(dot(grads, keys))
         lse, delta = stat(ahead, head, win), stat(ahead, HEADS + head, win)
-        queries, douts = q_ref[ahead, :], da_ref[ahead, :]
-        scores = dot(queries * masks[half], k_ref[own, :], NT) * 0.125
+        queries, douts = load(0, ahead), load(3, ahead)
+        scores = dot(queries * masks[half], load(1, own), NT) * 0.125
         probs = jnp.exp(jnp.where(allowed_two, scores - lse, NEG))
-        dprobs = dot(douts * masks[half], v_ref[own, :], NT)
+        dprobs = dot(douts * masks[half], load(2, own), NT)
         grads = (probs * (dprobs - delta)).astype(BF)
         dks.append(dot(grads, queries, TN))
         dvs.append(dot(probs.astype(BF), douts, TN))
-    width = pairs * LANES
-    for i, (parts, scale) in enumerate(((dqs, 0.125), (dks, 0.125), (dvs, 1.0))):
-        column = pl.multiple_of(i * width + pair * LANES, LANES)
-        out_ref[:, pl.ds(column, LANES)] = (
-            jnp.where(lane < HDIM, parts[0], parts[1]) * scale
-        ).astype(BF)
+    return [
+        (jnp.where(lane < HDIM, parts[0], parts[1]) * scale).astype(BF)
+        for parts, scale in ((dqs, 0.125), (dks, 0.125), (dvs, 1.0))
+    ]
+
+
+def attn_bwd_kernel(
+    rows, win, pairs, pos_ref, q_ref, k_ref, v_ref, da_ref, stat_ref, segc_ref, segr_ref, out_ref
+):
+    pair = pl.program_id(0)
+    refs = (q_ref, k_ref, v_ref, da_ref)
+    grads = attn_bwd_pair(
+        rows,
+        win,
+        pair,
+        pos_ref[0],
+        k_ref.shape[0],
+        lambda which, where: refs[which][where, :],
+        stat_ref,
+        segc_ref,
+        segr_ref,
+    )
+    for i, value in enumerate(grads):
+        column = pl.multiple_of((i * pairs + pair) * LANES, LANES)
+        out_ref[:, pl.ds(column, LANES)] = value
 
 
 def attn_bwd(pos, qkv, douts, stats, seg_row, seg_col, rows):
@@ -229,37 +244,43 @@
     )(half_scores, picks)
 
 
-def pick_bwd_kernel(weight_ref, grad_ref, picks_ref, out_ref):
+def pick_bwd_kernel(weight_ref, grad_ref, picks_ref, out_ref, score_t, first_t, second_t):
     rows = picks_ref.shape[0]
     lane = iota((rows, LANES), 1)
-    weights, grads, picks = weight_ref[...], grad_ref[...], picks_ref[...]
+    weights, grads = weight_ref[...], grad_ref[...]
     score = (weights * (grads - by_head(lane, jnp.sum, 0.0, weights * grads))).astype(BF)
-    score = score.astype(F32)
-    index = (picks // NK, picks % NK)
-    key = iota((rows, NK), 1)
-    for c in range(MHEADS):
-        totals = [jnp.zeros((rows, NK), F32) for _ in range(2)]
+    score_t[...] = score.astype(F32).T
+    picks_t = picks_ref[...].T
+    first_t[...] = picks_t // NK
+    second_t[...] = picks_t % NK
+    key = iota((NK, rows), 0)
+
+    def head(c, _):
+        first = jnp.zeros((NK, rows), F32)
+        second = jnp.zeros((NK, rows), F32)
         for j in range(TOPK):
-            column = slice(c * TOPK + j, c * TOPK + j + 1)
-            for e in range(2):
-                totals[e] = totals[e] + jnp.where(
-                    key == index[e][:, column], score[:, column], 0.0
-                )
-        for e in range(2):
-            base = (c * 2 + e) * NK
-            out_ref[:, base : base + NK] = totals[e].astype(BF)
+            at = pl.ds(c * TOPK + j, 1)
+            value = score_t[at, :]
+            first = first + jnp.where(key == first_t[at, :], value, 0.0)
+            second = second + jnp.where(key == second_t[at, :], value, 0.0)
+        for e, total in enumerate((first, second)):
+            base = pl.multiple_of((c * 2 + e) * NK, LANES)
+            out_ref[:, pl.ds(base, NK)] = total.T.astype(BF)
+        return 0
+
+    lax.fori_loop(0, MHEADS, head, 0)
 
 
 def pick_bwd(weights, grads, picks):
     rows = picks.shape[0]
-    block = 32
-    spec = pl.BlockSpec((block, LANES), lambda i: (i, 0))
     return pl.pallas_call(
         pick_bwd_kernel,
-        grid=(rows // block,),
-        in_specs=[spec, spec, spec],
-        out_specs=pl.BlockSpec((block, MHEADS * 2 * NK), lambda i: (i, 0)),
         out_shape=jax.ShapeDtypeStruct((rows, MHEADS * 2 * NK), BF),
+        scratch_shapes=[
+            pltpu.VMEM((LANES, rows), F32),
+            pltpu.VMEM((LANES, rows), jnp.int32),
+            pltpu.VMEM((LANES, rows), jnp.int32),
+        ],
         name="pick_bwd",
     )(weights, grads, picks)
 
@@ -352,7 +373,7 @@
     )
     real = (rows_of << (flat_bits + 1)) + flat
     spare = ((spare_owner * local_rows + local_rows - 1) << (flat_bits + 1)) + (1 << flat_bits)
-    keys = lax.sort(jnp.concatenate([real, spare]))
+    keys = lax.sort(jnp.concatenate([real, spare]), is_stable=False)
     return keys.reshape(owners, capacity)
 
 
@@ -382,45 +403,54 @@
     return copy
 
 
-def reduce_planes(held, ready, x1, y1, x2, y2, zin, send, recv):
+def plane_tasks(held, x1, y1, x2, y2, zin, send, recv):
     g, m, across, along, _ = places()
     diagonal = 3 - g
     half = held.shape[2] // 2
     low, high = pl.ds(0, half), pl.ds(half, half)
     to_x, to_y = (across, m), (along, m)
-    sent, ones, twos, threes = [], [], [], []
-    for k in range(4):
-        ready(k)
-        a = push(held.at[k, diagonal, low], x1.at[k], send.at[0, k], recv.at[0, k], to_x)
-        b = push(held.at[k, diagonal, high], y1.at[k], send.at[1, k], recv.at[1, k], to_y)
-        ones.append((a, b))
-    for k in range(4):
-        a, b = ones[k]
-        a.wait_recv()
-        b.wait_recv()
+    ones, twos, threes, totals = {}, {}, {}, {}
+
+    def first(k):
+        ones[k] = (
+            push(held.at[k, diagonal, low], x1.at[k], send.at[0, k], recv.at[0, k], to_x),
+            push(held.at[k, diagonal, high], y1.at[k], send.at[1, k], recv.at[1, k], to_y),
+        )
+
+    def corner(k):
+        for copy in ones[k]:
+            copy.wait_recv()
         held[k, along, low] = held[k, along, low] + x1[k]
         held[k, across, high] = held[k, across, high] + y1[k]
-        a = push(held.at[k, across], x2.at[k], send.at[2, k], recv.at[2, k], to_x)
-        b = push(held.at[k, along], y2.at[k], send.at[3, k], recv.at[3, k], to_y)
-        twos.append((a, b))
-    total = None
-    for k in range(4):
-        a, b = twos[k]
-        a.wait_recv()
-        b.wait_recv()
+        twos[k] = (
+            push(held.at[k, across], x2.at[k], send.at[2, k], recv.at[2, k], to_x),
+            push(held.at[k, along], y2.at[k], send.at[3, k], recv.at[3, k], to_y),
+        )
+
+    def plane(k):
+        for copy in twos[k]:
+            copy.wait_recv()
         total = held[k, g].astype(F32) + x2[k].astype(F32) + y2[k].astype(F32)
-        if k < 3:
+        if k == 3:
+            totals[k] = total
+        else:
             held[k, g] = total.astype(BF)
             peer = (g, (m + 2 * (3 - k)) % 8)
-            threes.append(push(held.at[k, g], zin.at[k], send.at[4, k], recv.at[4, k], peer))
-    for k in range(3):
-        threes[k].wait_recv()
-        total = total + zin[k].astype(F32)
-    for pair in ones + twos:
-        sent.extend(pair)
-    for copy in sent + threes:
-        copy.wait_send()
-    return total
+            threes[k] = push(held.at[k, g], zin.at[k], send.at[4, k], recv.at[4, k], peer)
+
+    def last():
+        total = totals[3]
+        for k in range(3):
+            threes[k].wait_recv()
+            total = total + zin[k].astype(F32)
+        for k in range(4):
+            for copy in ones[k] + twos[k]:
+                copy.wait_send()
+            if k < 3:
+                threes[k].wait_send()
+        return total
+
+    return first, corner, plane, last
 
 
 def plane_peers():
@@ -442,11 +472,9 @@
     flat_bits,
     payload_ref,
     keys_ref,
-    picks_ref,
     values_ref,
     out_ref,
-    spread_ref,
-    sent_ref,
+    grad_ref,
     sent,
     parts,
     sibs,
@@ -457,9 +485,9 @@
     zin,
     held,
     spread,
+    table,
     own_sem,
-    spread_sem,
-    sent_sem,
+    table_sem,
     send,
     recv,
 ):
@@ -470,7 +498,7 @@
     width = columns - LANES
     local_rows = values_ref.shape[0]
     slots = keys_ref.shape[1]
-    his = spread.shape[1]
+    his = spread.shape[0]
     low_rows = local_rows // his
     low, high = pl.ds(0, rows // 2), pl.ds(rows // 2, rows // 2)
     enter(plane_peers())
@@ -595,13 +623,6 @@
         14: [lambda: corner_sum(2)],
     }
 
-    def spread_copy(i, buffer):
-        return pltpu.make_async_copy(
-            spread.at[buffer],
-            spread_ref.at[:, pl.ds(pl.multiple_of(i * 2 * rows, 2 * rows), 2 * rows), :],
-            spread_sem.at[buffer],
-        )
-
     def step(i, _):
         for when, todo in tasks.items():
 
@@ -611,15 +632,10 @@
                     task()
 
         copy(0, i, sent.at[i, core], sent.at[i, 1 - core], to_s).wait_recv()
-        pltpu.make_async_copy(sent.at[i], sent_ref.at[i], sent_sem.at[i]).start()
-        buffer = i % 2
-        pl.when(i >= 2)(lambda: spread_copy(i - 2, buffer).wait())
         k, j = i // 4, i % 4
         grp = (g // 2 + j // 2) % 2 * 2 + (g % 2 + j % 2) % 2
         base = grp * 8 + (z + 4 - k) % 4 * 2
-        local = picks_ref[pl.ds(pl.multiple_of(base * rows, 2 * rows), 2 * rows), :]
-        local = local - (g * 8 + m) * local_rows
-        lane, tile = local % LANES, local // LANES
+        lanes, tiles = [], []
         for c in range(2):
             key = keys_ref[pl.ds(base + c, 1), :]
             flat = key & ((1 << flat_bits) - 1)
@@ -629,6 +645,16 @@
             block = jnp.where(dummy, -1, (row // low_rows) * rows + token)
             is_token = iota((rows, slots), 0) == token
             is_pick = iota((LANES, slots), 0) == flat % LANES
+            place = jnp.concatenate(
+                [
+                    jnp.where(is_token, (row % LANES).astype(F32), 0.0).astype(BF),
+                    jnp.where(is_token, (row // LANES + 1).astype(F32), 0.0).astype(BF),
+                ],
+                axis=0,
+            )
+            place = dot(place, is_pick.astype(F32).astype(BF), NT).astype(jnp.int32)
+            lanes.append(place[:rows])
+            tiles.append(place[rows:] - 1)
             weights = sent[i, c, :, width:]
             found = dot(weights, is_token.astype(F32).astype(BF), TN)
             weight = jnp.sum(jnp.where(is_pick, found, 0.0), axis=0, keepdims=True)
@@ -638,13 +664,15 @@
                 jnp.where(is_block, weight, 0.0).astype(BF), is_low.astype(F32).astype(BF), NT
             ).astype(BF)
             for h in range(his):
-                spread[buffer, h, c * rows : (c + 1) * rows, :] = piece[h * rows : (h + 1) * rows]
+                spread[h, 2 * i + c] = piece[h * rows : (h + 1) * rows]
+        lane, tile = jnp.concatenate(lanes, axis=0), jnp.concatenate(tiles, axis=0)
         grads = sent[i, :, :, :width].reshape(2 * rows, width)
         total = jnp.zeros((2 * rows, width), F32)
         picked = jnp.zeros((2 * rows, LANES), F32)
         for h in range(his):
             table = values_ref[h * low_rows : (h + 1) * low_rows, :]
-            total = total + dot(spread[buffer, h], table)
+            piece = spread[h, pl.ds(2 * i, 2)].reshape(2 * rows, low_rows)
+            total = total + dot(piece, table)
             products = dot(grads, table, NT)
             for b in range(low_rows // LANES):
                 found = jnp.take_along_axis(
@@ -654,14 +682,33 @@
         parts[i, :, :, :width] = total.astype(BF).reshape(2, rows, width)
         parts[i, :, :, width:] = picked.astype(BF).reshape(2, rows, LANES)
         part_sibling(i).start()
-        spread_copy(i, buffer).start()
         return 0
+
+    def table_copy(h):
+        return pltpu.make_async_copy(table.at[h % 2], grad_ref.at[h], table_sem.at[h % 2])
+
+    def table_grad(h):
+        if h >= 2:
+            table_copy(h - 2).wait()
+
+        def some(n, _):
+            grads = sent[pl.ds(4 * n, 4), :, :, :width].reshape(8 * rows, width)
+            piece = spread[h, pl.ds(8 * n, 8)].reshape(8 * rows, low_rows)
+            table[h % 2] = jnp.where(n == 0, 0.0, table[h % 2]) + dot(piece, grads, TN)
+            return 0
+
+        lax.fori_loop(0, 4, some, 0)
+        table_copy(h).start()
 
     lax.fori_loop(0, 16, step, 0)
     plane_sum(2)
     pair_sum(3)
+    table_grad(0)
     corner_sum(3)
+    table_grad(1)
     plane_sum(3)
+    table_grad(2)
+    table_grad(3)
     total = held[...]
     for k in (1, 2, 3):
         three(k).wait_recv()
@@ -676,13 +723,11 @@
             todo += [to_sibling(4 * k + j), part_sibling(4 * k + j)]
         for item in todo:
             item.wait_send()
-    for i in (14, 15):
-        spread_copy(i, i % 2).wait()
-    for i in range(16):
-        pltpu.make_async_copy(sent.at[i], sent_ref.at[i], sent_sem.at[i]).wait()
-
-
-def memory_call(payload, keys, picks, values, flat_bits):
+    table_copy(2).wait()
+    table_copy(3).wait()
+
+
+def memory_call(payload, keys, values, flat_bits):
     rows, columns = payload.shape
     local_rows = values.shape[0]
     his = 4
@@ -692,12 +737,11 @@
     hbm = pl.BlockSpec(memory_space=pl.ANY)
     return pl.pallas_call(
         functools.partial(memory_kernel, flat_bits),
-        in_specs=[hbm, vmem, vmem, vmem],
-        out_specs=[vmem, hbm, hbm],
+        in_specs=[hbm, vmem, vmem],
+        out_specs=[vmem, hbm],
         out_shape=[
             jax.ShapeDtypeStruct((rows, columns), F32),
-            jax.ShapeDtypeStruct((his, 32 * rows, local_rows // his), BF),
-            jax.ShapeDtypeStruct((16, 2, rows, columns), BF),
+            jax.ShapeDtypeStruct((his, local_rows // his, columns - LANES), F32),
         ],
         scratch_shapes=[
             pltpu.VMEM((16, 2, rows, columns), BF),
@@ -709,18 +753,18 @@
             pltpu.VMEM(full, BF),
             pltpu.VMEM((3, rows, columns), BF),
             pltpu.VMEM((rows, columns), F32),
-            pltpu.VMEM((2, his, 2 * rows, local_rows // his), BF),
+            pltpu.VMEM((his, 32, rows, local_rows // his), BF),
+            pltpu.VMEM((2, local_rows // his, columns - LANES), F32),
             pltpu.SemaphoreType.DMA,
             pltpu.SemaphoreType.DMA((2,)),
-            pltpu.SemaphoreType.DMA((16,)),
             pltpu.SemaphoreType.DMA((12, 16)),
             pltpu.SemaphoreType.DMA((12, 16)),
         ],
         compiler_params=pltpu.CompilerParams(
-            collective_id=1, has_side_effects=True, vmem_limit_bytes=60 * 1024 * 1024
+            collective_id=1, has_side_effects=True, vmem_limit_bytes=63 * 1024 * 1024
         ),
         name="memory",
-    )(payload, keys, picks, values)
+    )(payload, keys, values)
 
 
 def gather_kernel(pieces, count, *refs):
@@ -892,72 +936,65 @@
 WIDTH = HEADS * HDIM
 KEYS = MHEADS * 2 * NK
 QUERIES = MHEADS * 2 * HALF
-F_MIXED, F_SECOND, F_ATTENDED, F_FIRST, F_COT, F_GATE, F_RESID = (i * WIDTH for i in range(7))
-F_HALF = 7 * WIDTH
-F_QKV = F_HALF + KEYS
-F_QUERY = F_QKV + 3 * WIDTH
-F_ALL = F_QUERY + QUERIES
-G_OUT, G_GATE, G_PROJ, G_HALF = 0, WIDTH, 2 * WIDTH, 3 * WIDTH
-G_QKV = G_HALF + KEYS
-G_KEYS = G_QKV + 3 * WIDTH
-G_GAIN = G_KEYS + 2 * HALF
-G_ALL = G_GAIN + LANES
-PRODUCTS = (
-    (F_MIXED, F_COT, WIDTH, G_OUT),
-    (F_SECOND, F_GATE, WIDTH, G_GATE),
-    (F_ATTENDED, F_RESID, WIDTH, G_PROJ),
-    (F_SECOND, F_HALF, KEYS, G_HALF),
-    (F_FIRST, F_QKV, 3 * WIDTH, G_QKV),
+EARLY = (WIDTH,) * 6 + (KEYS, QUERIES)
+EARLY_PRODUCTS = (
+    (0, 3 * WIDTH, WIDTH, 0),
+    (WIDTH, 4 * WIDTH, WIDTH, WIDTH),
+    (2 * WIDTH, 5 * WIDTH, WIDTH, 2 * WIDTH),
+    (WIDTH, 6 * WIDTH, KEYS, 3 * WIDTH),
 )
-
-
-def grads_kernel(
-    fact_ref, gain_ref, out_ref, fact, gains, held, x1, y1, x2, y2, zin, quarter, local_sem, send, recv
-):
-    g, m, across, along, sibling = places()
-    core, z = m % 2, m // 2
-    rows = fact_ref.shape[0]
-    enter(plane_peers())
+E_OUT, E_GATE, E_PROJ, E_HALF = 0, WIDTH, 2 * WIDTH, 3 * WIDTH
+E_KEYS = E_HALF + KEYS
+E_ALL = E_KEYS + 2 * HALF
+LATE = (WIDTH, 3 * WIDTH)
+LATE_PRODUCTS = ((0, WIDTH, 3 * WIDTH, 0),)
+L_GAIN = 3 * WIDTH
+L_ALL = L_GAIN + LANES
+
+
+def share_factors(moves, local_sem, send, recv):
+    g, _, _, _, sibling = places()
     copies = []
-    for i, (src, dst, count) in enumerate(((fact_ref, fact, rows), (gain_ref, gains, 16))):
-        near = pltpu.make_async_copy(src, dst.at[pl.ds(0, count)], local_sem.at[i])
+    for i, (src, dst, at, columns) in enumerate(moves):
+        count = src.shape[0]
+        where = pl.ds(at, columns)
+        far = push(
+            src, dst.at[pl.ds(count, count), where], send.at[5, i], recv.at[5, i], (g, sibling)
+        )
+        near = pltpu.make_async_copy(src, dst.at[pl.ds(0, count), where], local_sem.at[i])
         near.start()
-        far = push(
-            src, dst.at[pl.ds(count, count)], send.at[5, i], recv.at[5, i], (g, sibling)
-        )
         copies.append((near, far))
-    for near, far in copies:
-        near.wait()
-        far.wait_recv()
-    row = iota((32, LANES), 0) % 16
-    column = iota((32, LANES), 1)
-    select = ((row < 4) & (row // 2 == column)).astype(F32).astype(BF)
-    chunk = WIDTH
-
-    def ready(k):
-        block = (z + 3 - k) % 4 * 2 + core
-
-        def store(value, at):
-            for i in range(4):
-                held[k, i, :, at : at + value.shape[1]] = value[i * 32 : (i + 1) * 32].astype(BF)
-
-        for left, right, count, at in PRODUCTS:
-            lhs = fact[:, pl.ds(pl.multiple_of(left + block * LANES, LANES), LANES)]
-            for j in range(0, count, chunk):
-                store(dot(lhs, fact[:, right + j : right + j + chunk], TN), at + j)
-        lhs = fact[:, pl.ds(pl.multiple_of(F_HALF + block * NK, LANES), NK)]
-        rhs = fact[:, pl.ds(pl.multiple_of(F_QUERY + block * HALF, LANES), HALF)]
-        value = dot(lhs, rhs, TN)
-        for i in range(4):
-            for h in range(2):
-                first = i * 64 + h * 32
-                held[k, i, :, G_KEYS + h * HALF : G_KEYS + (h + 1) * HALF] = value[
-                    first : first + 32
-                ].astype(BF)
-        lhs = gains[:, pl.ds(pl.multiple_of(block * LANES, LANES), LANES)]
-        store(dot(lhs, select, TN), G_GAIN)
-
-    total = reduce_planes(held, ready, x1, y1, x2, y2, zin, send, recv)
+    return copies
+
+
+def factor_moves(refs, widths, fact):
+    moves, at = [], 0
+    for ref, columns in zip(refs, widths, strict=True):
+        moves.append((ref, fact, at, columns))
+        at += columns
+    return moves
+
+
+def store_blocks(held, k, value, at):
+    for i in range(4):
+        held[k, i, :, at : at + value.shape[1]] = value[i * 32 : (i + 1) * 32].astype(BF)
+
+
+def block_of(k):
+    m = lax.axis_index("mem")
+    return (m // 2 + 3 - k) % 4 * 2 + m % 2
+
+
+def products_of(k, fact, held, products):
+    block = block_of(k)
+    for left, right, count, at in products:
+        lhs = fact[:, pl.ds(pl.multiple_of(left + block * LANES, LANES), LANES)]
+        for j in range(0, count, WIDTH):
+            store_blocks(held, k, dot(lhs, fact[:, right + j : right + j + WIDTH], TN), at + j)
+
+
+def spread_quarters(total, quarter, send, recv):
+    g, m, across, along, _ = places()
     quarter[g] = total.astype(BF)
     to_x, to_y = (across, m), (along, m)
     low, high = pl.ds(0, 16), pl.ds(16, 16)
@@ -971,33 +1008,231 @@
     d.wait_recv()
     for copy in (a, b, c, d):
         copy.wait_send()
+
+
+def late_kernel(
+    first_ref, rows_ref, gain_ref, out_ref, fact, gains, held, x1, y1, x2, y2, zin, quarter, *sems
+):
+    local_sem, send, recv = sems
+    enter(plane_peers())
+    moves = factor_moves((first_ref, rows_ref), LATE, fact)
+    copies = share_factors([*moves, (gain_ref, gains, 0, WIDTH)], local_sem, send, recv)
+    first, corner, plane, last = plane_tasks(held, x1, y1, x2, y2, zin, send, recv)
+    for near, far in copies:
+        near.wait()
+        far.wait_recv()
+    row = iota((32, LANES), 0) % 16
+    column = iota((32, LANES), 1)
+    select = ((row < 4) & (row // 2 == column)).astype(F32).astype(BF)
+    for k in range(4):
+        products_of(k, fact, held, LATE_PRODUCTS)
+        lhs = gains[:, pl.ds(pl.multiple_of(block_of(k) * LANES, LANES), LANES)]
+        store_blocks(held, k, dot(lhs, select, TN), L_GAIN)
+        first(k)
+    for k in range(4):
+        corner(k)
+    for k in range(4):
+        plane(k)
+    spread_quarters(last(), quarter, send, recv)
     for _, far in copies:
         far.wait_send()
     out_ref[...] = quarter[...]
 
 
-def reduce_grads(factors, gains):
-    rows = factors.shape[0]
+def reduce_late(first, qkv_rows, gains):
+    rows = first.shape[0]
     return pl.pallas_call(
-        grads_kernel,
-        in_specs=[pl.BlockSpec(memory_space=pl.ANY)] * 2,
+        late_kernel,
+        in_specs=[pl.BlockSpec(memory_space=pl.ANY)] * 3,
         out_specs=pl.BlockSpec(memory_space=pltpu.VMEM),
-        out_shape=jax.ShapeDtypeStruct((4, 32, G_ALL), BF),
+        out_shape=jax.ShapeDtypeStruct((4, 32, L_ALL), BF),
         scratch_shapes=[
-            pltpu.VMEM((2 * rows, F_ALL), BF),
+            pltpu.VMEM((2 * rows, sum(LATE)), BF),
             pltpu.VMEM((32, WIDTH), BF),
-            pltpu.VMEM((4, 4, 32, G_ALL), BF),
-            *plane_scratch(32, G_ALL),
-            pltpu.VMEM((4, 32, G_ALL), BF),
-            pltpu.SemaphoreType.DMA((2,)),
+            pltpu.VMEM((4, 4, 32, L_ALL), BF),
+            *plane_scratch(32, L_ALL),
+            pltpu.VMEM((4, 32, L_ALL), BF),
+            pltpu.SemaphoreType.DMA((3,)),
             pltpu.SemaphoreType.DMA((7, 4)),
             pltpu.SemaphoreType.DMA((7, 4)),
         ],
         compiler_params=pltpu.CompilerParams(
-            collective_id=2, has_side_effects=True, vmem_limit_bytes=56 * 1024 * 1024
+            collective_id=2, has_side_effects=True, vmem_limit_bytes=40 * 1024 * 1024
         ),
-        name="reduce_grads",
-    )(factors, gains).reshape(4 * 32, G_ALL)
+        name="reduce_late",
+    )(first, qkv_rows, gains).reshape(4 * 32, L_ALL)
+
+
+def back_kernel(rows, win, *refs):
+    fact_refs, refs = refs[: len(EARLY)], refs[len(EARLY) :]
+    shared_ref, qkv_ref, proj_ref, segc_ref, segr_ref, out_ref, rows_ref = refs[:7]
+    fact, held, x1, y1, x2, y2, zin, quarter, shared, douts, stats = refs[7:18]
+    local_sem, send, recv = refs[18:]
+    g, m, _, _, sibling = places()
+    to_s = (g, sibling)
+    pairs = WIDTH // LANES
+    enter(plane_peers())
+
+    def part(owner):
+        return shared.at[pl.ds(pl.multiple_of(owner * rows, LANES), rows)]
+
+    def move(index, src, owner, peer):
+        return pltpu.make_async_remote_copy(
+            src_ref=src,
+            dst_ref=part(owner),
+            send_sem=send.at[7, index],
+            recv_sem=recv.at[7, index],
+            device_id=peer,
+            device_id_type=MESH,
+        )
+
+    def origin(d):
+        return (m + 8 - 2 * d) % 8
+
+    lines = [move(d, shared_ref, m, (g, (m + 2 * d) % 8)) for d in (1, 2, 3)]
+    side = move(0, shared_ref, m, to_s)
+    forward = [move(3 + d, part(origin(d)), origin(d), to_s) for d in (1, 2, 3)]
+    own = pltpu.make_async_copy(shared_ref, part(m), local_sem.at[len(EARLY)])
+    for copy in lines:
+        copy.start()
+    side.start()
+    own.start()
+    copies = share_factors(factor_moves(fact_refs, EARLY, fact), local_sem, send, recv)
+    first, corner, plane, last = plane_tasks(held, x1, y1, x2, y2, zin, send, recv)
+    for near, far in copies:
+        near.wait()
+        far.wait_recv()
+    for k in range(4):
+        products_of(k, fact, held, EARLY_PRODUCTS)
+        block = block_of(k)
+        lhs = fact[:, pl.ds(pl.multiple_of(6 * WIDTH + block * NK, LANES), NK)]
+        at = 6 * WIDTH + KEYS
+        rhs = fact[:, pl.ds(pl.multiple_of(at + block * HALF, LANES), HALF)]
+        value = dot(lhs, rhs, TN)
+        for i in range(4):
+            for h in range(2):
+                row = i * 64 + h * 32
+                held[k, i, :, E_KEYS + h * HALF : E_KEYS + (h + 1) * HALF] = value[
+                    row : row + 32
+                ].astype(BF)
+        first(k)
+    corner(0)
+    for copy, after in zip(lines, forward, strict=True):
+        copy.wait_recv()
+        after.start()
+    corner(1)
+    own.wait()
+    side.wait_recv()
+    for copy in forward:
+        copy.wait_recv()
+    corner(2)
+    for i in range(0, shared.shape[0], 2 * rows):
+        where = slice(i, i + 2 * rows)
+        douts[where, :] = dot(shared[where, :WIDTH], proj_ref[...], NT).astype(BF)
+        stats[where, :] = shared[where, WIDTH : WIDTH + 2 * HEADS].astype(F32) + shared[
+            where, WIDTH + 2 * HEADS : WIDTH + 4 * HEADS
+        ].astype(F32)
+    corner(3)
+
+    def load_of(pair):
+        def load(which, where):
+            ref, base = (douts, 0) if which == 3 else (qkv_ref, which * pairs)
+            return ref[where, pl.ds(pl.multiple_of((base + pair) * LANES, LANES), LANES)]
+
+        return load
+
+    def attend(pair, _):
+        grads = attn_bwd_pair(
+            rows, win, pair, m, shared.shape[0], load_of(pair), stats, segc_ref, segr_ref
+        )
+        for i, value in enumerate(grads):
+            column = pl.multiple_of((i * pairs + pair) * LANES, LANES)
+            rows_ref[:, pl.ds(column, LANES)] = value
+        return 0
+
+    for k in range(4):
+        lax.fori_loop(2 * k, 2 * k + 2, attend, 0)
+        plane(k)
+    spread_quarters(last(), quarter, send, recv)
+    for _, far in copies:
+        far.wait_send()
+    for copy in [*lines, side, *forward]:
+        copy.wait_send()
+    out_ref[...] = quarter[...]
+
+
+def reduce_back(factors, shared, qkv, proj, seg_col, seg_row):
+    rows = factors[0].shape[0]
+    group_len = qkv.shape[0]
+    win = min(group_len, group_len // 2 + rows)
+    hbm = pl.BlockSpec(memory_space=pl.ANY)
+    vmem = pl.BlockSpec(memory_space=pltpu.VMEM)
+    count = len(EARLY)
+    sums, qkv_rows = pl.pallas_call(
+        functools.partial(back_kernel, rows, win),
+        in_specs=[hbm] * (count + 1) + [vmem] * 4,
+        out_specs=[vmem, vmem],
+        out_shape=[
+            jax.ShapeDtypeStruct((4, 32, E_ALL), BF),
+            jax.ShapeDtypeStruct((rows, 3 * WIDTH), BF),
+        ],
+        scratch_shapes=[
+            pltpu.VMEM((2 * rows, sum(EARLY)), BF),
+            pltpu.VMEM((4, 4, 32, E_ALL), BF),
+            *plane_scratch(32, E_ALL),
+            pltpu.VMEM((4, 32, E_ALL), BF),
+            pltpu.VMEM((group_len, WIDTH + LANES), BF),
+            pltpu.VMEM((group_len, WIDTH), BF),
+            pltpu.VMEM((group_len, 2 * HEADS), F32),
+            pltpu.SemaphoreType.DMA((count + 1,)),
+            pltpu.SemaphoreType.DMA((8, count)),
+            pltpu.SemaphoreType.DMA((8, count)),
+        ],
+        compiler_params=pltpu.CompilerParams(
+            collective_id=4, has_side_effects=True, vmem_limit_bytes=56 * 1024 * 1024
+        ),
+        name="reduce_back",
+    )(*factors, shared, qkv, proj, seg_col, seg_row)
+    return sums.reshape(4 * 32, E_ALL), qkv_rows
+
+
+def finish_kernel(
+    early_ref, late_ref, keys_ref, table_ref, out, gate, proj, qkv, query, half, gains, whole, sem
+):
+    copy = pltpu.make_async_copy(table_ref, whole, sem)
+    copy.start()
+    for ref, first in ((out, E_OUT), (gate, E_GATE), (proj, E_PROJ)):
+        ref[...] = early_ref[:, first : first + WIDTH].astype(F32)
+    qkv[...] = late_ref[:, : 3 * WIDTH].astype(F32)
+    for c in range(MHEADS * 2):
+        table = keys_ref[c * NK : (c + 1) * NK, :]
+        query[:, c * HALF : (c + 1) * HALF] = dot(
+            early_ref[:, E_HALF + c * NK : E_HALF + (c + 1) * NK], table
+        )
+    for i in range(4):
+        for h in range(2):
+            first = i * 64 + h * 32
+            half[first : first + 32, :] = early_ref[
+                i * 32 : (i + 1) * 32, E_KEYS + h * HALF : E_KEYS + (h + 1) * HALF
+            ].astype(F32)
+    gains[...] = late_ref[:, L_GAIN:].astype(F32).T[:8]
+    copy.wait()
+
+
+def finish(early, late, keys, table):
+    rows = early.shape[0]
+    shapes = [(rows, WIDTH)] * 3 + [(rows, 3 * WIDTH), (rows, QUERIES), (2 * rows, HALF)]
+    shapes.append((8, LANES))
+    vmem, hbm = pl.BlockSpec(memory_space=pltpu.VMEM), pl.BlockSpec(memory_space=pl.ANY)
+    return pl.pallas_call(
+        finish_kernel,
+        in_specs=[vmem, vmem, vmem, hbm],
+        out_specs=[vmem] * len(shapes) + [hbm],
+        out_shape=[jax.ShapeDtypeStruct(shape, F32) for shape in [*shapes, table.shape]],
+        scratch_shapes=[pltpu.SemaphoreType.DMA],
+        compiler_params=pltpu.CompilerParams(vmem_limit_bytes=40 * 1024 * 1024),
+        name="finish",
+    )(early, late, keys, table)
 
 
 def rms_scale(values):
@@ -1042,7 +1277,6 @@
 
     flat_picks = picks.reshape(rows, MHEADS * TOPK)
     if linked:
-        picks_all = gather(flat_picks, ALL)
         gain_block = jnp.concatenate(
             [attn_gain[None], mem_gain[None], jnp.zeros((14, LANES), BF)]
         )
@@ -1112,16 +1346,16 @@
 
     payload = jnp.concatenate([memory_grad, weights_low], axis=1)
     if linked:
-        back, spread, sent = memory_call(payload, arrived, picks_all, memory_values, flat_bits)
-        sent = sent.reshape(owners * rows, width + LANES)
+        back, values_grad = memory_call(payload, arrived, memory_values, flat_bits)
     else:
         sent = gather(payload, ALL)
         part, spread = owner_call(arrived, sent, memory_values, flat_bits)
         back = lax.psum_scatter(part, "grp", scatter_dimension=0, tiled=True)
         back = lax.psum_scatter(back, "mem", scatter_dimension=0, tiled=True)
-    values_grad = jnp.einsum(
-        "hkl,kd->hld", spread, sent[:, :width], preferred_element_type=F32
-    ).reshape(local_rows, width)
+        values_grad = jnp.einsum(
+            "hkl,kd->hld", spread, sent[:, :width], preferred_element_type=F32
+        )
+    values_grad = values_grad.reshape(local_rows, width)
 
     memory_out = back[:, :width].astype(F32)
     weight_grad = back[:, width:].astype(F32)
@@ -1140,28 +1374,44 @@
     resid_grad = out_cotangent.astype(F32) + resid_from_norm
     resid_low = resid_grad.astype(BF)
     attn_grad = dot(resid_low, proj_full, NT).astype(BF)
-    delta = jnp.sum(
-        (attn_grad.astype(F32) * attn_sum).reshape(rows, HEADS, HDIM), axis=-1
+    heads = (iota((width, HEADS), 0) // HDIM == iota((width, HEADS), 1)).astype(F32)
+    delta = jnp.dot(
+        attn_grad.astype(F32) * attn_sum,
+        heads,
+        precision=lax.Precision.HIGHEST,
+        preferred_element_type=F32,
     )
     stats = jnp.concatenate([lse[:, :HEADS], delta], axis=1)
     stats_high = lax.reduce_precision(stats, 8, 7)
     stats_low = stats - stats_high
-    shared = gather(
-        jnp.concatenate(
-            [
-                resid_low,
-                stats_high.astype(BF),
-                stats_low.astype(BF),
-                jnp.zeros((rows, LANES - 4 * HEADS), BF),
-            ],
-            axis=1,
-        )
+    shared = jnp.concatenate(
+        [
+            resid_low,
+            stats_high.astype(BF),
+            stats_low.astype(BF),
+            jnp.zeros((rows, LANES - 4 * HEADS), BF),
+        ],
+        axis=1,
     )
-    stats_all = shared[:, width : width + 2 * HEADS].astype(F32) + shared[
-        :, width + 2 * HEADS : width + 4 * HEADS
-    ].astype(F32)
-    attn_grad_all = dot(shared[:, :width], proj_full, NT).astype(BF)
-    qkv_rows = attn_bwd(pos, qkv_all, attn_grad_all, stats_all, seg_row, seg_col, rows)
+    if linked:
+        early = (
+            mixed,
+            second,
+            attended,
+            out_cotangent,
+            gate_grad,
+            resid_low,
+            half_grad,
+            mem_query,
+        )
+        early, qkv_rows = reduce_back(early, shared, qkv_all, proj_full, seg_col, seg_row)
+    else:
+        shared = gather(shared)
+        stats_all = shared[:, width : width + 2 * HEADS].astype(F32) + shared[
+            :, width + 2 * HEADS : width + 4 * HEADS
+        ].astype(F32)
+        attn_grad_all = dot(shared[:, :width], proj_full, NT).astype(BF)
+        qkv_rows = attn_bwd(pos, qkv_all, attn_grad_all, stats_all, seg_row, seg_col, rows)
     scale_one = rms_scale(inputs)
     first_low = (inputs * scale_one * gain_one).astype(BF)
     first_grad = dot(qkv_rows, qkv_full, NT)
@@ -1169,43 +1419,21 @@
     tokens_grad = resid_grad + input_from_norm
 
     if linked:
-        factors = jnp.concatenate(
-            [
-                mixed,
-                second,
-                attended,
-                first_low,
-                out_cotangent,
-                gate_grad,
-                resid_low,
-                half_grad,
-                qkv_rows,
-                mem_query,
-            ],
-            axis=1,
-        )
         sums = jnp.stack([gain_one_grad, gain_two_grad])
         sums_high = lax.reduce_precision(sums, 8, 7)
         gain_rows = jnp.stack([sums_high, sums - sums_high], axis=1).reshape(4, width)
         gain_rows = jnp.concatenate([gain_rows.astype(BF), jnp.zeros((12, width), BF)])
-        reduced = reduce_grads(factors, gain_rows).astype(F32)
-        out_share = reduced[:, G_OUT : G_OUT + width]
-        gate_share = reduced[:, G_GATE : G_GATE + width]
-        proj_share = reduced[:, G_PROJ : G_PROJ + width]
-        qkv_share = reduced[:, G_QKV : G_QKV + 3 * width]
-        keys_share = (
-            reduced[:, G_KEYS : G_KEYS + 2 * HALF]
-            .reshape(4, 32, 2, HALF)
-            .transpose(0, 2, 1, 3)
-            .reshape(half_keys.shape)
-        )
-        query_share = jnp.einsum(
-            "rcn,cnf->rcf",
-            reduced[:, G_HALF : G_HALF + KEYS].astype(BF).reshape(rows, MHEADS * 2, NK),
-            key_table,
-            preferred_element_type=F32,
-        ).reshape(rows, QUERIES)
-        gain_sums = reduced[:, G_GAIN : G_GAIN + 2].T
+        late = reduce_late(first_low, qkv_rows, gain_rows)
+        (
+            out_share,
+            gate_share,
+            proj_share,
+            qkv_share,
+            query_share,
+            keys_share,
+            gain_sums,
+            values_grad,
+        ) = finish(early, late, keys_full, values_grad)
     else:
         keys_grad = jnp.einsum(
             "tcn,tcf->cnf",

time: 572 us -> 490 us (0.86)
  matrix products: 75.9 us -> 37.9 us
  local copies, waits for them, and re-layouts: 31.9 us -> 15.1 us
  between operations: 14.7 us -> 1.64 us
  other arithmetic: 31.6 us -> 19.9 us
  starting transfers between devices: 17.4 us -> 7.3 us
  Pallas kernels: 394 us -> 402 us
    dot_general x2 -> x1, matrix products: 27.6 us -> 0.76 us  [per_device(): jnp.dot(attn_grad.astype(F32) * attn_sum, heads, precision=lax.Precision....]
    dot_general x11 -> x10, matrix products: 44.8 us -> 34.6 us  [dot(): lax.dot_general(left, right, (dims, ((), ())), preferred_element_type=F32)]
    all_gather x2 -> x0, starting transfers between devices: 10.1 us -> none  [gather(): return lax.all_gather(x, axes, axis=0, tiled=True)]
    unnamed x6 -> x0, other arithmetic: 6.38 us -> none
    pallas_call x3 -> x4, Pallas kernels: 152 us -> 158 us  [the longest x1 92.6 us: reduce_back(): pl.pallas_call(functools.partial(back_kernel, rows, win), in_specs=[hbm]...]
    unnamed x65 -> x62, local copies, waits for them, and re-layouts: 12.8 us -> 8.68 us
  transfers between devices with their start and end apart: 3 -> 1, of which waited for: 1 -> 0; matrix products, arithmetic and copies ran while one was open for 11% -> 6% of each run, Pallas kernels for 21% -> 25%
where the time goes in v5:
time: 490 us; the launch traced here: 484 us
  Pallas kernels  402 us (82%)
  matrix products  37.9 us (8%)
  other arithmetic  19.9 us (4%)
  local copies, waits for them, and re-layouts  15.1 us (3%)
  starting transfers between devices  7.3 us (1%)
    pallas_call x1, Pallas kernels, memory_call(): pl.pallas_call(functools.partial(memory_kernel, flat_bits), in_specs=[hbm...  124 us
    pallas_call x1, Pallas kernels, gather_weights(): pl.pallas_call(functools.partial(gather_kernel, tuple(pieces), count), in...  107 us
    pallas_call x1, Pallas kernels, reduce_back(): pl.pallas_call(functools.partial(back_kernel, rows, win), in_specs=[hbm]...  92.6 us
    pallas_call x1, Pallas kernels, reduce_late(): pl.pallas_call(late_kernel, in_specs=[pl.BlockSpec(memory_space=pl.ANY)]...  52.1 us
    dot_general x10, matrix products, dot(): lax.dot_general(left, right, (dims, ((), ())), preferred_element_type=F32)  34.6 us
    pallas_call x1, Pallas kernels, attn_fwd(): pl.pallas_call(functools.partial(attn_fwd_kernel, rows, win), grid_spec=p...  10.2 us
  transfers between devices with their start and end apart: 1, of which 0 were waited for; matrix products, arithmetic and copies ran while one was open for 6% of the time, Pallas kernels for 25%

profile of v5, /device:TPU:0, one launch (start us, length us, event | category | flops | bytes accessed | tf_op | source)
XLA Modules:
  0.0 483.8 jit_solution(656827278437085816)
XLA Ops:
  0.6 0.0 copy-start.10
  0.7 1.0 copy.75
  1.7 0.2 reshape.294
  1.9 0.3 convert_reduce_fusion.1
  2.2 0.1 copy.76
  2.3 0.1 reduce-window.8
  2.4 0.1 reduce
  2.5 0.4 convert_reduce_fusion
  3.0 8.0 %sort.7 = s32[32768]{0:T(1024)} sort(s32[32768]{0:T(1024)S(1)} %pad_add_fusion), dimensions={0}, to_apply=%region_5.6 | sort | flops 491520 | bytes 262144 | tf_op jit(solution)/shard_map/sort | solution.py:376
  10.9 7.3 %all-to-all-start = ((s32[32,1,1024]{2,1,0:T(1,128)}), s32[32,1,1024]{2,1,0:T(1,128)S(1)}, u32[]{:S(2)}, u32[]{:S(2)}) async-start(s32[32,1,1024]{2,1,0:T(1,128)} %bitcast.15), calls=%async_computation | async-start | bytes 262144 | tf_op jit(solution)/shard_map/all_to_all | solution.py:1320
  18.2 0.1 fusion.12
  18.4 0.1 pad.13.clone
  18.5 0.7 maximum_maximum_fusion.refs_1_
  19.1 106.9 %gather_weights.1 = (bf16[1024,1024]{1,0:T(8,128)(2,1)}, bf16[128,128]{1,0:T(8,128)(2,1)}, bf16[1024,3072]{1,0:T(8,128)(2,1)}, bf16[1024,1024]{1,0:T(8,128)(2,1)...) custom-call(bf16[128,1024]{1,0:T(8,128)(2,1)} %refs_0_.1, ...), custom_call_target="tpu_custom_call" | custom-call | tf_op jit(solution)/shard_map/gather_weights/pallas_call | solution.py:921
  126.0 0.9 convert_bitcast_fusion
  126.9 2.1 fusion
  129.0 1.0 copy.70.qseg_ref.refs_11_
  130.0 11.6 %convolution_convert_fusion.q_ref.k_ref.v_ref.refs_9_ = bf16[1024,3072]{1,0:T(8,128)(2,1)} fusion(bf16[1024,3072]{1,0:T(8,128)(2,1)} %get-tuple-element.37, bf16[1024,1024]{1,0:T(8,128)(2,1)S(1)} %copy-done.22, f32[1024]{0:T(1024)S(1)} %bitcast.82, f32[1024]{0:T(1024)S(1)} %add_rsqrt_fusion), kind=kOutput, calls=%fused_computation | convolution fusion | flops 6449790976 | bytes 14688256 | tf_op jit(solution)/shard_map/dot_general | solution.py:25
  141.6 10.2 %attn_fwd.1 = (f32[128,1024]{1,0:T(8,128)}, f32[128,128]{1,0:T(8,128)}) custom-call(s32[1]{0:T(128)} %bitcast.pos_ref, bf16[1024,3072]{1,0:T(8,128)(2,1)} %convolution_convert_fusion.q_ref.k_ref.v_ref.refs_9_, bf16[1024,3072]{1,0:T(8,128)(2,1)} %convolution_convert_fusion.q_ref.k_ref.v_ref.refs_9_, ...), custom_call_target="tpu_custom_call" | custom-call | flops 335544320 | bytes 4194304 | tf_op jit(solution)/shard_map/attn_fwd/pallas_call | solution.py:76
  151.9 1.1 convert_element_type.84.refs_2_
  153.0 0.5 multiply_reduce_fusion.2
  153.5 0.1 multiply_convert_fusion.3.refs_1_
  153.7 1.0 copy-done.8
  154.6 0.4 fusion.38
  155.1 0.0 copy-start.24
  155.1 4.9 %convolution_convert_fusion.1.refs_7_ = bf16[128,4096]{1,0:T(8,128)(2,1)S(1)} fusion(bf16[128,1024]{1,0:T(8,128)(2,1)S(1)} %multiply_convert_fusion.3.refs_1_, bf16[1024,4096]{1,0:T(8,128)(2,1)} %get-tuple-element.43), kind=kOutput, calls=%fused_computation.3 | convolution fusion | flops 1074266112 | bytes 9699328 | tf_op jit(solution)/shard_map/dot_general | solution.py:25
  160.0 0.0 copy-start.7
  160.0 0.0 copy-start.15
  160.1 0.7 fusion.9
  160.8 0.2 copy-done.7
  161.0 0.2 copy-done.15
  161.2 0.9 copy-done.20
  162.1 1.6 multiply_convert_fusion.2
  163.7 1.3 copy.85.scores_ref
  165.1 0.7 copy.74.picks_ref
  165.8 2.9 pick_fwd.1
  168.7 1.5 pad_maximum_fusion.payload_ref
  170.2 0.7 copy.98
  170.9 124.2 %memory.1 = (f32[128,1152]{1,0:T(8,128)}, f32[4,512,1024]{2,1,0:T(8,128)}) custom-call(bf16[128,1152]{1,0:T(8,128)(2,1)} %pad_maximum_fusion.payload_ref, s32[32,1024]{1,0:T(8,128)} %bitcast.75, bf16[2048,1024]{1,0:T(8,128)(2,1)} %values_ref.1), custom_call_target="tpu_custom_call" | custom-call | tf_op jit(solution)/shard_map/memory/pallas_call | solution.py:738
  295.1 1.6 slice.30.grad_ref
  296.7 1.6 multiply_convert_fusion
  298.3 0.0 copy-start.19
  298.3 0.0 copy-start.18
  298.4 0.7 copy-done.19
  299.0 1.2 fusion.8
  300.2 6.8 %pick_bwd.1.refs_6_ = bf16[128,2048]{1,0:T(8,128)(2,1)} custom-call(f32[128,128]{1,0:T(8,128)} %get-tuple-element.46.weight_ref, f32[128,128]{1,0:T(8,128)} %slice.30.grad_ref, s32[128,128]{1,0:T(8,128)} %copy.74.picks_ref), custom_call_target="tpu_custom_call" | custom-call | tf_op jit(solution)/shard_map/pick_bwd/pallas_call | solution.py:276
  307.0 1.9 convolution_convert_fusion.2
  308.8 6.5 %fusion.39 = f32[128,1024]{1,0:T(8,128)S(1)} fusion(bf16[128,4096]{0,1:T(8,128)(2,1)S(1)} %bitcast.73, bf16[1024,4096]{1,0:T(8,128)(2,1)} %get-tuple-element.43), kind=kOutput, calls=%fused_computation.98 | convolution fusion | flops 1073741824 | bytes 9961472 | tf_op jit(solution)/shard_map/dot_general | solution.py:25
  315.4 0.0 copy-start.23
  315.4 1.0 multiply_reduce_fusion
  316.4 0.2 fusion.36.refs_5_
  316.5 0.5 copy-done.6
  317.0 0.1 copy-done.23
  317.1 0.8 fusion.7
  317.9 0.8 fusion.23
  318.7 0.1 fusion.27
  318.8 0.8 concatenate.39.refs_8_
  319.7 92.6 %reduce_back.1 = (bf16[4,32,6144]{2,1,0:T(8,128)(2,1)}, bf16[128,3072]{1,0:T(8,128)(2,1)}) custom-call(bf16[128,1024]{1,0:T(8,128)(2,1)} %copy-done.19, bf16[128,1024]{1,0:T(8,128)(2,1)} %copy-done.12, bf16[128,1024]{1,0:T(8,128)(2,1)} %copy-done.17, bf16[128,1024]{1,0:T(8,128)(2,1)} %refs_3_.3, bf16[128,1024]{1,0:T(8,128)(2,1)} %copy-done.18, ...), custom_call_target="tpu_custom_call" | custom-call | tf_op jit(solution)/shard_map/reduce_back/pallas_call | solution.py:1171
  412.3 6.1 %fusion.19 = (f32[1024]{0:T(1024)S(1)}, f32[128]{0:T(128)S(1)}, f32[128,1024]{1,0:T(8,128)}) fusion(bf16[128,1024]{1,0:T(8,128)(2,1)S(1)} %copy-done.11, f32[128]{0:T(128)S(1)} %get-tuple-element.86, f32[1024]{0:T(1024)S(1)} %bitcast.83, bf16[128,3072]{1,0:T(8,128)(2,1)} %get-tuple-element.48.rows_ref, bf16[1024,3072]{1,0:T(8,128)(2,1)} %get-tuple-element.37), kind=kOutput, calls=%fused_computation.37 | convolution fusion | flops 806222720 | bytes 7873536 | tf_op jit(solution)/shard_map/dot_general | solution.py:25
  418.5 2.6 fusion.17
  421.1 52.1 %reduce_late.1 = bf16[4,32,3200]{2,1,0:T(8,128)(2,1)S(1)} custom-call(bf16[128,1024]{1,0:T(8,128)(2,1)S(1)} %get-tuple-element.65.first_ref, bf16[128,3072]{1,0:T(8,128)(2,1)S(1)} %copy-done.3, bf16[16,1024]{1,0:T(8,128)(2,1)S(1)} %concatenate.40.gain_ref), custom_call_target="tpu_custom_call" | custom-call | tf_op jit(solution)/shard_map/reduce_late/pallas_call | solution.py:1044
  473.2 3.4 copy-done.2
  476.5 6.3 %finish.1 = (f32[128,1024]{1,0:T(8,128)}, f32[128,1024]{1,0:T(8,128)}, f32[128,1024]{1,0:T(8,128)}, f32[128,3072]{1,0:T(8,128)}, f32[128,4096]{1,0:T(8,128)}, /*...) custom-call(bf16[128,6144]{1,0:T(8,128)(2,1)S(1)} %bitcast.70, bf16[128,3200]{1,0:T(8,128)(2,1)S(1)} %bitcast.69, ...), custom_call_target="tpu_custom_call" | custom-call | tf_op jit(solution)/shard_map/finish/pallas_call | solution.py:1227
  482.9 0.5 slice_bitcast_fusion
  (63 shorter events, 0.3 us)
Async XLA Ops:
  0.6 17.6 %copy-start.10 = (bf16[128,1024]{1,0:T(8,128)(2,1)S(1)}, bf16[128,1024]{1,0:T(8,128)(2,1)}, u32[]{:S(2)}) copy-start(bf16[128,1024]{1,0:T(8,128)(2,1)} %refs_0_.1) | copy-start | bytes 786436
  0.7 17.8 %copy-start.28 = (bf16[128]{0:T(256)(128)(2,1)S(1)}, bf16[128]{0:T(256)(128)(2,1)}, u32[]{:S(2)}) copy-start(bf16[128]{0:T(256)(128)(2,1)} %param.19) | copy-start | bytes 772
  0.7 17.8 %copy-start.29 = (bf16[128]{0:T(256)(128)(2,1)S(1)}, bf16[128]{0:T(256)(128)(2,1)}, u32[]{:S(2)}) copy-start(bf16[128]{0:T(256)(128)(2,1)} %param.16) | copy-start | bytes 772
  10.9 159.3 %all-to-all-start = ((s32[32,1,1024]{2,1,0:T(1,128)}), s32[32,1,1024]{2,1,0:T(1,128)S(1)}, u32[]{:S(2)}, u32[]{:S(2)}) async-start(s32[32,1,1024]{2,1,0:T(1,128)} %bitcast.15), calls=%async_computation | async-start | bytes 262144 | tf_op jit(solution)/shard_map/all_to_all | solution.py:1320
  19.1 109.9 %copy-start.27 = (s32[1024]{0:T(1024)S(1)}, s32[1024]{0:T(1024)}, u32[]{:S(2)}) copy-start(s32[1024]{0:T(1024)} %param.14) | copy-start | bytes 12292
  126.0 4.0 copy-start.22
  141.6 11.3 %copy-start.5 = (bf16[1024,1024]{1,0:T(8,128)(2,1)S(1)}, bf16[1024,1024]{1,0:T(8,128)(2,1)}, u32[]{:S(2)}) copy-start(bf16[1024,1024]{1,0:T(8,128)(2,1)} %get-tuple-element.39.refs_10_) | copy-start | bytes 6291460
  141.6 11.3 %copy-start.11 = (bf16[128,1024]{1,0:T(8,128)(2,1)S(1)}, bf16[128,1024]{1,0:T(8,128)(2,1)}, u32[]{:S(2)}) copy-start(bf16[128,1024]{1,0:T(8,128)(2,1)} %refs_0_.1) | copy-start | bytes 786436
  152.9 2.2 copy-start.17
  152.9 1.7 copy-start.8
  153.7 6.4 %copy-start.12 = (bf16[128,1024]{1,0:T(8,128)(2,1)}, bf16[128,1024]{1,0:T(8,128)(2,1)S(1)}, u32[]{:S(2)}) copy-start(bf16[128,1024]{1,0:T(8,128)(2,1)S(1)} %multiply_convert_fusion.3.refs_1_) | copy-start | bytes 786436
  155.1 5.9 %copy-start.24 = (f32[128,1024]{1,0:T(8,128)}, f32[128,1024]{1,0:T(8,128)S(1)}, u32[]{:S(2)}) copy-start(f32[128,1024]{1,0:T(8,128)S(1)} %fusion.38) | copy-start | bytes 1572868
  155.1 4.9 %copy-start = (bf16[2048,512]{1,0:T(8,128)(2,1)S(1)}, bf16[2048,512]{1,0:T(8,128)(2,1)}, u32[]{:S(2)}) copy-start(bf16[2048,512]{1,0:T(8,128)(2,1)} %get-tuple-element.42.keys_ref) | copy-start | bytes 6291460
  160.0 1.0 copy-start.7
  160.0 1.2 copy-start.15
  160.1 2.0 copy-start.20
  163.7 1.3 copy-start.25
  295.1 4.0 copy-start.21
  298.3 0.7 copy-start.19
  298.3 17.0 %copy-start.18 = (bf16[128,1024]{1,0:T(8,128)(2,1)}, bf16[128,1024]{1,0:T(8,128)(2,1)S(1)}, u32[]{:S(2)}) copy-start(bf16[128,1024]{1,0:T(8,128)(2,1)S(1)} %get-tuple-element.63.refs_4_) | copy-start | bytes 786436
  298.4 8.6 %copy-start.1 = (bf16[2048,512]{1,0:T(8,128)(2,1)S(1)}, bf16[2048,512]{1,0:T(8,128)(2,1)}, u32[]{:S(2)}) copy-start(bf16[2048,512]{1,0:T(8,128)(2,1)} %get-tuple-element.42.keys_ref) | copy-start | bytes 6291460
  308.8 6.5 %copy-start.9 = (bf16[1024,1024]{1,0:T(8,128)(2,1)S(1)}, bf16[1024,1024]{1,0:T(8,128)(2,1)}, u32[]{:S(2)}) copy-start(bf16[1024,1024]{1,0:T(8,128)(2,1)} %get-tuple-element.41) | copy-start | bytes 6291460
  315.3 1.1 copy-start.16
  315.3 1.7 copy-start.6
  315.4 1.7 copy-start.23
  316.3 1.6 copy-start.13
  317.1 1.8 copy-start.14
  317.1 1.6 copy-start.26
  418.4 2.7 copy-start.3
  418.5 54.7 %copy-start.4 = (bf16[4,32,6144]{2,1,0:T(8,128)(2,1)S(1)}, bf16[4,32,6144]{2,1,0:T(8,128)(2,1)}, u32[]{:S(2)}) copy-start(bf16[4,32,6144]{2,1,0:T(8,128)(2,1)} %get-tuple-element.49) | copy-start | bytes 4718596
  473.2 3.4 copy-start.2

commit v6 on v5

--- a/solution.py
+++ b/solution.py
@@ -43,21 +43,18 @@
     return ((lane < HDIM).astype(BF), (lane >= HDIM).astype(BF))
 
 
-def attn_fwd_kernel(rows, win, pos_ref, q_ref, k_ref, v_ref, qseg_ref, kseg_ref, out_ref, lse_ref):
-    pair = pl.program_id(0)
-    row0 = pos_ref[0] * rows
+def attn_fwd_pair(rows, win, pair, position, query, load, qseg_ref, kseg_ref, lse):
+    row0 = position * rows
     start = pl.multiple_of(jnp.maximum(row0 + rows - win, 0), LANES)
-    keys = k_ref[pl.ds(start, win), :]
-    values = v_ref[pl.ds(start, win), :]
+    keys, values = load(1, pl.ds(start, win)), load(2, pl.ds(start, win))
     key_pos = start + iota((rows, win), 1)
     query_pos = row0 + iota((rows, win), 0)
     allowed = (key_pos <= query_pos) & (kseg_ref[:, pl.ds(start, win)] == qseg_ref[...])
     lane = iota((rows, LANES), 1)
     masks = half_masks()
     outs = []
-    lse = jnp.where(pair == 0, jnp.zeros((rows, LANES), F32), lse_ref[...])
     for half in range(2):
-        scores = dot(q_ref[...] * masks[half], keys, NT) * 0.125
+        scores = dot(query * masks[half], keys, NT) * 0.125
         scores = jnp.where(allowed, scores, NEG)
         top = jnp.max(scores, axis=1, keepdims=True)
         weights = jnp.exp(scores - top)
@@ -65,8 +62,24 @@
         probs = weights * (1.0 / total)
         outs.append(dot(probs.astype(BF), values))
         lse = jnp.where(lane == pair * 2 + half, top + jnp.log(total), lse)
-    out_ref[...] = jnp.where(lane < HDIM, outs[0], outs[1])
-    lse_ref[...] = lse
+    return jnp.where(lane < HDIM, outs[0], outs[1]), lse
+
+
+def attn_fwd_kernel(rows, win, pos_ref, q_ref, k_ref, v_ref, qseg_ref, kseg_ref, out_ref, lse_ref):
+    pair = pl.program_id(0)
+    refs = (q_ref, k_ref, v_ref)
+    lse = jnp.where(pair == 0, jnp.zeros((rows, LANES), F32), lse_ref[...])
+    out_ref[...], lse_ref[...] = attn_fwd_pair(
+        rows,
+        win,
+        pair,
+        pos_ref[0],
+        q_ref[...],
+        lambda which, where: refs[which][where, :],
+        qseg_ref,
+        kseg_ref,
+        lse,
+    )
 
 
 def attn_fwd(pos, qkv, seg_row, seg_col, rows):
@@ -244,7 +257,33 @@
     )(half_scores, picks)
 
 
-def pick_bwd_kernel(weight_ref, grad_ref, picks_ref, out_ref, score_t, first_t, second_t):
+def pick_bwd_kernel(
+    weight_ref,
+    grad_ref,
+    picks_ref,
+    table_ref,
+    out_ref,
+    whole_ref,
+    score_t,
+    first_t,
+    second_t,
+    stage,
+    in_sem,
+    out_sem,
+):
+    block = table_ref.shape[0] // MHEADS
+
+    def part(c):
+        return pl.ds(pl.multiple_of(c * block, block), block)
+
+    def fetch(c):
+        return pltpu.make_async_copy(table_ref.at[part(c)], stage.at[c], in_sem.at[c])
+
+    def put(c):
+        return pltpu.make_async_copy(stage.at[c], whole_ref.at[part(c)], out_sem.at[c])
+
+    for c in range(MHEADS):
+        fetch(c).start()
     rows = picks_ref.shape[0]
     lane = iota((rows, LANES), 1)
     weights, grads = weight_ref[...], grad_ref[...]
@@ -266,23 +305,40 @@
         for e, total in enumerate((first, second)):
             base = pl.multiple_of((c * 2 + e) * NK, LANES)
             out_ref[:, pl.ds(base, NK)] = total.T.astype(BF)
+        fetch(c).wait()
+        put(c).start()
         return 0
 
     lax.fori_loop(0, MHEADS, head, 0)
-
-
-def pick_bwd(weights, grads, picks):
+    for c in range(MHEADS):
+        put(c).wait()
+
+
+def pick_bwd(weights, grads, picks, table):
     rows = picks.shape[0]
+    last = grads.shape[1] // LANES - 1
+    spec = pl.BlockSpec((rows, LANES), lambda i: (0, 0))
+    hbm = pl.BlockSpec(memory_space=pltpu.HBM)
     return pl.pallas_call(
         pick_bwd_kernel,
-        out_shape=jax.ShapeDtypeStruct((rows, MHEADS * 2 * NK), BF),
+        grid=(1,),
+        in_specs=[spec, pl.BlockSpec((rows, LANES), lambda i: (0, last)), spec, hbm],
+        out_specs=[pl.BlockSpec((rows, MHEADS * 2 * NK), lambda i: (0, 0)), hbm],
+        out_shape=[
+            jax.ShapeDtypeStruct((rows, MHEADS * 2 * NK), BF),
+            jax.ShapeDtypeStruct(table.shape, table.dtype),
+        ],
         scratch_shapes=[
             pltpu.VMEM((LANES, rows), F32),
             pltpu.VMEM((LANES, rows), jnp.int32),
             pltpu.VMEM((LANES, rows), jnp.int32),
+            pltpu.VMEM((MHEADS, table.shape[0] // MHEADS, table.shape[1]), table.dtype),
+            pltpu.SemaphoreType.DMA((MHEADS,)),
+            pltpu.SemaphoreType.DMA((MHEADS,)),
         ],
+        compiler_params=pltpu.CompilerParams(vmem_limit_bytes=40 * 1024 * 1024),
         name="pick_bwd",
-    )(weights, grads, picks)
+    )(weights, grads, picks, table)
 
 
 def owner_kernel(
@@ -409,45 +465,63 @@
     half = held.shape[2] // 2
     low, high = pl.ds(0, half), pl.ds(half, half)
     to_x, to_y = (across, m), (along, m)
-    ones, twos, threes, totals = {}, {}, {}, {}
+
+    def copy(kind, k, src, dst, peer):
+        return pltpu.make_async_remote_copy(
+            src_ref=src,
+            dst_ref=dst,
+            send_sem=send.at[kind, k],
+            recv_sem=recv.at[kind, k],
+            device_id=peer,
+            device_id_type=MESH,
+        )
+
+    def ones(k):
+        return (
+            copy(0, k, held.at[k, diagonal, low], x1.at[k], to_x),
+            copy(1, k, held.at[k, diagonal, high], y1.at[k], to_y),
+        )
+
+    def twos(k):
+        return (
+            copy(2, k, held.at[k, across], x2.at[k], to_x),
+            copy(3, k, held.at[k, along], y2.at[k], to_y),
+        )
+
+    def three(k):
+        return copy(4, k, held.at[k, g], zin.at[k], (g, (m + 2 * (3 - k)) % 8))
 
     def first(k):
-        ones[k] = (
-            push(held.at[k, diagonal, low], x1.at[k], send.at[0, k], recv.at[0, k], to_x),
-            push(held.at[k, diagonal, high], y1.at[k], send.at[1, k], recv.at[1, k], to_y),
-        )
+        for item in ones(k):
+            item.start()
 
     def corner(k):
-        for copy in ones[k]:
-            copy.wait_recv()
+        for item in ones(k):
+            item.wait_recv()
         held[k, along, low] = held[k, along, low] + x1[k]
         held[k, across, high] = held[k, across, high] + y1[k]
-        twos[k] = (
-            push(held.at[k, across], x2.at[k], send.at[2, k], recv.at[2, k], to_x),
-            push(held.at[k, along], y2.at[k], send.at[3, k], recv.at[3, k], to_y),
-        )
+        for item in twos(k):
+            item.start()
+
+    def total_of(k):
+        for item in twos(k):
+            item.wait_recv()
+        return held[k, g].astype(F32) + x2[k].astype(F32) + y2[k].astype(F32)
 
     def plane(k):
-        for copy in twos[k]:
-            copy.wait_recv()
-        total = held[k, g].astype(F32) + x2[k].astype(F32) + y2[k].astype(F32)
-        if k == 3:
-            totals[k] = total
-        else:
-            held[k, g] = total.astype(BF)
-            peer = (g, (m + 2 * (3 - k)) % 8)
-            threes[k] = push(held.at[k, g], zin.at[k], send.at[4, k], recv.at[4, k], peer)
+        held[k, g] = total_of(k).astype(BF)
+        three(k).start()
 
     def last():
-        total = totals[3]
+        total = total_of(3)
         for k in range(3):
-            threes[k].wait_recv()
+            three(k).wait_recv()
             total = total + zin[k].astype(F32)
         for k in range(4):
-            for copy in ones[k] + twos[k]:
-                copy.wait_send()
+            for item in ones(k) + twos(k):
+                item.wait_send()
             if k < 3:
-                threes[k].wait_send()
+                three(k).wait_send()
         return total
 
     return first, corner, plane, last
@@ -767,15 +841,13 @@
     )(payload, keys, values)
 
 
-def gather_kernel(pieces, count, *refs):
-    sources, targets = refs[:count], refs[count : 2 * count]
-    local_sem, send, recv = refs[2 * count :]
+def gather_tasks(pieces, sources, targets, local_sem, send, recv):
     g, m, across, along, sibling = places()
     z = m // 2
     to_x, to_y, to_s = (across, m), (along, m), (g, sibling)
-    enter(plane_peers())
     total = range(len(pieces))
     ways = [(sign, hop) for hop in (1, 2, 3) for sign in (1, -1)]
+    shared = [p for p in total if pieces[p][3]]
 
     def view(piece, owner, quarter=None, part=None):
         array, first, columns, _ = pieces[piece]
@@ -805,9 +877,8 @@
         peer = (g, (m + 8 + 2 * ways[way][0]) % 8)
         return copy(p, way, block, peer, src)
 
-    def has(way, hop=None):
+    def has(way):
         sign, distance = ways[way]
-        distance = distance if hop is None else hop
         return z >= distance if sign > 0 else z + distance <= 3
 
     def more(way):
@@ -832,11 +903,11 @@
         return copy(p, 30 + way, view(p, origin(way)), to_s)
 
     def first(p):
-        array, start, columns, shared = pieces[p]
+        array, start, columns, is_shared = pieces[p]
         ref = sources[array]
         whole = ref.at[:, pl.ds(start, columns)]
         src = whole
-        if shared:
+        if is_shared:
             quarter = ref.shape[0] // 4
             src = ref.at[pl.ds(g * quarter, quarter), pl.ds(start, columns)]
         return (
@@ -845,98 +916,236 @@
             copy(p, 36, view(p, m), to_s, whole),
         )
 
-    for p in total:
-        out, near, side = first(p)
-        for way in (0, 1):
-            pl.when(more(way))(out[way].start)
-        near.start()
-        side.start()
-
-    def arrive(p, hop):
-        for way in (2 * hop - 2, 2 * hop - 1):
-
-            @pl.when(has(way))
-            def _():
-                line(p, way, origin(way)).wait_recv()
-                if hop < 3:
-                    pl.when(more(way))(line(p, way + 2, origin(way)).start)
-                if pieces[p][3]:
-                    for item in planes(p, way):
+    def begin():
+        for p in total:
+            for way in (0, 1):
+                pl.when(more(way))(first(p)[0][way].start)
+        for p in total:
+            _, near, side = first(p)
+            near.start()
+            side.start()
+
+    def level(hop):
+        return (2 * hop - 2, 2 * hop - 1)
+
+    def arrive(hop):
+        for p in total:
+            for way in level(hop):
+
+                @pl.when(has(way))
+                def _():
+                    line(p, way, origin(way)).wait_recv()
+                    if hop < 3:
+                        pl.when(more(way))(line(p, way + 2, origin(way)).start)
+
+        for p in total:
+            for way in level(hop):
+
+                @pl.when(has(way))
+                def _():
+                    for item in planes(p, way) if p in shared else [core(p, way)]:
                         item.start()
-                else:
+
+    def turn(hop):
+        for p in shared:
+            for way in level(hop):
+
+                @pl.when(has(way))
+                def _():
+                    for item, after in zip(planes(p, way), corners(p, way), strict=True):
+                        item.wait_recv()
+                        after.start()
+
+    def cross(hop):
+        for p in shared:
+            for way in level(hop):
+
+                @pl.when(has(way))
+                def _():
+                    for item in corners(p, way):
+                        item.wait_recv()
                     core(p, way).start()
 
-    def turn(p, hop):
-        for way in (2 * hop - 2, 2 * hop - 1):
-
-            @pl.when(has(way))
-            def _():
-                for item, after in zip(planes(p, way), corners(p, way), strict=True):
-                    item.wait_recv()
-                    after.start()
-
-    def cross(p, hop):
-        for way in (2 * hop - 2, 2 * hop - 1):
-
-            @pl.when(has(way))
-            def _():
-                for item in corners(p, way):
-                    item.wait_recv()
-                core(p, way).start()
-
-    shared = [p for p in total if pieces[p][3]]
-    for hop in range(1, 6):
+    def end():
         for p in total:
-            if hop <= 3:
-                arrive(p, hop)
-            if p in shared and 1 <= hop - 1 <= 3:
-                turn(p, hop - 1)
-            if p in shared and 1 <= hop - 2 <= 3:
-                cross(p, hop - 2)
-    for p in total:
-        out, near, side = first(p)
-        near.wait()
-        side.wait()
-        for way in (0, 1):
-            pl.when(more(way))(out[way].wait_send)
-        for way in range(6):
-
-            @pl.when(has(way))
-            def _():
-                core(p, way).wait()
-                if ways[way][1] < 3:
-                    pl.when(more(way))(line(p, way + 2, origin(way)).wait_send)
-                if pieces[p][3]:
-                    for item in planes(p, way) + corners(p, way):
-                        item.wait_send()
-
-
-def gather_weights(arrays, chunk, own_count):
+            out, near, side = first(p)
+            near.wait()
+            side.wait()
+            for way in (0, 1):
+                pl.when(more(way))(out[way].wait_send)
+            for way in range(6):
+
+                @pl.when(has(way))
+                def _():
+                    core(p, way).wait()
+                    if ways[way][1] < 3:
+                        pl.when(more(way))(line(p, way + 2, origin(way)).wait_send)
+                    if p in shared:
+                        for item in planes(p, way) + corners(p, way):
+                            item.wait_send()
+
+    return begin, arrive, turn, cross, end
+
+
+def pieces_of(arrays, chunk, own_count):
     pieces = []
     for i, x in enumerate(arrays):
         columns = x.shape[1]
         for first in range(0, columns, chunk):
             pieces.append((i, first, min(chunk, columns - first), i >= own_count))
+    return tuple(pieces)
+
+
+def gathered(arrays):
+    return [jax.ShapeDtypeStruct((8 * x.shape[0], x.shape[1]), x.dtype) for x in arrays]
+
+
+def gather_sems(pieces):
+    return [
+        pltpu.SemaphoreType.DMA((len(pieces),)),
+        pltpu.SemaphoreType.DMA((len(pieces), 37)),
+        pltpu.SemaphoreType.DMA((len(pieces), 37)),
+    ]
+
+
+def gather_kernel(pieces, count, *refs):
+    enter(plane_peers())
+    begin, arrive, turn, cross, end = gather_tasks(
+        pieces, refs[:count], refs[count : 2 * count], *refs[2 * count :]
+    )
+    begin()
+    arrive(1)
+    arrive(2)
+    turn(1)
+    arrive(3)
+    turn(2)
+    cross(1)
+    turn(3)
+    cross(2)
+    cross(3)
+    end()
+
+
+def gather_first(arrays, chunk, own_count):
+    pieces = pieces_of(arrays, chunk, own_count)
     count = len(arrays)
     return pl.pallas_call(
-        functools.partial(gather_kernel, tuple(pieces), count),
-        in_specs=[pl.BlockSpec(memory_space=pl.ANY)] * count,
+        functools.partial(gather_kernel, pieces, count),
+        in_specs=[pl.BlockSpec(memory_space=pltpu.VMEM)] * count,
         out_specs=[pl.BlockSpec(memory_space=pl.ANY)] * count,
-        out_shape=[jax.ShapeDtypeStruct((8 * x.shape[0], x.shape[1]), x.dtype) for x in arrays],
-        scratch_shapes=[
-            pltpu.SemaphoreType.DMA((len(pieces),)),
-            pltpu.SemaphoreType.DMA((len(pieces), 37)),
-            pltpu.SemaphoreType.DMA((len(pieces), 37)),
+        out_shape=gathered(arrays),
+        scratch_shapes=gather_sems(pieces),
+        compiler_params=pltpu.CompilerParams(collective_id=3, has_side_effects=True),
+        name="gather_first",
+    )(*arrays)
+
+
+def gather_attend_kernel(pieces, count, rows, win, *refs):
+    sources, refs = refs[:count], refs[count:]
+    tokens_ref, gain_ref, weight_ref, segc_ref, segr_ref = refs[:5]
+    targets, refs = refs[5 : 5 + count], refs[5 + count :]
+    qkv_ref, out_ref, lse_ref, first_ref = refs[:4]
+    m = lax.axis_index("mem")
+    group_len, width = tokens_ref.shape
+    pairs = width // LANES
+    enter(plane_peers())
+    begin, arrive, turn, cross, end = gather_tasks(pieces, sources, targets, *refs[4:])
+
+    def normalize():
+        block = 2 * rows
+
+        def some(i, _):
+            where = pl.ds(pl.multiple_of(i * block, block), block)
+            values = tokens_ref[where, :].astype(F32)
+            first_ref[where, :] = (values * rms_scale(values) * gain_ref[...]).astype(BF)
+            return 0
+
+        lax.fori_loop(0, group_len // block, some, 0)
+
+    def project(i, _):
+        where = pl.ds(pl.multiple_of(i * 3 * LANES, LANES), 3 * LANES)
+        qkv_ref[:, where] = dot(first_ref[...], weight_ref[:, where]).astype(BF)
+
+        @pl.when(i == 2)
+        def _():
+            arrive(1)
+
+        @pl.when(i == 6)
+        def _():
+            arrive(2)
+
+        return 0
+
+    def load_of(pair):
+        def load(which, where):
+            column = pl.multiple_of((which * pairs + pair) * LANES, LANES)
+            return qkv_ref[where, pl.ds(column, LANES)]
+
+        return load
+
+    own = pl.ds(pl.multiple_of(m * rows, LANES), rows)
+
+    def attend(pair, _):
+        load = load_of(pair)
+        value, lse_ref[...] = attn_fwd_pair(
+            rows, win, pair, m, load(0, own), load, segc_ref.at[own], segr_ref, lse_ref[...]
+        )
+        out_ref[:, pl.ds(pl.multiple_of(pair * LANES, LANES), LANES)] = value
+
+        @pl.when(pair == 0)
+        def _():
+            turn(1)
+
+        @pl.when(pair == 3)
+        def _():
+            arrive(3)
+
+        @pl.when(pair == 5)
+        def _():
+            turn(2)
+            cross(1)
+
+        return 0
+
+    lse_ref[...] = jnp.zeros_like(lse_ref)
+    begin()
+    normalize()
+    lax.fori_loop(0, 8, project, 0)
+    lax.fori_loop(0, 8, attend, 0)
+    turn(3)
+    cross(2)
+    cross(3)
+    end()
+
+
+def gather_attend(arrays, chunk, tokens, gain, weight, seg_col, seg_row, rows):
+    pieces = pieces_of(arrays, chunk, 0)
+    count = len(arrays)
+    group_len, width = tokens.shape
+    win = min(group_len, group_len // 2 + rows)
+    vmem, hbm = pl.BlockSpec(memory_space=pltpu.VMEM), pl.BlockSpec(memory_space=pl.ANY)
+    return pl.pallas_call(
+        functools.partial(gather_attend_kernel, pieces, count, rows, win),
+        in_specs=[vmem] * (count + 5),
+        out_specs=[hbm] * count + [vmem] * 3,
+        out_shape=[
+            *gathered(arrays),
+            jax.ShapeDtypeStruct((group_len, 3 * width), BF),
+            jax.ShapeDtypeStruct((rows, width), F32),
+            jax.ShapeDtypeStruct((rows, LANES), F32),
         ],
-        compiler_params=pltpu.CompilerParams(collective_id=3, has_side_effects=True),
-        name="gather_weights",
-    )(*arrays)
+        scratch_shapes=[pltpu.VMEM((group_len, width), BF), *gather_sems(pieces)],
+        compiler_params=pltpu.CompilerParams(
+            collective_id=5, has_side_effects=True, vmem_limit_bytes=48 * 1024 * 1024
+        ),
+        name="gather_attend",
+    )(*arrays, tokens, gain, weight, seg_col, seg_row)
 
 
 WIDTH = HEADS * HDIM
 KEYS = MHEADS * 2 * NK
 QUERIES = MHEADS * 2 * HALF
-EARLY = (WIDTH,) * 6 + (KEYS, QUERIES)
+EARLY = (WIDTH,) * 6 + (KEYS,)
 EARLY_PRODUCTS = (
     (0, 3 * WIDTH, WIDTH, 0),
     (WIDTH, 4 * WIDTH, WIDTH, WIDTH),
@@ -944,8 +1153,7 @@
     (WIDTH, 6 * WIDTH, KEYS, 3 * WIDTH),
 )
 E_OUT, E_GATE, E_PROJ, E_HALF = 0, WIDTH, 2 * WIDTH, 3 * WIDTH
-E_KEYS = E_HALF + KEYS
-E_ALL = E_KEYS + 2 * HALF
+E_ALL = E_HALF + KEYS
 LATE = (WIDTH, 3 * WIDTH)
 LATE_PRODUCTS = ((0, WIDTH, 3 * WIDTH, 0),)
 L_GAIN = 3 * WIDTH
@@ -1011,56 +1219,123 @@
 
 
 def late_kernel(
-    first_ref, rows_ref, gain_ref, out_ref, fact, gains, held, x1, y1, x2, y2, zin, quarter, *sems
+    first_ref,
+    rows_ref,
+    gain_ref,
+    half_ref,
+    query_ref,
+    out_ref,
+    keys_ref,
+    fact,
+    gains,
+    wide,
+    held,
+    x1,
+    y1,
+    x2,
+    y2,
+    zin,
+    quarter,
+    tables,
+    arrived,
+    local_sem,
+    send,
+    recv,
 ):
-    local_sem, send, recv = sems
+    g, m, _, _, _ = places()
+    core, z = m % 2, m // 2
     enter(plane_peers())
     moves = factor_moves((first_ref, rows_ref), LATE, fact)
-    copies = share_factors([*moves, (gain_ref, gains, 0, WIDTH)], local_sem, send, recv)
+    moves.append((gain_ref, gains, 0, WIDTH))
+    moves += factor_moves((half_ref, query_ref), (KEYS, QUERIES), wide)
+    copies = share_factors(moves, local_sem, send, recv)
     first, corner, plane, last = plane_tasks(held, x1, y1, x2, y2, zin, send, recv)
-    for near, far in copies:
+    for near, far in copies[:3]:
         near.wait()
         far.wait_recv()
     row = iota((32, LANES), 0) % 16
     column = iota((32, LANES), 1)
     select = ((row < 4) & (row // 2 == column)).astype(F32).astype(BF)
-    for k in range(4):
+
+    def table(d):
+        block = (z + d) % 4 * 2 + core
+        lhs = wide[:, pl.ds(pl.multiple_of(block * NK, LANES), NK)]
+        rhs = wide[:, pl.ds(pl.multiple_of(KEYS + block * HALF, LANES), HALF)]
+        return dot(lhs, rhs, TN)
+
+    def line(k):
+        return pltpu.make_async_remote_copy(
+            src_ref=tables.at[k],
+            dst_ref=arrived.at[k],
+            send_sem=send.at[7, k],
+            recv_sem=recv.at[7, k],
+            device_id=(g, (m + 2 * (k + 1)) % 8),
+            device_id_type=MESH,
+        )
+
+    def ready(k, _):
         products_of(k, fact, held, LATE_PRODUCTS)
         lhs = gains[:, pl.ds(pl.multiple_of(block_of(k) * LANES, LANES), LANES)]
         store_blocks(held, k, dot(lhs, select, TN), L_GAIN)
         first(k)
+        return 0
+
+    lax.fori_loop(0, 4, ready, 0)
+    for near, far in copies[3:]:
+        near.wait()
+        far.wait_recv()
+
+    def send_table(k, _):
+        tables[k] = table(k + 1).astype(BF)
+        line(k).start()
+        return 0
+
+    lax.fori_loop(0, 3, send_table, 0)
+    keys_ref[...] = table(0)
     for k in range(4):
         corner(k)
-    for k in range(4):
+    for k in range(3):
         plane(k)
     spread_quarters(last(), quarter, send, recv)
+    for k in range(3):
+        line(k).wait_recv()
+        keys_ref[...] += arrived[k].astype(F32)
+        line(k).wait_send()
     for _, far in copies:
         far.wait_send()
     out_ref[...] = quarter[...]
 
 
-def reduce_late(first, qkv_rows, gains):
+def reduce_late(first, qkv_rows, gains, half, query):
     rows = first.shape[0]
-    return pl.pallas_call(
+    vmem = pl.BlockSpec(memory_space=pltpu.VMEM)
+    sums, keys = pl.pallas_call(
         late_kernel,
-        in_specs=[pl.BlockSpec(memory_space=pl.ANY)] * 3,
-        out_specs=pl.BlockSpec(memory_space=pltpu.VMEM),
-        out_shape=jax.ShapeDtypeStruct((4, 32, L_ALL), BF),
+        in_specs=[pl.BlockSpec(memory_space=pl.ANY)] * 5,
+        out_specs=[vmem, vmem],
+        out_shape=[
+            jax.ShapeDtypeStruct((4, 32, L_ALL), BF),
+            jax.ShapeDtypeStruct((NK, HALF), F32),
+        ],
         scratch_shapes=[
             pltpu.VMEM((2 * rows, sum(LATE)), BF),
             pltpu.VMEM((32, WIDTH), BF),
+            pltpu.VMEM((2 * rows, KEYS + QUERIES), BF),
             pltpu.VMEM((4, 4, 32, L_ALL), BF),
             *plane_scratch(32, L_ALL),
             pltpu.VMEM((4, 32, L_ALL), BF),
-            pltpu.SemaphoreType.DMA((3,)),
-            pltpu.SemaphoreType.DMA((7, 4)),
-            pltpu.SemaphoreType.DMA((7, 4)),
+            pltpu.VMEM((3, NK, HALF), BF),
+            pltpu.VMEM((3, NK, HALF), BF),
+            pltpu.SemaphoreType.DMA((5,)),
+            pltpu.SemaphoreType.DMA((8, 5)),
+            pltpu.SemaphoreType.DMA((8, 5)),
         ],
         compiler_params=pltpu.CompilerParams(
-            collective_id=2, has_side_effects=True, vmem_limit_bytes=40 * 1024 * 1024
+            collective_id=2, has_side_effects=True, vmem_limit_bytes=48 * 1024 * 1024
         ),
         name="reduce_late",
-    )(first, qkv_rows, gains).reshape(4 * 32, L_ALL)
+    )(first, qkv_rows, gains, half, query)
+    return sums.reshape(4 * 32, L_ALL), keys
 
 
 def back_kernel(rows, win, *refs):
@@ -1102,20 +1377,13 @@
     for near, far in copies:
         near.wait()
         far.wait_recv()
-    for k in range(4):
+
+    def ready(k, _):
         products_of(k, fact, held, EARLY_PRODUCTS)
-        block = block_of(k)
-        lhs = fact[:, pl.ds(pl.multiple_of(6 * WIDTH + block * NK, LANES), NK)]
-        at = 6 * WIDTH + KEYS
-        rhs = fact[:, pl.ds(pl.multiple_of(at + block * HALF, LANES), HALF)]
-        value = dot(lhs, rhs, TN)
-        for i in range(4):
-            for h in range(2):
-                row = i * 64 + h * 32
-                held[k, i, :, E_KEYS + h * HALF : E_KEYS + (h + 1) * HALF] = value[
-                    row : row + 32
-                ].astype(BF)
         first(k)
+        return 0
+
+    lax.fori_loop(0, 4, ready, 0)
     corner(0)
     for copy, after in zip(lines, forward, strict=True):
         copy.wait_recv()
@@ -1126,12 +1394,15 @@
     for copy in forward:
         copy.wait_recv()
     corner(2)
-    for i in range(0, shared.shape[0], 2 * rows):
-        where = slice(i, i + 2 * rows)
+    def project(i, _):
+        where = pl.ds(pl.multiple_of(i * 2 * rows, 2 * rows), 2 * rows)
         douts[where, :] = dot(shared[where, :WIDTH], proj_ref[...], NT).astype(BF)
         stats[where, :] = shared[where, WIDTH : WIDTH + 2 * HEADS].astype(F32) + shared[
             where, WIDTH + 2 * HEADS : WIDTH + 4 * HEADS
         ].astype(F32)
+        return 0
+
+    lax.fori_loop(0, shared.shape[0] // (2 * rows), project, 0)
     corner(3)
 
     def load_of(pair):
@@ -1148,11 +1419,11 @@
         for i, value in enumerate(grads):
             column = pl.multiple_of((i * pairs + pair) * LANES, LANES)
             rows_ref[:, pl.ds(column, LANES)] = value
+        for k in range(3):
+            pl.when(pair == 2 * k + 1)(functools.partial(plane, k))
         return 0
 
-    for k in range(4):
-        lax.fori_loop(2 * k, 2 * k + 2, attend, 0)
-        plane(k)
+    lax.fori_loop(0, pairs, attend, 0)
     spread_quarters(last(), quarter, send, recv)
     for _, far in copies:
         far.wait_send()
@@ -1196,11 +1467,22 @@
     return sums.reshape(4 * 32, E_ALL), qkv_rows
 
 
+def fold_kernel(query_ref, keys_ref, out_ref):
+    for c in range(MHEADS * 2):
+        out_ref[:, c * NK : (c + 1) * NK] = dot(
+            query_ref[:, c * HALF : (c + 1) * HALF], keys_ref[c * NK : (c + 1) * NK, :], NT
+        ).astype(BF)
+
+
+def fold(query, keys):
+    return pl.pallas_call(
+        fold_kernel, out_shape=jax.ShapeDtypeStruct((query.shape[0], KEYS), BF), name="fold"
+    )(query, keys)
+
+
 def finish_kernel(
-    early_ref, late_ref, keys_ref, table_ref, out, gate, proj, qkv, query, half, gains, whole, sem
+    early_ref, late_ref, keys_ref, out, gate, proj, qkv, query, gains
 ):
-    copy = pltpu.make_async_copy(table_ref, whole, sem)
-    copy.start()
     for ref, first in ((out, E_OUT), (gate, E_GATE), (proj, E_PROJ)):
         ref[...] = early_ref[:, first : first + WIDTH].astype(F32)
     qkv[...] = late_ref[:, : 3 * WIDTH].astype(F32)
@@ -1209,30 +1491,19 @@
         query[:, c * HALF : (c + 1) * HALF] = dot(
             early_ref[:, E_HALF + c * NK : E_HALF + (c + 1) * NK], table
         )
-    for i in range(4):
-        for h in range(2):
-            first = i * 64 + h * 32
-            half[first : first + 32, :] = early_ref[
-                i * 32 : (i + 1) * 32, E_KEYS + h * HALF : E_KEYS + (h + 1) * HALF
-            ].astype(F32)
     gains[...] = late_ref[:, L_GAIN:].astype(F32).T[:8]
-    copy.wait()
-
-
-def finish(early, late, keys, table):
+
+
+def finish(early, late, keys):
     rows = early.shape[0]
-    shapes = [(rows, WIDTH)] * 3 + [(rows, 3 * WIDTH), (rows, QUERIES), (2 * rows, HALF)]
+    shapes = [(rows, WIDTH)] * 3 + [(rows, 3 * WIDTH), (rows, QUERIES)]
     shapes.append((8, LANES))
-    vmem, hbm = pl.BlockSpec(memory_space=pltpu.VMEM), pl.BlockSpec(memory_space=pl.ANY)
     return pl.pallas_call(
         finish_kernel,
-        in_specs=[vmem, vmem, vmem, hbm],
-        out_specs=[vmem] * len(shapes) + [hbm],
-        out_shape=[jax.ShapeDtypeStruct(shape, F32) for shape in [*shapes, table.shape]],
-        scratch_shapes=[pltpu.SemaphoreType.DMA],
+        out_shape=[jax.ShapeDtypeStruct(shape, F32) for shape in shapes],
         compiler_params=pltpu.CompilerParams(vmem_limit_bytes=40 * 1024 * 1024),
         name="finish",
-    )(early, late, keys, table)
+    )(early, late, keys)
 
 
 def rms_scale(values):
@@ -1280,28 +1551,8 @@
         gain_block = jnp.concatenate(
             [attn_gain[None], mem_gain[None], jnp.zeros((14, LANES), BF)]
         )
-        (
-            tokens_all,
-            gains,
-            qkv_full,
-            proj_full,
-            keys_full,
-            query_full,
-            gate_full,
-            output_full,
-        ) = gather_weights(
-            (
-                tokens,
-                gain_block,
-                qkv_weight,
-                attn_proj,
-                half_keys,
-                query_weight,
-                gate_weight,
-                out_weight,
-            ),
-            2 * width,
-            2,
+        tokens_all, gains, qkv_full, keys_full = gather_first(
+            (tokens, gain_block, qkv_weight, half_keys), 3 * width // 2, 2
         )
         gains = gains.reshape(8, 16, LANES)[:, :2].transpose(1, 0, 2).reshape(2, width)
     else:
@@ -1315,33 +1566,49 @@
         output_full = gather(out_weight)
     gains = gains.astype(F32)
     gain_one, gain_two = gains[0:1], gains[1:2]
+    seg_row, seg_col = segment_ids.reshape(1, group_len), segment_ids.reshape(group_len, 1)
 
     requests = route(picks, owners, local_rows, capacity, flat_bits)
     arrived = lax.all_to_all(requests, ALL, split_axis=0, concat_axis=0, tiled=True)
 
-    inputs_all = tokens_all.astype(F32)
-    first_all = (inputs_all * rms_scale(inputs_all) * gain_one).astype(BF)
-    qkv_all = dot(first_all, qkv_full).astype(BF)
-    seg_row, seg_col = segment_ids.reshape(1, group_len), segment_ids.reshape(group_len, 1)
-    attn_sum, lse = attn_fwd(pos, qkv_all, seg_row, seg_col, rows)
+    if linked:
+        folded = fold(query_weight, keys_full)
+        proj_full, folded_full, gate_full, output_full, qkv_all, attn_sum, lse = gather_attend(
+            (attn_proj, folded, gate_weight, out_weight),
+            width,
+            tokens_all,
+            gain_one,
+            qkv_full,
+            seg_col,
+            seg_row,
+            rows,
+        )
+    else:
+        inputs_all = tokens_all.astype(F32)
+        first_all = (inputs_all * rms_scale(inputs_all) * gain_one).astype(BF)
+        qkv_all = dot(first_all, qkv_full).astype(BF)
+        attn_sum, lse = attn_fwd(pos, qkv_all, seg_row, seg_col, rows)
     attended = attn_sum.astype(BF)
     inputs = tokens.astype(F32)
     residual = inputs + dot(attended, proj_full)
     scale_two = rms_scale(residual)
     second = (residual * scale_two * gain_two).astype(BF)
-    mem_query = dot(second, query_full).astype(BF)
     gate_pre = dot(second, gate_full)
     mixed_grad = dot(out_cotangent, output_full, NT)
     sig = jax.nn.sigmoid(gate_pre)
     gate_act = gate_pre * sig
     memory_grad = (mixed_grad * gate_act).astype(BF)
-    key_table = keys_full.reshape(MHEADS * 2, NK, HALF)
-    half_scores = jnp.einsum(
-        "tcf,cnf->tcn",
-        mem_query.reshape(rows, MHEADS * 2, HALF),
-        key_table,
-        preferred_element_type=F32,
-    ).reshape(rows, MHEADS * 2 * NK)
+    if linked:
+        half_scores = dot(second, folded_full)
+    else:
+        mem_query = dot(second, query_full).astype(BF)
+        key_table = keys_full.reshape(MHEADS * 2, NK, HALF)
+        half_scores = jnp.einsum(
+            "tcf,cnf->tcn",
+            mem_query.reshape(rows, MHEADS * 2, HALF),
+            key_table,
+            preferred_element_type=F32,
+        ).reshape(rows, KEYS)
     pick_weights, weights_low = pick_fwd(half_scores, flat_picks)
 
     payload = jnp.concatenate([memory_grad, weights_low], axis=1)
@@ -1358,18 +1625,22 @@
     values_grad = values_grad.reshape(local_rows, width)
 
     memory_out = back[:, :width].astype(F32)
-    weight_grad = back[:, width:].astype(F32)
     mixed = (memory_out * gate_act).astype(BF)
     block_out = (residual + dot(mixed, output_full)).astype(BF)
     gate_grad = (mixed_grad * memory_out * (sig * (1.0 + gate_pre * (1.0 - sig)))).astype(BF)
-    half_grad = pick_bwd(pick_weights, weight_grad, flat_picks)
-    half_cube = half_grad.reshape(rows, MHEADS * 2, NK)
-    query_grad = (
-        jnp.einsum("tcn,cnf->tcf", half_cube, key_table, preferred_element_type=F32)
-        .astype(BF)
-        .reshape(rows, MHEADS * 2 * HALF)
+    half_grad, values_grad = pick_bwd(
+        pick_weights, back.astype(F32), flat_picks, values_grad
     )
-    second_grad = dot(gate_grad, gate_full, NT) + dot(query_grad, query_full, NT)
+    if linked:
+        second_grad = dot(gate_grad, gate_full, NT) + dot(half_grad, folded_full, NT)
+    else:
+        half_cube = half_grad.reshape(rows, MHEADS * 2, NK)
+        query_grad = (
+            jnp.einsum("tcn,cnf->tcf", half_cube, key_table, preferred_element_type=F32)
+            .astype(BF)
+            .reshape(rows, QUERIES)
+        )
+        second_grad = dot(gate_grad, gate_full, NT) + dot(query_grad, query_full, NT)
     resid_from_norm, gain_two_grad = rms_back(residual, scale_two, gain_two, second_grad)
     resid_grad = out_cotangent.astype(F32) + resid_from_norm
     resid_low = resid_grad.astype(BF)
@@ -1402,7 +1673,6 @@
             gate_grad,
             resid_low,
             half_grad,
-            mem_query,
         )
         early, qkv_rows = reduce_back(early, shared, qkv_all, proj_full, seg_col, seg_row)
     else:
@@ -1423,17 +1693,17 @@
         sums_high = lax.reduce_precision(sums, 8, 7)
         gain_rows = jnp.stack([sums_high, sums - sums_high], axis=1).reshape(4, width)
         gain_rows = jnp.concatenate([gain_rows.astype(BF), jnp.zeros((12, width), BF)])
-        late = reduce_late(first_low, qkv_rows, gain_rows)
+        late, keys_share = reduce_late(
+            first_low, qkv_rows, gain_rows, early[:, E_HALF:], query_weight
+        )
         (
             out_share,
             gate_share,
             proj_share,
             qkv_share,
             query_share,
-            keys_share,
             gain_sums,
-            values_grad,
-        ) = finish(early, late, keys_full, values_grad)
+        ) = finish(early, late, keys_full)
     else:
         keys_grad = jnp.einsum(
             "tcn,tcf->cnf",

time: 490 us -> 461 us (0.941)
  matrix products: 37.9 us -> 15.7 us
    dot_general x10 -> x9, matrix products: 34.6 us -> 14.9 us  [dot(): lax.dot_general(left, right, (dims, ((), ())), preferred_element_type=F32)]
    pallas_call x1, Pallas kernels: 92.6 us -> 83.8 us  [reduce_back(): pl.pallas_call(functools.partial(back_kernel, rows, win), in_specs=[hbm]...]
    pallas_call x1, Pallas kernels: 52.1 us -> 60.5 us  [reduce_late(): pl.pallas_call(late_kernel, in_specs=[pl.BlockSpec(memory_space=pl.ANY)]...]
    pallas_call x4 -> x5, Pallas kernels: 130 us -> 127 us  [the longest x1 58.6 us: gather_first(): pl.pallas_call(functools.partial(gather_kernel, pieces, count), in_specs=...]
    unnamed x62 -> x85, local copies, waits for them, and re-layouts: 8.68 us -> 10.8 us
  transfers between devices with their start and end apart: 1 -> 1, of which waited for: 0 -> 0; matrix products, arithmetic and copies ran while one was open for 6% -> 2% of each run, Pallas kernels for 25% -> 26%
where the time goes in v6:
time: 461 us; the launch traced here: 455 us
  Pallas kernels  400 us (87%)
  other arithmetic  16.2 us (4%)
  matrix products  15.7 us (3%)
  local copies, waits for them, and re-layouts  14.2 us (3%)
  starting transfers between devices  7.3 us (2%)
    pallas_call x1, Pallas kernels, memory_call(): pl.pallas_call(functools.partial(memory_kernel, flat_bits), in_specs=[hbm...  126 us
    pallas_call x1, Pallas kernels, reduce_back(): pl.pallas_call(functools.partial(back_kernel, rows, win), in_specs=[hbm]...  83.8 us
    pallas_call x1, Pallas kernels, reduce_late(): pl.pallas_call(late_kernel, in_specs=[pl.BlockSpec(memory_space=pl.ANY)]...  60.5 us
    pallas_call x1, Pallas kernels, gather_first(): pl.pallas_call(functools.partial(gather_kernel, pieces, count), in_specs=...  58.6 us
    pallas_call x1, Pallas kernels, gather_attend(): pl.pallas_call(functools.partial(gather_attend_kernel, pieces, count, row...  54.7 us
    dot_general x9, matrix products, dot(): lax.dot_general(left, right, (dims, ((), ())), preferred_element_type=F32)  14.9 us
    unnamed x85, local copies, waits for them, and re-layouts  10.8 us
  transfers between devices with their start and end apart: 1, of which 0 were waited for; matrix products, arithmetic and copies ran while one was open for 2% of the time, Pallas kernels for 26%

profile of v6, /device:TPU:0, one launch (start us, length us, event | category | flops | bytes accessed | tf_op | source)
XLA Modules:
  0.0 455.3 jit_solution(11502264199459076986)
XLA Ops:
  0.6 0.0 copy-start.25
  0.7 0.0 copy-start.18
  0.7 1.0 copy.62
  1.7 0.2 reshape.264
  1.9 0.3 convert_reduce_fusion.1
  2.3 0.1 copy.63
  2.3 0.1 reduce-window.8
  2.4 0.1 reduce
  2.5 0.4 convert_reduce_fusion
  3.0 8.0 %sort.7 = s32[32768]{0:T(1024)} sort(s32[32768]{0:T(1024)S(1)} %pad_add_fusion), dimensions={0}, to_apply=%region_4.5 | sort | flops 491520 | bytes 262144 | tf_op jit(solution)/shard_map/sort | solution.py:432
  10.9 7.3 %all-to-all-start = ((s32[32,1,1024]{2,1,0:T(1,128)}), s32[32,1,1024]{2,1,0:T(1,128)S(1)}, u32[]{:S(2)}, u32[]{:S(2)}) async-start(s32[32,1,1024]{2,1,0:T(1,128)} %bitcast.11), calls=%async_computation | async-start | bytes 262144 | tf_op jit(solution)/shard_map/all_to_all | solution.py:1572
  18.3 0.1 fusion.3
  18.4 0.1 pad.13.clone
  18.5 0.7 maximum_maximum_fusion.refs_1_
  19.1 58.6 %gather_first.1 = (bf16[1024,1024]{1,0:T(8,128)(2,1)}, bf16[128,128]{1,0:T(8,128)(2,1)}, bf16[1024,3072]{1,0:T(8,128)(2,1)}, bf16[2048,512]{1,0:T(8,128)(2,1)}) custom-call(bf16[128,1024]{1,0:T(8,128)(2,1)} %refs_0_.2, bf16[16,128]{1,0:T(8,128)(2,1)} %maximum_maximum_fusion.refs_1_, bf16[128,3072]{1,0:T(8,128)(2,1)} %refs_2_.2, bf16[256,512]{1,0:T(8,128)(2,1)} %refs_3_.3), custom_call_target="tpu_custom_call" | custom-call | tf_op jit(solution)/shard_map/gather_first/pallas_call | solution.py:1032
  77.8 0.7 slice.37
  78.5 0.0 copy-start.14
  78.5 0.0 copy-start.16
  78.6 0.2 copy.59.refs_7_.refs_10_
  78.8 0.0 copy-start.4
  78.8 3.7 fold.1.refs_1_
  82.5 1.0 copy-done.9
  83.6 54.7 %gather_attend.1 = (bf16[1024,1024]{1,0:T(8,128)(2,1)S(1)}, bf16[1024,2048]{1,0:T(8,128)(2,1)}, bf16[1024,1024]{1,0:T(8,128)(2,1)}, bf16[1024,1024]{1,0:T(8,128)...) custom-call(bf16[128,1024]{1,0:T(8,128)(2,1)S(1)} %copy-done.14, ...), custom_call_target="tpu_custom_call" | custom-call | tf_op jit(solution)/shard_map/gather_attend/pallas_call | solution.py:1127
  138.2 0.0 copy-start
  138.3 0.0 copy-start.10
  138.4 0.5 multiply_reduce_fusion.2
  138.9 0.4 copy-done.32
  139.3 0.1 multiply_convert_fusion.3.refs_1_
  139.4 0.2 copy-done
  139.7 0.2 copy-done.10
  139.8 1.4 copy-done.23
  141.2 0.4 fusion.26
  141.6 0.8 copy-done.21
  142.4 1.7 fusion.27.scores_ref
  144.1 0.0 copy-start.38
  144.1 1.6 multiply_convert_fusion.2
  145.8 0.7 copy.61.picks_ref
  146.5 3.0 pick_fwd.1
  149.5 1.5 pad_maximum_fusion.payload_ref
  151.0 0.7 copy.73
  151.7 126.1 %memory.1 = (f32[128,1152]{1,0:T(8,128)}, f32[4,512,1024]{2,1,0:T(8,128)}) custom-call(bf16[128,1152]{1,0:T(8,128)(2,1)} %pad_maximum_fusion.payload_ref, s32[32,1024]{1,0:T(8,128)} %bitcast.59, bf16[2048,1024]{1,0:T(8,128)(2,1)} %values_ref.1), custom_call_target="tpu_custom_call" | custom-call | tf_op jit(solution)/shard_map/memory/pallas_call | solution.py:812
  277.8 1.8 multiply_convert_fusion
  279.6 0.2 copy-done.36
  279.9 1.2 fusion.2
  281.0 0.5 copy-done.24
  281.6 0.8 fusion.28
  282.5 3.4 copy-done.3
  285.8 7.1 %pick_bwd.1 = (bf16[128,2048]{1,0:T(8,128)(2,1)S(1)}, f32[2048,1024]{1,0:T(8,128)}) custom-call(f32[128,128]{1,0:T(8,128)S(1)} %copy-done.17, f32[128,1152]{1,0:T(8,128)S(1)} %copy-done.8, s32[128,128]{1,0:T(8,128)S(1)} %copy-done.13, f32[2048,1024]{1,0:T(8,128)S(1)} %bitcast.50), custom_call_target="tpu_custom_call" | custom-call | tf_op jit(solution)/shard_map/pick_bwd/pallas_call | solution.py:322
  293.0 0.0 copy-start.1
  293.0 0.0 copy-start.11
  293.0 1.6 multiply_reduce_fusion
  294.7 0.2 fusion.25.refs_5_
  294.9 0.0 copy-done.11
  294.9 0.8 fusion.1
  295.7 0.8 fusion.12
  296.5 0.1 fusion.16
  296.6 0.8 concatenate.39.refs_7_
  297.4 83.8 %reduce_back.1 = (bf16[4,32,5120]{2,1,0:T(8,128)(2,1)}, bf16[128,3072]{1,0:T(8,128)(2,1)}) custom-call(bf16[128,1024]{1,0:T(8,128)(2,1)} %copy-done.33, bf16[128,1024]{1,0:T(8,128)(2,1)} %copy-done.29, bf16[128,1024]{1,0:T(8,128)(2,1)} %copy-done.32, bf16[128,1024]{1,0:T(8,128)(2,1)} %refs_3_.5, bf16[128,1024]{1,0:T(8,128)(2,1)} %copy-done.34, ...), custom_call_target="tpu_custom_call" | custom-call | tf_op jit(solution)/shard_map/reduce_back/pallas_call | solution.py:1442
  381.2 6.2 %fusion.10 = (f32[1024]{0:T(1024)S(1)}, f32[128]{0:T(128)S(1)}, f32[128,1024]{1,0:T(8,128)}) fusion(bf16[128,1024]{1,0:T(8,128)(2,1)S(1)} %copy-done.26, f32[128]{0:T(128)S(1)} %get-tuple-element.93, f32[1024]{0:T(1024)S(1)} %get-tuple-element.79, bf16[128,3072]{1,0:T(8,128)(2,1)} %get-tuple-element.54.rows_ref, ...), kind=kOutput, calls=%fused_computation.24 | convolution fusion | flops 806222720 | bytes 7873536 | tf_op jit(solution)/shard_map/dot_general | solution.py:25
  387.6 2.7 fusion.8
  390.3 60.5 %reduce_late.1 = (bf16[4,32,3200]{2,1,0:T(8,128)(2,1)S(1)}, f32[256,512]{1,0:T(8,128)S(1)}) custom-call(bf16[128,1024]{1,0:T(8,128)(2,1)S(1)} %get-tuple-element.71.first_ref, bf16[128,3072]{1,0:T(8,128)(2,1)S(1)} %copy-done.6, bf16[16,1024]{1,0:T(8,128)(2,1)S(1)} %concatenate.40.gain_ref, bf16[128,2048]{1,0:T(8,128)(2,1)S(1)} %slice.40.half_ref, ...), custom_call_target="tpu_custom_call" | custom-call | tf_op jit(solution)/shard_map/reduce_late/pallas_call | solution.py:1312
  450.8 2.7 finish.1
  453.5 0.5 slice_bitcast_fusion.1
  454.0 0.8 copy.75
  (82 shorter events, 0.4 us)
Async XLA Ops:
  0.6 17.6 %copy-start.25 = (bf16[128,1024]{1,0:T(8,128)(2,1)S(1)}, bf16[128,1024]{1,0:T(8,128)(2,1)}, u32[]{:S(2)}) copy-start(bf16[128,1024]{1,0:T(8,128)(2,1)} %refs_0_.2) | copy-start | bytes 786436
  0.7 17.8 %copy-start.39 = (bf16[128]{0:T(256)(128)(2,1)S(1)}, bf16[128]{0:T(256)(128)(2,1)}, u32[]{:S(2)}) copy-start(bf16[128]{0:T(256)(128)(2,1)} %param.19) | copy-start | bytes 772
  0.7 17.8 %copy-start.40 = (bf16[128]{0:T(256)(128)(2,1)S(1)}, bf16[128]{0:T(256)(128)(2,1)}, u32[]{:S(2)}) copy-start(bf16[128]{0:T(256)(128)(2,1)} %param.16) | copy-start | bytes 772
  0.7 77.8 %copy-start.18 = (s32[1024]{0:T(1024)S(1)}, s32[1024]{0:T(1024)}, u32[]{:S(2)}) copy-start(s32[1024]{0:T(1024)} %param.14) | copy-start | bytes 12292
  10.9 140.0 %all-to-all-start = ((s32[32,1,1024]{2,1,0:T(1,128)}), s32[32,1,1024]{2,1,0:T(1,128)S(1)}, u32[]{:S(2)}, u32[]{:S(2)}) async-start(s32[32,1,1024]{2,1,0:T(1,128)} %bitcast.11), calls=%async_computation | async-start | bytes 262144 | tf_op jit(solution)/shard_map/all_to_all | solution.py:1572
  78.5 4.0 copy-start.14
  78.5 4.0 copy-start.15
  78.5 4.0 copy-start.16
  78.8 59.5 %copy-start.4 = (s32[1024,1]{1,0:T(8,128)}, s32[1024,1]{1,0:T(8,128)S(1)}, u32[]{:S(2)}) copy-start(s32[1024,1]{1,0:T(8,128)S(1)} %copy.59.refs_7_.refs_10_) | copy-start | bytes 12292
  82.5 1.0 copy-start.9
  83.6 54.8 %copy-start.26 = (bf16[128,1024]{1,0:T(8,128)(2,1)S(1)}, bf16[128,1024]{1,0:T(8,128)(2,1)}, u32[]{:S(2)}) copy-start(bf16[128,1024]{1,0:T(8,128)(2,1)} %refs_0_.2) | copy-start | bytes 786436
  138.2 1.4 copy-start
  138.3 1.6 copy-start.10
  138.3 1.0 copy-start.32
  138.3 2.9 copy-start.23
  138.3 4.1 copy-start.21
  138.9 140.7 %copy-start.19 = (f32[128,1024]{1,0:T(8,128)}, f32[128,1024]{1,0:T(8,128)S(1)}, u32[]{:S(2)}) copy-start(f32[128,1024]{1,0:T(8,128)S(1)} %get-tuple-element.85) | copy-start | bytes 1572868
  139.8 4.3 copy-start.29
  141.6 2.5 copy-start.37
  142.4 1.7 copy-start.30
  142.4 1.7 copy-start.35
  144.1 1.7 copy-start.38
  277.8 2.1 copy-start.36
  279.6 2.8 copy-start.33
  279.6 2.8 copy-start.34
  279.6 1.9 copy-start.24
  281.0 1.4 copy-start.8
  281.0 1.4 copy-start.13
  281.0 1.4 copy-start.17
  282.4 3.4 copy-start.3
  285.8 7.1 %copy-start.20 = (f32[128,1024]{1,0:T(8,128)S(1)}, f32[128,1024]{1,0:T(8,128)}, u32[]{:S(2)}) copy-start(f32[128,1024]{1,0:T(8,128)} %copy-done.19) | copy-start | bytes 1572868
  285.8 7.1 %copy-start.22 = (bf16[1024,2048]{1,0:T(8,128)(2,1)S(1)}, bf16[1024,2048]{1,0:T(8,128)(2,1)}, u32[]{:S(2)}) copy-start(bf16[1024,2048]{1,0:T(8,128)(2,1)} %get-tuple-element.46) | copy-start | bytes 12582916
  292.9 1.7 copy-start.12
  292.9 1.7 copy-start.31
  293.0 1.9 copy-start.1
  293.0 1.9 copy-start.11
  294.6 2.0 copy-start.27
  294.9 1.7 copy-start.28
  381.2 6.3 %copy-start.7 = (bf16[4,32,5120]{2,1,0:T(8,128)(2,1)S(1)}, bf16[4,32,5120]{2,1,0:T(8,128)(2,1)}, u32[]{:S(2)}) copy-start(bf16[4,32,5120]{2,1,0:T(8,128)(2,1)} %get-tuple-element.55) | copy-start | bytes 3932164
  387.4 2.9 copy-start.5
  387.4 2.9 copy-start.6
  387.6 63.2 %copy-start.2 = (bf16[2048,512]{1,0:T(8,128)(2,1)S(1)}, bf16[2048,512]{1,0:T(8,128)(2,1)}, u32[]{:S(2)}) copy-start(bf16[2048,512]{1,0:T(8,128)(2,1)} %get-tuple-element.38.keys_ref) | copy-start | bytes 6291460

commit v7 on v6

--- a/solution.py
+++ b/solution.py
@@ -966,25 +966,35 @@
                         item.wait_recv()
                     core(p, way).start()
 
-    def end():
+    def receive():
         for p in total:
-            out, near, side = first(p)
+            _, near, side = first(p)
             near.wait()
-            side.wait()
+            side.wait_recv()
+            for way in range(6):
+
+                @pl.when(has(way))
+                def _():
+                    core(p, way).wait_recv()
+
+    def drain():
+        for p in total:
+            out, _, side = first(p)
+            side.wait_send()
             for way in (0, 1):
                 pl.when(more(way))(out[way].wait_send)
             for way in range(6):
 
                 @pl.when(has(way))
                 def _():
-                    core(p, way).wait()
+                    core(p, way).wait_send()
                     if ways[way][1] < 3:
                         pl.when(more(way))(line(p, way + 2, origin(way)).wait_send)
                     if p in shared:
                         for item in planes(p, way) + corners(p, way):
                             item.wait_send()
 
-    return begin, arrive, turn, cross, end
+    return begin, arrive, turn, cross, receive, drain
 
 
 def pieces_of(arrays, chunk, own_count):
@@ -1008,72 +1018,68 @@
     ]
 
 
-def gather_kernel(pieces, count, *refs):
-    enter(plane_peers())
-    begin, arrive, turn, cross, end = gather_tasks(
-        pieces, refs[:count], refs[count : 2 * count], *refs[2 * count :]
-    )
-    begin()
-    arrive(1)
-    arrive(2)
-    turn(1)
-    arrive(3)
-    turn(2)
-    cross(1)
-    turn(3)
-    cross(2)
-    cross(3)
-    end()
-
-
-def gather_first(arrays, chunk, own_count):
-    pieces = pieces_of(arrays, chunk, own_count)
-    count = len(arrays)
-    return pl.pallas_call(
-        functools.partial(gather_kernel, pieces, count),
-        in_specs=[pl.BlockSpec(memory_space=pltpu.VMEM)] * count,
-        out_specs=[pl.BlockSpec(memory_space=pl.ANY)] * count,
-        out_shape=gathered(arrays),
-        scratch_shapes=gather_sems(pieces),
-        compiler_params=pltpu.CompilerParams(collective_id=3, has_side_effects=True),
-        name="gather_first",
-    )(*arrays)
-
-
-def gather_attend_kernel(pieces, count, rows, win, *refs):
-    sources, refs = refs[:count], refs[count:]
-    tokens_ref, gain_ref, weight_ref, segc_ref, segr_ref = refs[:5]
-    targets, refs = refs[5 : 5 + count], refs[5 + count :]
-    qkv_ref, out_ref, lse_ref, first_ref = refs[:4]
+def gather_kernel(sets, rows, win, *refs):
+    sources, refs = refs[:7], refs[7:]
+    query_ref, segc_ref, segr_ref = refs[:3]
+    targets, refs = refs[3:9], refs[9:]
+    qkv_ref, out_ref, lse_ref, gains = refs[:4]
+    tokens, gain_row, normal, folded = refs[4:8]
+    sems = refs[8:]
+    keys_src, qkv_src, proj_src, gate_src, head_src, tokens_src, gain_src = sources
+    keys_full, weight_full, proj_full, gate_full, head_full, folded_full = targets
     m = lax.axis_index("mem")
-    group_len, width = tokens_ref.shape
+    group_len, width = tokens.shape
     pairs = width // LANES
     enter(plane_peers())
-    begin, arrive, turn, cross, end = gather_tasks(pieces, sources, targets, *refs[4:])
+    k_set, a_set, c_set, b_set = (
+        gather_tasks(pieces, src, dst, *sems[3 * i : 3 * i + 3])
+        for i, (pieces, src, dst) in enumerate(
+            zip(
+                sets,
+                (
+                    [keys_src],
+                    [tokens_src, gain_src, qkv_src],
+                    [folded],
+                    [proj_src, gate_src, head_src],
+                ),
+                (
+                    [keys_full],
+                    [tokens, gains, weight_full],
+                    [folded_full],
+                    [proj_full, gate_full, head_full],
+                ),
+                strict=True,
+            )
+        )
+    )
+    begin, arrive, turn, cross, receive, drain = range(6)
+
+    def go(which, task, *hop):
+        which[task](*hop)
+
+    def fold():
+        for c in range(MHEADS * 2):
+            folded[:, c * NK : (c + 1) * NK] = dot(
+                query_ref[:, c * HALF : (c + 1) * HALF], keys_full[c * NK : (c + 1) * NK, :], NT
+            ).astype(BF)
 
     def normalize():
+        for i in range(8):
+            gain_row[:, i * LANES : (i + 1) * LANES] = gains[i * 16 : i * 16 + 1, :].astype(F32)
         block = 2 * rows
 
         def some(i, _):
             where = pl.ds(pl.multiple_of(i * block, block), block)
-            values = tokens_ref[where, :].astype(F32)
-            first_ref[where, :] = (values * rms_scale(values) * gain_ref[...]).astype(BF)
+            values = tokens[where, :].astype(F32)
+            normal[where, :] = (values * rms_scale(values) * gain_row[...]).astype(BF)
             return 0
 
         lax.fori_loop(0, group_len // block, some, 0)
 
     def project(i, _):
         where = pl.ds(pl.multiple_of(i * 3 * LANES, LANES), 3 * LANES)
-        qkv_ref[:, where] = dot(first_ref[...], weight_ref[:, where]).astype(BF)
-
-        @pl.when(i == 2)
-        def _():
-            arrive(1)
-
-        @pl.when(i == 6)
-        def _():
-            arrive(2)
-
+        qkv_ref[:, where] = dot(normal[...], weight_full[:, where]).astype(BF)
+        during(i, PROJECT_TASKS)
         return 0
 
     def load_of(pair):
@@ -1091,55 +1097,106 @@
             rows, win, pair, m, load(0, own), load, segc_ref.at[own], segr_ref, lse_ref[...]
         )
         out_ref[:, pl.ds(pl.multiple_of(pair * LANES, LANES), LANES)] = value
-
-        @pl.when(pair == 0)
-        def _():
-            turn(1)
-
-        @pl.when(pair == 3)
-        def _():
-            arrive(3)
-
-        @pl.when(pair == 5)
-        def _():
-            turn(2)
-            cross(1)
-
+        during(pair, ATTEND_TASKS)
         return 0
 
+    def during(i, tasks):
+        for when, todo in tasks.items():
+
+            @pl.when(i == when)
+            def _():
+                for which, task, hop in todo:
+                    go(which, task, hop)
+
+    PROJECT_TASKS = {
+        0: [(c_set, turn, 1), (b_set, arrive, 2)],
+        2: [(b_set, turn, 1), (c_set, arrive, 3)],
+        4: [(c_set, turn, 2), (b_set, arrive, 3)],
+        6: [(b_set, turn, 2), (c_set, cross, 1)],
+    }
+    ATTEND_TASKS = {
+        0: [(c_set, turn, 3), (b_set, cross, 1)],
+        2: [(b_set, turn, 3), (c_set, cross, 2)],
+        3: [(b_set, cross, 2)],
+        4: [(c_set, cross, 3)],
+        5: [(b_set, cross, 3)],
+    }
     lse_ref[...] = jnp.zeros_like(lse_ref)
-    begin()
+    go(k_set, begin)
+    go(a_set, begin)
+    go(k_set, arrive, 1)
+    go(k_set, arrive, 2)
+    go(a_set, arrive, 1)
+    go(k_set, turn, 1)
+    go(k_set, arrive, 3)
+    go(k_set, turn, 2)
+    go(k_set, cross, 1)
+    go(k_set, turn, 3)
+    go(k_set, cross, 2)
+    go(a_set, arrive, 2)
+    go(k_set, cross, 3)
+    go(a_set, turn, 1)
+    go(k_set, receive)
+    fold()
+    go(c_set, begin)
+    go(b_set, begin)
+    go(a_set, arrive, 3)
+    go(a_set, turn, 2)
+    go(a_set, cross, 1)
+    go(c_set, arrive, 1)
+    go(a_set, turn, 3)
+    go(b_set, arrive, 1)
+    go(a_set, cross, 2)
+    go(a_set, cross, 3)
+    go(c_set, arrive, 2)
+    go(a_set, receive)
     normalize()
     lax.fori_loop(0, 8, project, 0)
     lax.fori_loop(0, 8, attend, 0)
-    turn(3)
-    cross(2)
-    cross(3)
-    end()
-
-
-def gather_attend(arrays, chunk, tokens, gain, weight, seg_col, seg_row, rows):
-    pieces = pieces_of(arrays, chunk, 0)
-    count = len(arrays)
-    group_len, width = tokens.shape
+    go(c_set, receive)
+    go(b_set, receive)
+    for one in (k_set, a_set, c_set, b_set):
+        go(one, drain)
+
+
+def gather_weights(keys, qkv, proj, gate, head, tokens, gains, query, seg_col, seg_row, rows):
+    sets = (
+        pieces_of([keys], WIDTH, 0),
+        pieces_of([tokens, gains, qkv], 3 * WIDTH, 2),
+        pieces_of([jax.ShapeDtypeStruct((query.shape[0], KEYS), BF)], KEYS, 0),
+        pieces_of([proj, gate, head], WIDTH, 0),
+    )
+    group_len = seg_col.shape[0]
+    width = tokens.shape[1]
     win = min(group_len, group_len // 2 + rows)
     vmem, hbm = pl.BlockSpec(memory_space=pltpu.VMEM), pl.BlockSpec(memory_space=pl.ANY)
+    sems = []
+    for pieces in sets:
+        sems += gather_sems(pieces)
     return pl.pallas_call(
-        functools.partial(gather_attend_kernel, pieces, count, rows, win),
-        in_specs=[vmem] * (count + 5),
-        out_specs=[hbm] * count + [vmem] * 3,
+        functools.partial(gather_kernel, sets, rows, win),
+        in_specs=[vmem] * 10,
+        out_specs=[vmem, vmem, hbm, hbm, hbm, hbm, vmem, vmem, vmem, vmem],
         out_shape=[
-            *gathered(arrays),
+            *gathered([keys, qkv, proj, gate, head]),
+            jax.ShapeDtypeStruct((8 * query.shape[0], KEYS), BF),
             jax.ShapeDtypeStruct((group_len, 3 * width), BF),
             jax.ShapeDtypeStruct((rows, width), F32),
             jax.ShapeDtypeStruct((rows, LANES), F32),
+            *gathered([gains]),
         ],
-        scratch_shapes=[pltpu.VMEM((group_len, width), BF), *gather_sems(pieces)],
+        scratch_shapes=[
+            pltpu.VMEM((group_len, width), BF),
+            pltpu.VMEM((1, width), F32),
+            pltpu.VMEM((group_len, width), BF),
+            pltpu.VMEM((query.shape[0], KEYS), BF),
+            *sems,
+        ],
         compiler_params=pltpu.CompilerParams(
-            collective_id=5, has_side_effects=True, vmem_limit_bytes=48 * 1024 * 1024
+            collective_id=3, has_side_effects=True, vmem_limit_bytes=56 * 1024 * 1024
         ),
-        name="gather_attend",
-    )(*arrays, tokens, gain, weight, seg_col, seg_row)
+        name="gather_weights",
+    )(keys, qkv, proj, gate, head, tokens, gains, query, seg_col, seg_row)
 
 
 WIDTH = HEADS * HDIM
@@ -1467,19 +1524,6 @@
     return sums.reshape(4 * 32, E_ALL), qkv_rows
 
 
-def fold_kernel(query_ref, keys_ref, out_ref):
-    for c in range(MHEADS * 2):
-        out_ref[:, c * NK : (c + 1) * NK] = dot(
-            query_ref[:, c * HALF : (c + 1) * HALF], keys_ref[c * NK : (c + 1) * NK, :], NT
-        ).astype(BF)
-
-
-def fold(query, keys):
-    return pl.pallas_call(
-        fold_kernel, out_shape=jax.ShapeDtypeStruct((query.shape[0], KEYS), BF), name="fold"
-    )(query, keys)
-
-
 def finish_kernel(
     early_ref, late_ref, keys_ref, out, gate, proj, qkv, query, gains
 ):
@@ -1551,10 +1595,6 @@
         gain_block = jnp.concatenate(
             [attn_gain[None], mem_gain[None], jnp.zeros((14, LANES), BF)]
         )
-        tokens_all, gains, qkv_full, keys_full = gather_first(
-            (tokens, gain_block, qkv_weight, half_keys), 3 * width // 2, 2
-        )
-        gains = gains.reshape(8, 16, LANES)[:, :2].transpose(1, 0, 2).reshape(2, width)
     else:
         gains = lax.all_gather(jnp.stack([attn_gain, mem_gain]), "mem", axis=1, tiled=True)
         tokens_all = gather(tokens)
@@ -1564,25 +1604,41 @@
         keys_full = gather(half_keys)
         gate_full = gather(gate_weight)
         output_full = gather(out_weight)
-    gains = gains.astype(F32)
-    gain_one, gain_two = gains[0:1], gains[1:2]
+        gains = gains.astype(F32)
+        gain_one, gain_two = gains[0:1], gains[1:2]
     seg_row, seg_col = segment_ids.reshape(1, group_len), segment_ids.reshape(group_len, 1)
 
     requests = route(picks, owners, local_rows, capacity, flat_bits)
     arrived = lax.all_to_all(requests, ALL, split_axis=0, concat_axis=0, tiled=True)
 
     if linked:
-        folded = fold(query_weight, keys_full)
-        proj_full, folded_full, gate_full, output_full, qkv_all, attn_sum, lse = gather_attend(
-            (attn_proj, folded, gate_weight, out_weight),
-            width,
-            tokens_all,
-            gain_one,
+        (
+            keys_full,
             qkv_full,
+            proj_full,
+            gate_full,
+            output_full,
+            folded_full,
+            qkv_all,
+            attn_sum,
+            lse,
+            gains,
+        ) = gather_weights(
+            half_keys,
+            qkv_weight,
+            attn_proj,
+            gate_weight,
+            out_weight,
+            tokens,
+            gain_block,
+            query_weight,
             seg_col,
             seg_row,
             rows,
         )
+        gains = gains.reshape(8, 16, LANES)[:, :2].transpose(1, 0, 2).reshape(2, width)
+        gains = gains.astype(F32)
+        gain_one, gain_two = gains[0:1], gains[1:2]
     else:
         inputs_all = tokens_all.astype(F32)
         first_all = (inputs_all * rms_scale(inputs_all) * gain_one).astype(BF)

time: 461 us -> 442 us (0.959)
  Pallas kernels: 400 us -> 380 us
    pallas_call x3 -> x1, Pallas kernels: 117 us -> 98.4 us  [gather_weights(): pl.pallas_call(functools.partial(gather_kernel, sets, rows, win), in_spec...]
    unnamed x85 -> x69, local copies, waits for them, and re-layouts: 10.8 us -> 7.24 us
  transfers between devices with their start and end apart: 1 -> 1, of which waited for: 0 -> 0; matrix products, arithmetic and copies ran while one was open for 2% -> 3% of each run, Pallas kernels for 26% -> 23%
where the time goes in v7:
time: 442 us; the launch traced here: 436 us
  Pallas kernels  380 us (86%)
  other arithmetic  18.1 us (4%)
  matrix products  17.5 us (4%)
  local copies, waits for them, and re-layouts  11.4 us (3%)
  starting transfers between devices  7.47 us (2%)
    pallas_call x1, Pallas kernels, memory_call(): pl.pallas_call(functools.partial(memory_kernel, flat_bits), in_specs=[hbm...  125 us
    pallas_call x1, Pallas kernels, gather_weights(): pl.pallas_call(functools.partial(gather_kernel, sets, rows, win), in_spec...  98.4 us
    pallas_call x1, Pallas kernels, reduce_back(): pl.pallas_call(functools.partial(back_kernel, rows, win), in_specs=[hbm]...  83.4 us
    pallas_call x1, Pallas kernels, reduce_late(): pl.pallas_call(late_kernel, in_specs=[pl.BlockSpec(memory_space=pl.ANY)]...  60.5 us
    dot_general x9, matrix products, dot(): lax.dot_general(left, right, (dims, ((), ())), preferred_element_type=F32)  16.7 us
  transfers between devices with their start and end apart: 1, of which 0 were waited for; matrix products, arithmetic and copies ran while one was open for 3% of the time, Pallas kernels for 23%

profile of v7, /device:TPU:0, one launch (start us, length us, event | category | flops | bytes accessed | tf_op | source)
XLA Modules:
  0.0 436.2 jit_solution(9120438928362190637)
XLA Ops:
  0.6 0.0 copy-start.15
  0.7 0.0 copy-start.31
  0.7 0.0 copy-start.32
  0.7 1.0 copy.57
  1.7 0.2 reshape.264
  1.9 0.3 convert_reduce_fusion.1
  2.2 0.1 copy.58
  2.3 0.1 reduce-window.8
  2.4 0.1 reduce
  2.5 0.4 convert_reduce_fusion
  3.0 8.0 %sort.7 = s32[32768]{0:T(1024)} sort(s32[32768]{0:T(1024)S(1)} %pad_add_fusion), dimensions={0}, to_apply=%region_4.5 | sort | flops 491520 | bytes 262144 | tf_op jit(solution)/shard_map/sort | solution.py:432
  10.9 7.5 %all-to-all-start = ((s32[32,1,1024]{2,1,0:T(1,128)}), s32[32,1,1024]{2,1,0:T(1,128)S(1)}, u32[]{:S(2)}, u32[]{:S(2)}) async-start(s32[32,1,1024]{2,1,0:T(1,128)} %bitcast.10), calls=%async_computation | async-start | bytes 262144 | tf_op jit(solution)/shard_map/all_to_all | solution.py:1612
  18.4 1.7 copy.54.refs_8_.refs_10_
  20.1 0.1 fusion.3
  20.3 0.1 pad.13.clone
  20.3 0.7 maximum_maximum_fusion.refs_6_
  21.0 98.4 %gather_weights.1 = (bf16[2048,512]{1,0:T(8,128)(2,1)}, bf16[1024,3072]{1,0:T(8,128)(2,1)}, bf16[1024,1024]{1,0:T(8,128)(2,1)}, bf16[1024,1024]{1,0:T(8,128)(2,1...) custom-call(bf16[256,512]{1,0:T(8,128)(2,1)} %refs_0_.1, ...), custom_call_target="tpu_custom_call" | custom-call | tf_op jit(solution)/shard_map/gather_weights/pallas_call | solution.py:1176
  119.5 1.1 convert_element_type.61.refs_2_
  120.5 0.9 convert_bitcast_fusion
  121.4 0.0 copy-done.16
  121.4 0.0 copy-start.11
  121.5 2.3 multiply_reduce_fusion.2
  123.7 0.0 copy-start.10
  123.8 0.1 multiply_convert_fusion.3.refs_1_
  123.9 0.0 copy-start.19
  123.9 0.0 copy-done.13
  123.9 0.5 fusion.27
  124.4 0.0 copy-start.28
  124.4 0.0 copy-done.11
  124.4 1.7 fusion.28.scores_ref
  126.1 0.0 copy-done.20
  126.1 0.4 copy-done.25
  126.5 1.6 multiply_convert_fusion.2
  128.2 0.7 copy.56.picks_ref
  128.9 3.0 pick_fwd.1
  131.9 1.5 pad_maximum_fusion.payload_ref
  133.4 0.0 all-to-all-done
  133.4 0.7 copy.66
  134.1 125.0 %memory.1 = (f32[128,1152]{1,0:T(8,128)}, f32[4,512,1024]{2,1,0:T(8,128)}) custom-call(bf16[128,1152]{1,0:T(8,128)(2,1)} %pad_maximum_fusion.payload_ref, s32[32,1024]{1,0:T(8,128)} %bitcast.51, bf16[2048,1024]{1,0:T(8,128)(2,1)} %values_ref.1), custom_call_target="tpu_custom_call" | custom-call | tf_op jit(solution)/shard_map/memory/pallas_call | solution.py:812
  259.1 1.8 multiply_convert_fusion
  260.9 0.0 copy-start.23
  260.9 0.2 copy-done.26
  261.1 1.2 fusion.2
  262.3 0.5 copy-done.14
  262.8 0.8 fusion.29
  263.7 3.4 copy-done
  267.1 7.1 %pick_bwd.1 = (bf16[128,2048]{1,0:T(8,128)(2,1)S(1)}, f32[2048,1024]{1,0:T(8,128)}) custom-call(f32[128,128]{1,0:T(8,128)S(1)} %copy-done.8, f32[128,1152]{1,0:T(8,128)S(1)} %copy-done.4, s32[128,128]{1,0:T(8,128)S(1)} %copy-done.7, f32[2048,1024]{1,0:T(8,128)S(1)} %bitcast.47), custom_call_target="tpu_custom_call" | custom-call | tf_op jit(solution)/shard_map/pick_bwd/pallas_call | solution.py:322
  274.2 0.0 copy-start.6
  274.2 0.0 copy-start.21
  274.2 1.6 multiply_reduce_fusion
  275.9 0.0 copy-start.17
  275.9 0.2 fusion.25.refs_5_
  276.1 0.0 copy-done.27
  276.1 0.8 fusion.1
  277.0 0.8 fusion.12
  277.8 0.1 fusion.16
  277.9 0.8 concatenate.39.refs_7_
  278.7 83.4 %reduce_back.1 = (bf16[4,32,5120]{2,1,0:T(8,128)(2,1)}, bf16[128,3072]{1,0:T(8,128)(2,1)}) custom-call(bf16[128,1024]{1,0:T(8,128)(2,1)} %copy-done.23, bf16[128,1024]{1,0:T(8,128)(2,1)} %copy-done.19, bf16[128,1024]{1,0:T(8,128)(2,1)} %copy-done.22, bf16[128,1024]{1,0:T(8,128)(2,1)} %refs_3_.3, bf16[128,1024]{1,0:T(8,128)(2,1)} %copy-done.24, ...), custom_call_target="tpu_custom_call" | custom-call | tf_op jit(solution)/shard_map/reduce_back/pallas_call | solution.py:1499
  362.2 6.2 %fusion.10 = (f32[1024]{0:T(1024)S(1)}, f32[128]{0:T(128)S(1)}, f32[128,1024]{1,0:T(8,128)}) fusion(bf16[128,1024]{1,0:T(8,128)(2,1)S(1)} %copy-done.16, f32[128]{0:T(128)S(1)} %get-tuple-element.90, f32[1024]{0:T(1024)S(1)} %bitcast.61, bf16[128,3072]{1,0:T(8,128)(2,1)} %get-tuple-element.50.rows_ref, bf16[1024,3072]{1,0:T(8,128)(2,1)} %get-tuple-element.51), kind=kOutput, calls=%fused_computation.24 | convolution fusion | flops 806222720 | bytes 7873536 | tf_op jit(solution)/shard_map/dot_general | solution.py:25
  368.5 2.7 fusion.8
  371.2 60.5 %reduce_late.1 = (bf16[4,32,3200]{2,1,0:T(8,128)(2,1)S(1)}, f32[256,512]{1,0:T(8,128)S(1)}) custom-call(bf16[128,1024]{1,0:T(8,128)(2,1)S(1)} %get-tuple-element.69.first_ref, bf16[128,3072]{1,0:T(8,128)(2,1)S(1)} %copy-done.2, bf16[16,1024]{1,0:T(8,128)(2,1)S(1)} %concatenate.40.gain_ref, bf16[128,2048]{1,0:T(8,128)(2,1)S(1)} %slice.37.half_ref, ...), custom_call_target="tpu_custom_call" | custom-call | tf_op jit(solution)/shard_map/reduce_late/pallas_call | solution.py:1369
  431.7 2.7 finish.1
  434.5 0.5 slice_bitcast_fusion
  435.0 0.8 copy.68
  (63 shorter events, 0.3 us)
Async XLA Ops:
  0.6 19.5 %copy-start.15 = (bf16[128,1024]{1,0:T(8,128)(2,1)S(1)}, bf16[128,1024]{1,0:T(8,128)(2,1)}, u32[]{:S(2)}) copy-start(bf16[128,1024]{1,0:T(8,128)(2,1)} %refs_5_.1) | copy-start | bytes 786436
  0.7 19.7 %copy-start.31 = (bf16[128]{0:T(256)(128)(2,1)S(1)}, bf16[128]{0:T(256)(128)(2,1)}, u32[]{:S(2)}) copy-start(bf16[128]{0:T(256)(128)(2,1)} %param.19) | copy-start | bytes 772
  0.7 19.7 %copy-start.32 = (bf16[128]{0:T(256)(128)(2,1)S(1)}, bf16[128]{0:T(256)(128)(2,1)}, u32[]{:S(2)}) copy-start(bf16[128]{0:T(256)(128)(2,1)} %param.16) | copy-start | bytes 772
  10.9 122.5 %all-to-all-start = ((s32[32,1,1024]{2,1,0:T(1,128)}), s32[32,1,1024]{2,1,0:T(1,128)S(1)}, u32[]{:S(2)}, u32[]{:S(2)}) async-start(s32[32,1,1024]{2,1,0:T(1,128)} %bitcast.10), calls=%async_computation | async-start | bytes 262144 | tf_op jit(solution)/shard_map/all_to_all | solution.py:1612
  21.0 100.4 %copy-start.16 = (bf16[128,1024]{1,0:T(8,128)(2,1)S(1)}, bf16[128,1024]{1,0:T(8,128)(2,1)}, u32[]{:S(2)}) copy-start(bf16[128,1024]{1,0:T(8,128)(2,1)} %refs_5_.1) | copy-start | bytes 786436
  120.5 3.8 copy-start.22
  120.5 3.3 copy-start.13
  121.4 3.0 copy-start.11
  123.7 152.2 %copy-start.10 = (f32[128,1024]{1,0:T(8,128)}, f32[128,1024]{1,0:T(8,128)S(1)}, u32[]{:S(2)}) copy-start(f32[128,1024]{1,0:T(8,128)S(1)} %get-tuple-element.82) | copy-start | bytes 1572868
  123.9 2.3 copy-start.19
  124.4 1.8 copy-start.28
  124.4 1.7 copy-start.20
  124.4 2.1 copy-start.25
  126.5 1.7 copy-start.29
  259.1 2.1 copy-start.26
  260.9 2.8 copy-start.23
  260.9 2.8 copy-start.24
  260.9 1.9 copy-start.14
  262.3 1.4 copy-start.4
  262.3 1.4 copy-start.7
  262.3 1.4 copy-start.8
  263.7 3.4 copy-start
  267.1 7.1 %copy-start.12 = (bf16[1024,2048]{1,0:T(8,128)(2,1)S(1)}, bf16[1024,2048]{1,0:T(8,128)(2,1)}, u32[]{:S(2)}) copy-start(bf16[1024,2048]{1,0:T(8,128)(2,1)} %get-tuple-element.42) | copy-start | bytes 12582916
  274.2 1.7 copy-start.6
  274.2 1.7 copy-start.21
  274.2 1.9 copy-start.9
  274.2 1.9 copy-start.27
  275.9 1.1 copy-start.17
  276.1 1.7 copy-start.18
  276.1 1.6 copy-start.30
  362.1 6.3 %copy-start.3 = (bf16[4,32,5120]{2,1,0:T(8,128)(2,1)S(1)}, bf16[4,32,5120]{2,1,0:T(8,128)(2,1)}, u32[]{:S(2)}) copy-start(bf16[4,32,5120]{2,1,0:T(8,128)(2,1)} %get-tuple-element.52) | copy-start | bytes 3932164
  368.3 2.9 copy-start.1
  368.3 2.9 copy-start.2
  368.5 63.2 %copy-start.5 = (bf16[2048,512]{1,0:T(8,128)(2,1)S(1)}, bf16[2048,512]{1,0:T(8,128)(2,1)}, u32[]{:S(2)}) copy-start(bf16[2048,512]{1,0:T(8,128)(2,1)} %get-tuple-element.54.keys_ref) | copy-start | bytes 6291460

commit v8 on v7

--- a/solution.py
+++ b/solution.py
@@ -1258,17 +1258,22 @@
             store_blocks(held, k, dot(lhs, fact[:, right + j : right + j + WIDTH], TN), at + j)
 
 
-def spread_quarters(total, quarter, send, recv):
+def spread_quarters(total, quarter, kind, send, recv):
     g, m, across, along, _ = places()
     quarter[g] = total.astype(BF)
+    half = quarter.shape[1] // 2
     to_x, to_y = (across, m), (along, m)
-    low, high = pl.ds(0, 16), pl.ds(16, 16)
-    a = push(quarter.at[g], quarter.at[g], send.at[6, 0], recv.at[6, 0], to_x)
-    b = push(quarter.at[g], quarter.at[g], send.at[6, 1], recv.at[6, 1], to_y)
+    low, high = pl.ds(0, half), pl.ds(half, half)
+
+    def go(i, block, peer):
+        return push(block, block, send.at[kind, i], recv.at[kind, i], peer)
+
+    a = go(0, quarter.at[g], to_x)
+    b = go(1, quarter.at[g], to_y)
     a.wait_recv()
-    c = push(quarter.at[across, low], quarter.at[across, low], send.at[6, 2], recv.at[6, 2], to_y)
+    c = go(2, quarter.at[across, low], to_y)
     b.wait_recv()
-    d = push(quarter.at[along, high], quarter.at[along, high], send.at[6, 3], recv.at[6, 3], to_x)
+    d = go(3, quarter.at[along, high], to_x)
     c.wait_recv()
     d.wait_recv()
     for copy in (a, b, c, d):
@@ -1295,6 +1300,7 @@
     quarter,
     tables,
     arrived,
+    spread,
     local_sem,
     send,
     recv,
@@ -1317,8 +1323,8 @@
     def table(d):
         block = (z + d) % 4 * 2 + core
         lhs = wide[:, pl.ds(pl.multiple_of(block * NK, LANES), NK)]
-        rhs = wide[:, pl.ds(pl.multiple_of(KEYS + block * HALF, LANES), HALF)]
-        return dot(lhs, rhs, TN)
+        at = KEYS + block * HALF + g * (HALF // 4)
+        return dot(lhs, wide[:, pl.ds(pl.multiple_of(at, LANES), HALF // 4)], TN)
 
     def line(k):
         return pltpu.make_async_remote_copy(
@@ -1348,16 +1354,19 @@
         return 0
 
     lax.fori_loop(0, 3, send_table, 0)
-    keys_ref[...] = table(0)
+    keys = table(0)
     for k in range(4):
         corner(k)
     for k in range(3):
         plane(k)
-    spread_quarters(last(), quarter, send, recv)
     for k in range(3):
         line(k).wait_recv()
-        keys_ref[...] += arrived[k].astype(F32)
+        keys = keys + arrived[k].astype(F32)
         line(k).wait_send()
+    spread_quarters(keys, spread, 8, send, recv)
+    for i in range(4):
+        keys_ref[:, i * (HALF // 4) : (i + 1) * (HALF // 4)] = spread[i].astype(F32)
+    spread_quarters(last(), quarter, 6, send, recv)
     for _, far in copies:
         far.wait_send()
     out_ref[...] = quarter[...]
@@ -1381,11 +1390,12 @@
             pltpu.VMEM((4, 4, 32, L_ALL), BF),
             *plane_scratch(32, L_ALL),
             pltpu.VMEM((4, 32, L_ALL), BF),
-            pltpu.VMEM((3, NK, HALF), BF),
-            pltpu.VMEM((3, NK, HALF), BF),
+            pltpu.VMEM((3, NK, HALF // 4), BF),
+            pltpu.VMEM((3, NK, HALF // 4), BF),
+            pltpu.VMEM((4, NK, HALF // 4), BF),
             pltpu.SemaphoreType.DMA((5,)),
-            pltpu.SemaphoreType.DMA((8, 5)),
-            pltpu.SemaphoreType.DMA((8, 5)),
+            pltpu.SemaphoreType.DMA((9, 5)),
+            pltpu.SemaphoreType.DMA((9, 5)),
         ],
         compiler_params=pltpu.CompilerParams(
             collective_id=2, has_side_effects=True, vmem_limit_bytes=48 * 1024 * 1024
@@ -1481,7 +1491,7 @@
         return 0
 
     lax.fori_loop(0, pairs, attend, 0)
-    spread_quarters(last(), quarter, send, recv)
+    spread_quarters(last(), quarter, 6, send, recv)
     for _, far in copies:
         far.wait_send()
     for copy in [*lines, side, *forward]:

time: 442 us -> 431 us (0.975)
  Pallas kernels: 380 us -> 370 us
    pallas_call x1, Pallas kernels: 60.5 us -> 50.3 us  [reduce_late(): pl.pallas_call(late_kernel, in_specs=[pl.BlockSpec(memory_space=pl.ANY)]...]
  transfers between devices with their start and end apart: 1 -> 1, of which waited for: 0 -> 0; matrix products, arithmetic and copies ran while one was open for 3% -> 3% of each run, Pallas kernels for 23% -> 24%
where the time goes in v8:
time: 431 us; the launch traced here: 426 us
  Pallas kernels  370 us (86%)
  other arithmetic  18.1 us (4%)
  matrix products  17.4 us (4%)
  local copies, waits for them, and re-layouts  11.4 us (3%)
  starting transfers between devices  7.47 us (2%)
    pallas_call x1, Pallas kernels, memory_call(): pl.pallas_call(functools.partial(memory_kernel, flat_bits), in_specs=[hbm...  125 us
    pallas_call x1, Pallas kernels, gather_weights(): pl.pallas_call(functools.partial(gather_kernel, sets, rows, win), in_spec...  98.4 us
    pallas_call x1, Pallas kernels, reduce_back(): pl.pallas_call(functools.partial(back_kernel, rows, win), in_specs=[hbm]...  83.4 us
    pallas_call x1, Pallas kernels, reduce_late(): pl.pallas_call(late_kernel, in_specs=[pl.BlockSpec(memory_space=pl.ANY)]...  50.3 us
    dot_general x9, matrix products, dot(): lax.dot_general(left, right, (dims, ((), ())), preferred_element_type=F32)  16.7 us
  transfers between devices with their start and end apart: 1, of which 0 were waited for; matrix products, arithmetic and copies ran while one was open for 3% of the time, Pallas kernels for 24%

profile of v8, /device:TPU:0, one launch (start us, length us, event | category | flops | bytes accessed | tf_op | source)
XLA Modules:
  0.0 426.0 jit_solution(7796255520685479365)
XLA Ops:
  0.6 0.0 copy-start.15
  0.7 1.0 copy.57
  1.7 0.2 reshape.264
  1.9 0.3 convert_reduce_fusion.1
  2.2 0.1 copy.58
  2.3 0.1 reduce-window.8
  2.4 0.1 reduce
  2.5 0.4 convert_reduce_fusion
  3.0 8.0 %sort.7 = s32[32768]{0:T(1024)} sort(s32[32768]{0:T(1024)S(1)} %pad_add_fusion), dimensions={0}, to_apply=%region_4.5 | sort | flops 491520 | bytes 262144 | tf_op jit(solution)/shard_map/sort | solution.py:432
  10.9 7.5 %all-to-all-start = ((s32[32,1,1024]{2,1,0:T(1,128)}), s32[32,1,1024]{2,1,0:T(1,128)S(1)}, u32[]{:S(2)}, u32[]{:S(2)}) async-start(s32[32,1,1024]{2,1,0:T(1,128)} %bitcast.10), calls=%async_computation | async-start | bytes 262144 | tf_op jit(solution)/shard_map/all_to_all | solution.py:1622
  18.4 1.7 copy.54.refs_8_.refs_10_
  20.1 0.1 fusion.3
  20.3 0.1 pad.13.clone
  20.3 0.0 copy-done.31
  20.3 0.7 maximum_maximum_fusion.refs_6_
  21.0 98.4 %gather_weights.1 = (bf16[2048,512]{1,0:T(8,128)(2,1)}, bf16[1024,3072]{1,0:T(8,128)(2,1)}, bf16[1024,1024]{1,0:T(8,128)(2,1)}, bf16[1024,1024]{1,0:T(8,128)(2,1...) custom-call(bf16[256,512]{1,0:T(8,128)(2,1)} %refs_0_.1, ...), custom_call_target="tpu_custom_call" | custom-call | tf_op jit(solution)/shard_map/gather_weights/pallas_call | solution.py:1176
  119.5 1.1 convert_element_type.61.refs_2_
  120.5 0.9 convert_bitcast_fusion
  121.5 2.3 multiply_reduce_fusion.2
  123.7 0.0 copy-start.10
  123.8 0.1 multiply_convert_fusion.3.refs_1_
  123.9 0.0 copy-start.19
  123.9 0.5 fusion.27
  124.4 0.0 copy-start.28
  124.4 0.0 copy-done.11
  124.4 1.7 fusion.28.scores_ref
  126.1 0.0 copy-done.19
  126.1 0.4 copy-done.25
  126.5 1.6 multiply_convert_fusion.2
  128.2 0.7 copy.56.picks_ref
  128.9 3.0 pick_fwd.1
  131.9 1.5 pad_maximum_fusion.payload_ref
  133.4 0.0 all-to-all-done
  133.4 0.7 copy.66
  134.1 125.0 %memory.1 = (f32[128,1152]{1,0:T(8,128)}, f32[4,512,1024]{2,1,0:T(8,128)}) custom-call(bf16[128,1152]{1,0:T(8,128)(2,1)} %pad_maximum_fusion.payload_ref, s32[32,1024]{1,0:T(8,128)} %bitcast.51, bf16[2048,1024]{1,0:T(8,128)(2,1)} %values_ref.1), custom_call_target="tpu_custom_call" | custom-call | tf_op jit(solution)/shard_map/memory/pallas_call | solution.py:812
  259.1 0.0 copy-start.26
  259.1 1.8 multiply_convert_fusion
  260.9 0.0 copy-start.23
  260.9 0.2 copy-done.26
  261.1 1.2 fusion.2
  262.3 0.5 copy-done.14
  262.8 0.8 fusion.29
  263.7 0.0 copy-done.23
  263.7 0.0 copy-done.24
  263.7 0.0 copy-done.4
  263.7 3.4 copy-done
  267.1 7.1 %pick_bwd.1 = (bf16[128,2048]{1,0:T(8,128)(2,1)S(1)}, f32[2048,1024]{1,0:T(8,128)}) custom-call(f32[128,128]{1,0:T(8,128)S(1)} %copy-done.8, f32[128,1152]{1,0:T(8,128)S(1)} %copy-done.4, s32[128,128]{1,0:T(8,128)S(1)} %copy-done.7, f32[2048,1024]{1,0:T(8,128)S(1)} %bitcast.47), custom_call_target="tpu_custom_call" | custom-call | tf_op jit(solution)/shard_map/pick_bwd/pallas_call | solution.py:322
  274.2 0.0 copy-start.6
  274.2 0.0 copy-start.21
  274.2 1.6 multiply_reduce_fusion
  275.9 0.0 copy-start.17
  275.9 0.2 fusion.25.refs_5_
  276.1 0.0 copy-done.27
  276.1 0.8 fusion.1
  277.0 0.8 fusion.12
  277.8 0.1 fusion.16
  277.9 0.8 concatenate.39.refs_7_
  278.7 83.4 %reduce_back.1 = (bf16[4,32,5120]{2,1,0:T(8,128)(2,1)}, bf16[128,3072]{1,0:T(8,128)(2,1)}) custom-call(bf16[128,1024]{1,0:T(8,128)(2,1)} %copy-done.23, bf16[128,1024]{1,0:T(8,128)(2,1)} %copy-done.19, bf16[128,1024]{1,0:T(8,128)(2,1)} %copy-done.22, bf16[128,1024]{1,0:T(8,128)(2,1)} %refs_3_.3, bf16[128,1024]{1,0:T(8,128)(2,1)} %copy-done.24, ...), custom_call_target="tpu_custom_call" | custom-call | tf_op jit(solution)/shard_map/reduce_back/pallas_call | solution.py:1509
  362.2 6.2 %fusion.10 = (f32[1024]{0:T(1024)S(1)}, f32[128]{0:T(128)S(1)}, f32[128,1024]{1,0:T(8,128)}) fusion(bf16[128,1024]{1,0:T(8,128)(2,1)S(1)} %copy-done.16, f32[128]{0:T(128)S(1)} %get-tuple-element.90, f32[1024]{0:T(1024)S(1)} %bitcast.61, bf16[128,3072]{1,0:T(8,128)(2,1)} %get-tuple-element.50.rows_ref, bf16[1024,3072]{1,0:T(8,128)(2,1)} %get-tuple-element.51), kind=kOutput, calls=%fused_computation.24 | convolution fusion | flops 806222720 | bytes 7873536 | tf_op jit(solution)/shard_map/dot_general | solution.py:25
  368.5 2.7 fusion.8
  371.2 50.3 %reduce_late.1 = (bf16[4,32,3200]{2,1,0:T(8,128)(2,1)S(1)}, f32[256,512]{1,0:T(8,128)S(1)}) custom-call(bf16[128,1024]{1,0:T(8,128)(2,1)S(1)} %get-tuple-element.69.first_ref, bf16[128,3072]{1,0:T(8,128)(2,1)S(1)} %copy-done.2, bf16[16,1024]{1,0:T(8,128)(2,1)S(1)} %concatenate.40.gain_ref, bf16[128,2048]{1,0:T(8,128)(2,1)S(1)} %slice.37.half_ref, ...), custom_call_target="tpu_custom_call" | custom-call | tf_op jit(solution)/shard_map/reduce_late/pallas_call | solution.py:1378
  421.5 2.7 finish.1
  424.3 0.5 slice_bitcast_fusion
  424.8 0.8 copy.68
  (63 shorter events, 0.3 us)
Async XLA Ops:
  0.6 19.5 %copy-start.15 = (bf16[128,1024]{1,0:T(8,128)(2,1)S(1)}, bf16[128,1024]{1,0:T(8,128)(2,1)}, u32[]{:S(2)}) copy-start(bf16[128,1024]{1,0:T(8,128)(2,1)} %refs_5_.1) | copy-start | bytes 786436
  0.7 19.7 %copy-start.31 = (bf16[128]{0:T(256)(128)(2,1)S(1)}, bf16[128]{0:T(256)(128)(2,1)}, u32[]{:S(2)}) copy-start(bf16[128]{0:T(256)(128)(2,1)} %param.19) | copy-start | bytes 772
  0.7 19.7 %copy-start.32 = (bf16[128]{0:T(256)(128)(2,1)S(1)}, bf16[128]{0:T(256)(128)(2,1)}, u32[]{:S(2)}) copy-start(bf16[128]{0:T(256)(128)(2,1)} %param.16) | copy-start | bytes 772
  10.9 122.5 %all-to-all-start = ((s32[32,1,1024]{2,1,0:T(1,128)}), s32[32,1,1024]{2,1,0:T(1,128)S(1)}, u32[]{:S(2)}, u32[]{:S(2)}) async-start(s32[32,1,1024]{2,1,0:T(1,128)} %bitcast.10), calls=%async_computation | async-start | bytes 262144 | tf_op jit(solution)/shard_map/all_to_all | solution.py:1622
  21.0 100.4 %copy-start.16 = (bf16[128,1024]{1,0:T(8,128)(2,1)S(1)}, bf16[128,1024]{1,0:T(8,128)(2,1)}, u32[]{:S(2)}) copy-start(bf16[128,1024]{1,0:T(8,128)(2,1)} %refs_5_.1) | copy-start | bytes 786436
  120.5 3.8 copy-start.22
  120.5 3.3 copy-start.13
  121.4 3.0 copy-start.11
  123.7 152.2 %copy-start.10 = (f32[128,1024]{1,0:T(8,128)}, f32[128,1024]{1,0:T(8,128)S(1)}, u32[]{:S(2)}) copy-start(f32[128,1024]{1,0:T(8,128)S(1)} %get-tuple-element.82) | copy-start | bytes 1572868
  123.9 2.3 copy-start.19
  124.4 1.8 copy-start.28
  124.4 1.7 copy-start.20
  124.4 2.1 copy-start.25
  126.5 1.7 copy-start.29
  259.1 2.1 copy-start.26
  260.9 2.8 copy-start.23
  260.9 2.8 copy-start.24
  260.9 1.9 copy-start.14
  262.3 1.4 copy-start.4
  262.3 1.4 copy-start.7
  262.3 1.4 copy-start.8
  263.7 3.4 copy-start
  267.1 7.1 %copy-start.12 = (bf16[1024,2048]{1,0:T(8,128)(2,1)S(1)}, bf16[1024,2048]{1,0:T(8,128)(2,1)}, u32[]{:S(2)}) copy-start(bf16[1024,2048]{1,0:T(8,128)(2,1)} %get-tuple-element.42) | copy-start | bytes 12582916
  274.2 1.7 copy-start.6
  274.2 1.7 copy-start.21
  274.2 1.9 copy-start.9
  274.2 1.9 copy-start.27
  275.9 1.1 copy-start.17
  276.1 1.7 copy-start.18
  276.1 1.6 copy-start.30
  362.1 6.3 %copy-start.3 = (bf16[4,32,5120]{2,1,0:T(8,128)(2,1)S(1)}, bf16[4,32,5120]{2,1,0:T(8,128)(2,1)}, u32[]{:S(2)}) copy-start(bf16[4,32,5120]{2,1,0:T(8,128)(2,1)} %get-tuple-element.52) | copy-start | bytes 3932164
  368.3 2.9 copy-start.1
  368.3 2.9 copy-start.2
  368.5 53.0 %copy-start.5 = (bf16[2048,512]{1,0:T(8,128)(2,1)S(1)}, bf16[2048,512]{1,0:T(8,128)(2,1)}, u32[]{:S(2)}) copy-start(bf16[2048,512]{1,0:T(8,128)(2,1)} %get-tuple-element.54.keys_ref) | copy-start | bytes 6291460

commit v9 on v8

--- a/solution.py
+++ b/solution.py
@@ -684,8 +684,7 @@
         1: [lambda: from_plane(0)],
         2: [lambda: from_line(1)],
         3: [lambda: from_corner(0), lambda: from_line(2)],
-        4: [lambda: from_line(3), lambda: pair_sum(0)],
-        5: [lambda: from_plane(1)],
+        4: [lambda: from_line(3), lambda: pair_sum(0), lambda: from_plane(1)],
         6: [lambda: corner_sum(0)],
         7: [lambda: from_corner(1)],
         8: [lambda: from_plane(2), lambda: pair_sum(1)],
@@ -775,8 +774,8 @@
         table_copy(h).start()
 
     lax.fori_loop(0, 16, step, 0)
+    pair_sum(3)
     plane_sum(2)
-    pair_sum(3)
     table_grad(0)
     corner_sum(3)
     table_grad(1)

time: 431 us -> 431 us (level)
  no operation moved by 1% of the time
where the time goes in v9:
time: 431 us; the launch traced here: 426 us
  Pallas kernels  370 us (86%)
  other arithmetic  18.1 us (4%)
  matrix products  17.5 us (4%)
  local copies, waits for them, and re-layouts  11.4 us (3%)
  starting transfers between devices  7.47 us (2%)
    pallas_call x1, Pallas kernels, memory_call(): pl.pallas_call(functools.partial(memory_kernel, flat_bits), in_specs=[hbm...  125 us
    pallas_call x1, Pallas kernels, gather_weights(): pl.pallas_call(functools.partial(gather_kernel, sets, rows, win), in_spec...  98.4 us
    pallas_call x1, Pallas kernels, reduce_back(): pl.pallas_call(functools.partial(back_kernel, rows, win), in_specs=[hbm]...  83.5 us
    pallas_call x1, Pallas kernels, reduce_late(): pl.pallas_call(late_kernel, in_specs=[pl.BlockSpec(memory_space=pl.ANY)]...  50.3 us
    dot_general x9, matrix products, dot(): lax.dot_general(left, right, (dims, ((), ())), preferred_element_type=F32)  16.7 us
  transfers between devices with their start and end apart: 1, of which 0 were waited for; matrix products, arithmetic and copies ran while one was open for 3% of the time, Pallas kernels for 24%

profile of v9, /device:TPU:0, one launch (start us, length us, event | category | flops | bytes accessed | tf_op | source)
XLA Modules:
  0.0 425.9 jit_solution(1941837642867352507)
XLA Ops:
  0.6 0.0 copy-start.15
  0.7 1.0 copy.57
  1.7 0.2 reshape.264
  1.9 0.3 convert_reduce_fusion.1
  2.2 0.1 copy.58
  2.3 0.1 reduce-window.8
  2.4 0.1 reduce
  2.5 0.4 convert_reduce_fusion
  3.0 8.0 %sort.7 = s32[32768]{0:T(1024)} sort(s32[32768]{0:T(1024)S(1)} %pad_add_fusion), dimensions={0}, to_apply=%region_4.5 | sort | flops 491520 | bytes 262144 | tf_op jit(solution)/shard_map/sort | solution.py:432
  10.9 7.5 %all-to-all-start = ((s32[32,1,1024]{2,1,0:T(1,128)}), s32[32,1,1024]{2,1,0:T(1,128)S(1)}, u32[]{:S(2)}, u32[]{:S(2)}) async-start(s32[32,1,1024]{2,1,0:T(1,128)} %bitcast.10), calls=%async_computation | async-start | bytes 262144 | tf_op jit(solution)/shard_map/all_to_all | solution.py:1621
  18.4 1.7 copy.54.refs_8_.refs_10_
  20.1 0.0 copy-done.15
  20.1 0.1 fusion.3
  20.3 0.1 pad.13.clone
  20.3 0.0 copy-done.31
  20.3 0.7 maximum_maximum_fusion.refs_6_
  21.0 98.4 %gather_weights.1 = (bf16[2048,512]{1,0:T(8,128)(2,1)}, bf16[1024,3072]{1,0:T(8,128)(2,1)}, bf16[1024,1024]{1,0:T(8,128)(2,1)}, bf16[1024,1024]{1,0:T(8,128)(2,1...) custom-call(bf16[256,512]{1,0:T(8,128)(2,1)} %refs_0_.1, ...), custom_call_target="tpu_custom_call" | custom-call | tf_op jit(solution)/shard_map/gather_weights/pallas_call | solution.py:1175
  119.5 1.1 convert_element_type.61.refs_2_
  120.5 0.9 convert_bitcast_fusion
  121.5 2.3 multiply_reduce_fusion.2
  123.7 0.0 copy-start.10
  123.8 0.1 multiply_convert_fusion.3.refs_1_
  123.9 0.0 copy-start.19
  123.9 0.5 fusion.27
  124.4 0.0 copy-start.28
  124.4 0.0 copy-done.11
  124.4 1.7 fusion.28.scores_ref
  126.1 0.4 copy-done.25
  126.5 1.6 multiply_convert_fusion.2
  128.2 0.7 copy.56.picks_ref
  128.9 3.0 pick_fwd.1
  131.9 1.5 pad_maximum_fusion.payload_ref
  133.4 0.0 all-to-all-done
  133.4 0.7 copy.66
  134.1 124.9 %memory.1 = (f32[128,1152]{1,0:T(8,128)}, f32[4,512,1024]{2,1,0:T(8,128)}) custom-call(bf16[128,1152]{1,0:T(8,128)(2,1)} %pad_maximum_fusion.payload_ref, s32[32,1024]{1,0:T(8,128)} %bitcast.51, bf16[2048,1024]{1,0:T(8,128)(2,1)} %values_ref.1), custom_call_target="tpu_custom_call" | custom-call | tf_op jit(solution)/shard_map/memory/pallas_call | solution.py:811
  259.0 1.8 multiply_convert_fusion
  260.8 0.0 copy-start.23
  260.8 0.0 copy-start.24
  260.8 0.0 copy-start.14
  260.8 0.2 copy-done.26
  261.0 1.2 fusion.2
  262.2 0.5 copy-done.14
  262.7 0.8 fusion.29
  263.6 3.4 copy-done
  267.0 7.1 %pick_bwd.1 = (bf16[128,2048]{1,0:T(8,128)(2,1)S(1)}, f32[2048,1024]{1,0:T(8,128)}) custom-call(f32[128,128]{1,0:T(8,128)S(1)} %copy-done.8, f32[128,1152]{1,0:T(8,128)S(1)} %copy-done.4, s32[128,128]{1,0:T(8,128)S(1)} %copy-done.7, f32[2048,1024]{1,0:T(8,128)S(1)} %bitcast.47), custom_call_target="tpu_custom_call" | custom-call | tf_op jit(solution)/shard_map/pick_bwd/pallas_call | solution.py:322
  274.1 0.0 copy-start.6
  274.1 0.0 copy-start.21
  274.1 1.6 multiply_reduce_fusion
  275.8 0.0 copy-start.17
  275.8 0.2 fusion.25.refs_5_
  276.0 0.0 copy-done.9
  276.0 0.0 copy-done.27
  276.0 0.8 fusion.1
  276.9 0.8 fusion.12
  277.7 0.1 fusion.16
  277.8 0.0 copy-done.18
  277.8 0.8 concatenate.39.refs_7_
  278.6 83.5 %reduce_back.1 = (bf16[4,32,5120]{2,1,0:T(8,128)(2,1)}, bf16[128,3072]{1,0:T(8,128)(2,1)}) custom-call(bf16[128,1024]{1,0:T(8,128)(2,1)} %copy-done.23, bf16[128,1024]{1,0:T(8,128)(2,1)} %copy-done.19, bf16[128,1024]{1,0:T(8,128)(2,1)} %copy-done.22, bf16[128,1024]{1,0:T(8,128)(2,1)} %refs_3_.3, bf16[128,1024]{1,0:T(8,128)(2,1)} %copy-done.24, ...), custom_call_target="tpu_custom_call" | custom-call | tf_op jit(solution)/shard_map/reduce_back/pallas_call | solution.py:1508
  362.1 6.2 %fusion.10 = (f32[1024]{0:T(1024)S(1)}, f32[128]{0:T(128)S(1)}, f32[128,1024]{1,0:T(8,128)}) fusion(bf16[128,1024]{1,0:T(8,128)(2,1)S(1)} %copy-done.16, f32[128]{0:T(128)S(1)} %get-tuple-element.90, f32[1024]{0:T(1024)S(1)} %bitcast.61, bf16[128,3072]{1,0:T(8,128)(2,1)} %get-tuple-element.50.rows_ref, bf16[1024,3072]{1,0:T(8,128)(2,1)} %get-tuple-element.51), kind=kOutput, calls=%fused_computation.24 | convolution fusion | flops 806222720 | bytes 7873536 | tf_op jit(solution)/shard_map/dot_general | solution.py:25
  368.4 2.7 fusion.8
  371.1 50.3 %reduce_late.1 = (bf16[4,32,3200]{2,1,0:T(8,128)(2,1)S(1)}, f32[256,512]{1,0:T(8,128)S(1)}) custom-call(bf16[128,1024]{1,0:T(8,128)(2,1)S(1)} %get-tuple-element.69.first_ref, bf16[128,3072]{1,0:T(8,128)(2,1)S(1)} %copy-done.2, bf16[16,1024]{1,0:T(8,128)(2,1)S(1)} %concatenate.40.gain_ref, bf16[128,2048]{1,0:T(8,128)(2,1)S(1)} %slice.37.half_ref, ...), custom_call_target="tpu_custom_call" | custom-call | tf_op jit(solution)/shard_map/reduce_late/pallas_call | solution.py:1377
  421.4 2.7 finish.1
  424.2 0.5 slice_bitcast_fusion
  424.7 0.8 copy.68
  (63 shorter events, 0.3 us)
Async XLA Ops:
  0.6 19.5 %copy-start.15 = (bf16[128,1024]{1,0:T(8,128)(2,1)S(1)}, bf16[128,1024]{1,0:T(8,128)(2,1)}, u32[]{:S(2)}) copy-start(bf16[128,1024]{1,0:T(8,128)(2,1)} %refs_5_.1) | copy-start | bytes 786436
  0.7 19.7 %copy-start.31 = (bf16[128]{0:T(256)(128)(2,1)S(1)}, bf16[128]{0:T(256)(128)(2,1)}, u32[]{:S(2)}) copy-start(bf16[128]{0:T(256)(128)(2,1)} %param.19) | copy-start | bytes 772
  0.7 19.7 %copy-start.32 = (bf16[128]{0:T(256)(128)(2,1)S(1)}, bf16[128]{0:T(256)(128)(2,1)}, u32[]{:S(2)}) copy-start(bf16[128]{0:T(256)(128)(2,1)} %param.16) | copy-start | bytes 772
  10.9 122.5 %all-to-all-start = ((s32[32,1,1024]{2,1,0:T(1,128)}), s32[32,1,1024]{2,1,0:T(1,128)S(1)}, u32[]{:S(2)}, u32[]{:S(2)}) async-start(s32[32,1,1024]{2,1,0:T(1,128)} %bitcast.10), calls=%async_computation | async-start | bytes 262144 | tf_op jit(solution)/shard_map/all_to_all | solution.py:1621
  21.0 100.4 %copy-start.16 = (bf16[128,1024]{1,0:T(8,128)(2,1)S(1)}, bf16[128,1024]{1,0:T(8,128)(2,1)}, u32[]{:S(2)}) copy-start(bf16[128,1024]{1,0:T(8,128)(2,1)} %refs_5_.1) | copy-start | bytes 786436
  120.5 3.8 copy-start.22
  120.5 3.3 copy-start.13
  121.4 3.0 copy-start.11
  123.7 152.1 %copy-start.10 = (f32[128,1024]{1,0:T(8,128)}, f32[128,1024]{1,0:T(8,128)S(1)}, u32[]{:S(2)}) copy-start(f32[128,1024]{1,0:T(8,128)S(1)} %get-tuple-element.82) | copy-start | bytes 1572868
  123.9 2.3 copy-start.19
  124.4 1.8 copy-start.28
  124.4 1.7 copy-start.20
  124.4 2.1 copy-start.25
  126.5 1.7 copy-start.29
  259.0 2.1 copy-start.26
  260.8 2.8 copy-start.23
  260.8 2.8 copy-start.24
  260.8 1.9 copy-start.14
  262.2 1.4 copy-start.4
  262.2 1.4 copy-start.7
  262.2 1.4 copy-start.8
  263.6 3.4 copy-start
  267.0 7.1 %copy-start.12 = (bf16[1024,2048]{1,0:T(8,128)(2,1)S(1)}, bf16[1024,2048]{1,0:T(8,128)(2,1)}, u32[]{:S(2)}) copy-start(bf16[1024,2048]{1,0:T(8,128)(2,1)} %get-tuple-element.42) | copy-start | bytes 12582916
  274.1 1.7 copy-start.6
  274.1 1.7 copy-start.21
  274.1 1.9 copy-start.9
  274.1 1.9 copy-start.27
  275.8 1.1 copy-start.17
  276.0 1.7 copy-start.18
  276.0 1.6 copy-start.30
  362.1 6.3 %copy-start.3 = (bf16[4,32,5120]{2,1,0:T(8,128)(2,1)S(1)}, bf16[4,32,5120]{2,1,0:T(8,128)(2,1)}, u32[]{:S(2)}) copy-start(bf16[4,32,5120]{2,1,0:T(8,128)(2,1)} %get-tuple-element.52) | copy-start | bytes 3932164
  368.2 2.9 copy-start.1
  368.2 2.9 copy-start.2
  368.4 53.0 %copy-start.5 = (bf16[2048,512]{1,0:T(8,128)(2,1)S(1)}, bf16[2048,512]{1,0:T(8,128)(2,1)}, u32[]{:S(2)}) copy-start(bf16[2048,512]{1,0:T(8,128)(2,1)} %get-tuple-element.54.keys_ref) | copy-start | bytes 6291460
